TPU v7x, 32 devices: a whole 2x2x4 slice. The times are simulated.
32 devices in a mesh: wide: 8 (over y, x, core), narrow: 4 (over z).
Axes of the slice: x: 2, y: 2, z: 4, core: 2. Of those that a mesh axis runs over, the one named last changes fastest.
Arguments:
- tokens: bfloat16 [16384, 768], P(('wide', 'narrow')), may hold values from -6 to 6
- lengths: int32 [32], P(('wide', 'narrow')), may hold values from 1 to 512, as said below
- query_weight: bfloat16 [589824], P(('wide', 'narrow')), may hold values from -0.21875 to 0.21875
- query_bias: bfloat16 [768], P(('wide', 'narrow')), may hold values from -3 to 3
- key_weight: bfloat16 [589824], P(('wide', 'narrow')), may hold values from -0.21875 to 0.21875
- value_weight: bfloat16 [589824], P(('wide', 'narrow')), may hold values from -0.21875 to 0.21875
- value_bias: bfloat16 [768], P(('wide', 'narrow')), may hold values from -3 to 3
- output_weight: bfloat16 [589824], P(('wide', 'narrow')), may hold values from -3.5 to 3.5
- output_bias: bfloat16 [768], P(('wide', 'narrow')), may hold values from -3 to 3
- attn_gain: bfloat16 [768], P(('wide', 'narrow')), may hold values from 0.099609375 to 1.8984375
- attn_shift: bfloat16 [768], P(('wide', 'narrow')), may hold values from -3 to 3
- inner_weight: bfloat16 [2359296], P(('wide', 'narrow')), may hold values from -0.21875 to 0.21875
- inner_bias: bfloat16 [3072], P(('wide', 'narrow')), may hold values from -3 to 3
- outer_weight: bfloat16 [2359296], P(('wide', 'narrow')), may hold values from -0.15625 to 0.15625
- outer_bias: bfloat16 [768], P(('wide', 'narrow')), may hold values from -3 to 3
- ffn_gain: bfloat16 [768], P(('wide', 'narrow')), may hold values from 0.099609375 to 1.8984375
- ffn_shift: bfloat16 [768], P(('wide', 'narrow')), may hold values from -3 to 3
- cotangent: bfloat16 [16384, 768], P(('wide', 'narrow')), may hold values from -6 to 6
Outputs:
- output: bfloat16 [16384, 768], P(('wide', 'narrow'))
- tokens_grad: bfloat16 [16384, 768], P(('wide', 'narrow'))
- query_weight_grad: float32 [589824], P(('wide', 'narrow'))
- query_bias_grad: float32 [768], P(('wide', 'narrow'))
- key_weight_grad: float32 [589824], P(('wide', 'narrow'))
- value_weight_grad: float32 [589824], P(('wide', 'narrow'))
- value_bias_grad: float32 [768], P(('wide', 'narrow'))
- output_weight_grad: float32 [589824], P(('wide', 'narrow'))
- output_bias_grad: float32 [768], P(('wide', 'narrow'))
- attn_gain_grad: float32 [768], P(('wide', 'narrow'))
- attn_shift_grad: float32 [768], P(('wide', 'narrow'))
- inner_weight_grad: float32 [2359296], P(('wide', 'narrow'))
- inner_bias_grad: float32 [3072], P(('wide', 'narrow'))
- outer_weight_grad: float32 [2359296], P(('wide', 'narrow'))
- outer_bias_grad: float32 [768], P(('wide', 'narrow'))
- ffn_gain_grad: float32 [768], P(('wide', 'narrow'))
- ffn_shift_grad: float32 [768], P(('wide', 'narrow'))
Inputs may be any that keep to these rules, and one draw needn't show every extreme that they name: Every length is 1 to 512; some sequence has exactly 512; lengths vary from device to device.
All inputs are finite; a program needn't handle non-finite values.
Results may differ from a plain program's by a relative error of at most 0.015.
Values may be sent and summed in bfloat16 or wider, within the bound.
No kernel may reach another device: no remote copies, remote signals or barrier semaphores. Data moves between devices by JAX's collectives and lax.ppermute only.
A program may use at most 192 MiB of HBM per device.

v0:
```python
import functools

import jax
import jax.numpy as jnp
from jax import lax
from jax.experimental import pallas as pl
from jax.experimental.pallas import tpu as pltpu
from jax.sharding import PartitionSpec as P

HEADS = 12
HEAD_DIM = 64
EPSILON = 1e-06
SCALE = 0.125
AXES = ("wide", "narrow")
SMALL = 128
BIAS_AT = 16
F32 = jnp.float32
BF16 = jnp.bfloat16
NT = (((1,), (1,)), ((), ()))
NN = (((1,), (0,)), ((), ()))
MIB = 1024 * 1024
DECLARED = 5.5e8
TIMES = {
    "pack": 1.3,
    "z_join": 0.3,
    "turn_tokens": 1.0,
    "project": 4.0,
    "attend": 8.4,
    "mix": 3.0,
    "inner": 11.0,
    "outer": 8.0,
    "slope": 6.0,
    "grad_outer": 2.6,
    "normed_back": 50.0,
    "add_halves": 0.5,
    "grad_inner": 3.2,
    "attend_back": 11.4,
    "plane_sum": 0.6,
    "pair_sum": 4.0,
    "stack_small": 0.1,
    "grad_first": 0.3,
    "tokens_back": 0.3,
    "finish": 0.8,
}


def dot(left, right, dims=NN):
    return lax.dot_general(left, right, dims, preferred_element_type=F32)


def vmem():
    return pl.BlockSpec(memory_space=pltpu.VMEM)


def smem():
    return pl.BlockSpec(memory_space=pltpu.SMEM)


def hbm():
    return pl.BlockSpec(memory_space=pltpu.HBM)


def sds(shape, dtype=BF16):
    return jax.ShapeDtypeStruct(shape, dtype)


def call(kernel, name, args, in_specs, out_shape, out_specs=None, scratch=(), limit=32, grid=None, prefetch=0, alias=None):
    many = isinstance(out_shape, (tuple, list))
    if out_specs is None:
        out_specs = tuple(vmem() for _ in out_shape) if many else vmem()
    if grid is None:
        spec = dict(in_specs=in_specs, out_specs=out_specs, scratch_shapes=list(scratch))
    else:
        spec = dict(
            grid_spec=pltpu.PrefetchScalarGridSpec(
                num_scalar_prefetch=prefetch,
                grid=grid,
                in_specs=in_specs,
                out_specs=out_specs,
                scratch_shapes=list(scratch),
            )
        )
    args = [
        pltpu.with_memory_space_constraint(a, pltpu.HBM) if i >= prefetch and in_specs[i - prefetch].memory_space is pltpu.HBM else a
        for i, a in enumerate(args)
    ]
    return pl.pallas_call(
        kernel,
        out_shape=out_shape,
        name=name,
        input_output_aliases=alias or {},
        compiler_params=pltpu.CompilerParams(vmem_limit_bytes=limit * MIB),
        cost_estimate=pl.CostEstimate(flops=int(TIMES[name] * DECLARED), bytes_accessed=0, transcendentals=0),
        **spec,
    )(*args)


def swap(value, mask):
    return lax.ppermute(value, AXES, [(i, i ^ mask) for i in range(32)])


def after(value, *others):
    return lax.optimization_barrier((value,) + others)[0]


def pack_kernel(*refs):
    given, (first, second, third), rest = refs[:15], refs[15:18], refs[18:]
    held, (scr, sems) = rest[:15], rest[15:]
    copies = [pltpu.make_async_copy(src, dst, sems.at[i]) for i, (src, dst) in enumerate(zip(given, held))]
    for copy in copies:
        copy.start()

    def spread(i, dst, col):
        copies[i].wait()
        total = held[i].shape[0]
        rows = dst.shape[0]
        blocks = total // rows
        scr[0:total] = held[i][...].astype(F32)
        for c in range(blocks):
            dst[:, col + c * 128 : col + (c + 1) * 128] = scr[pl.ds(c, rows, stride=blocks), :].astype(BF16)
        return col + blocks * 128

    col = 0
    for i in range(4):
        col = spread(i, first, col)
    for copy in copies[6:]:
        copy.wait()
    rows = first.shape[0]
    lines = [held[6 + i][...].astype(F32).reshape(1, rows) for i in range(8)]
    block = jnp.concatenate(lines, axis=0)
    block = jnp.concatenate([block, jnp.zeros((8, 128 - rows), F32)], axis=1)
    block = jnp.concatenate([block, jnp.zeros((120, 128), F32)], axis=0)
    scr[0:128] = block.T
    wide = held[14][...].astype(F32).reshape(1, 4 * rows)
    scr[0:1, BIAS_AT : BIAS_AT + 4 * rows] = wide
    first[:, col : col + SMALL] = scr[0:rows].astype(BF16)
    spread(4, second, 0)
    spread(5, third, 0)


def pack(weights, vectors, rows, width, hidden):
    flat = [w.reshape(-1, 128) for w in weights]
    ratio = hidden // width
    args = flat + vectors
    return call(
        pack_kernel,
        "pack",
        args,
        [hbm()] * len(args),
        (sds((rows, 4 * width + SMALL)), sds((rows, hidden)), sds((rows * ratio, width))),
        scratch=[pltpu.VMEM(a.shape, BF16) for a in args]
        + [pltpu.VMEM((max(f.shape[0] for f in flat), 128), F32), pltpu.SemaphoreType.DMA((15,))],
        limit=8,
    )


def z_join_kernel(at_ref, a0, a1, a2, a3, out):
    rows = a0.shape[0]
    z = lax.rem(at_ref[0], 4)
    for m, piece in enumerate((a0, a1, a2, a3)):
        out[pl.ds(pl.multiple_of((z ^ m) * rows, 8), rows), :] = piece[...]


def z_swaps(own):
    return [own] + [swap(own, m) for m in (1, 2, 3)]


def z_join(at, pieces):
    rows, cols = pieces[0].shape
    return call(z_join_kernel, "z_join", [at] + pieces, [smem()] + [vmem()] * 4, sds((4 * rows, cols)), limit=8)


def forward_halves(x, y):
    half = x.shape[1] // 256 * 128
    return [swap(x[:, :half], 16), swap(y[:, half:], 8)]


def row_blocks(own, x, y, diag):
    out = []
    for pieces in ([own], [x], [y], diag):
        out += [pieces, [swap(p, 4) for p in pieces]]
    return out


def flat_blocks(blocks):
    return [p for pieces in blocks for p in pieces]


PIECES = 10


def block_copies(at_ref, refs, scr, sems):
    group = at_ref[0] // 4
    lists, k = [], 0
    for m in range(8):
        halves = 2 if m >= 6 else 1
        col, mine = 0, []
        for _ in range(halves):
            rows, cols = refs[k].shape
            start = pl.multiple_of((group ^ m) * rows, 8)
            mine.append(pltpu.make_async_copy(refs[k], scr.at[pl.ds(start, rows), pl.ds(col, cols)], sems.at[k]))
            col += cols
            k += 1
        lists.append(mine)
    return lists


def fetch_all(at_ref, refs, scr, sems):
    lists = block_copies(at_ref, refs, scr, sems)
    for mine in lists:
        for copy in mine:
            copy.start()
    for mine in lists:
        for copy in mine:
            copy.wait()


def store_halves(group, value, keep, send, lead=()):
    part = value.shape[0] // 8
    core = lax.rem(group, 2)
    for b in range(8):
        slot = (group ^ b) // 2
        piece = value[b * part : (b + 1) * part]

        @pl.when(core == b % 2)
        def _():
            keep[lead + (pl.ds(slot, 1),)] = piece[None]

        @pl.when(core != b % 2)
        def _():
            send[lead + (pl.ds(slot, 1),)] = piece[None]


def turned(value):
    return value.astype(F32).T.astype(BF16)


def turn_kernel(at_ref, tokens, keep, send):
    store_halves(at_ref[0] // 4, turned(tokens[...]), keep, send)


def turn_tokens(at, tokens):
    size, width = tokens.shape
    out = sds((4, width // 8, size))
    return call(turn_kernel, "turn_tokens", [at, tokens], [smem(), vmem()], (out, out), limit=8)


def qkv_kernel(at_ref, tokens, *refs):
    pieces, (q, k, v, lines, bias, w_out, scr, sems) = refs[:PIECES], refs[PIECES:]
    width = tokens.shape[1]
    fetch_all(at_ref, pieces, scr, sems)
    w_out[...] = scr[:, 3 * width : 4 * width]
    tails = scr[:, 4 * width :].astype(F32)
    rows = tails.T[:16]
    lines[...] = rows
    each = width // 32
    for d in range(32):
        bias[:, 4 * each * d : 4 * each * (d + 1)] = tails[each * d : each * d + 1, BIAS_AT : BIAS_AT + 4 * each]
    x = tokens[...]
    q[...] = (dot(x, scr[:, :width]) + rows[0:1]).astype(BF16)
    k[...] = dot(x, scr[:, width : 2 * width]).astype(BF16)
    v[...] = (dot(x, scr[:, 2 * width : 3 * width]) + rows[1:2]).astype(BF16)


def project(at, tokens, blocks):
    size, width = tokens.shape
    cols = blocks[0][0].shape[1]
    args = [at, tokens] + flat_blocks(blocks)
    return call(
        qkv_kernel,
        "project",
        args,
        [smem(), vmem()] + [hbm()] * PIECES,
        (sds((size, width)),) * 3 + (sds((16, width), F32), sds((1, 4 * width), F32), sds((width, width))),
        scratch=[pltpu.VMEM((width, cols), BF16), pltpu.SemaphoreType.DMA((PIECES,))],
        limit=20,
    )


def head_lanes(h):
    lane = lax.broadcasted_iota(jnp.int32, (1, 2 * HEAD_DIM), 1)
    return (lane // HEAD_DIM) == h


def attend_kernel(len_ref, q_ref, k_ref, v_ref, mixed_ref, turned_ref, lse_ref):
    length = len_ref[0]
    q, k, v = q_ref[...], k_ref[...], v_ref[...]
    size = q.shape[0]
    keep = lax.broadcasted_iota(jnp.int32, (size, 1), 0) < length
    v_t = turned(v)
    parts = []
    for h in range(2):
        q_head = jnp.where(head_lanes(h), q.astype(F32) * SCALE, 0.0).astype(BF16)
        scores = jnp.where(keep, dot(k, q_head, NT), -1e30)
        top = jnp.max(scores, axis=0, keepdims=True)
        shifted = jnp.exp(scores - top)
        total = jnp.sum(shifted, axis=0, keepdims=True)
        mixed = dot(v_t[h * HEAD_DIM : (h + 1) * HEAD_DIM], shifted.astype(BF16)) / total
        parts.append(mixed)
        lse_ref[0, h : h + 1, :] = top + jnp.log(total)
    mixed = jnp.concatenate(parts, axis=0)
    turned_ref[...] = mixed.astype(BF16)
    mixed_ref[...] = mixed.T.astype(BF16)


def attend(lengths, q, k, v):
    size, width = q.shape
    pairs = width // 128
    tile = pl.BlockSpec((size, 128), lambda i, n: (0, i))
    return call(
        attend_kernel,
        "attend",
        [lengths, q, k, v],
        [tile] * 3,
        (sds((size, width)), sds((width, size)), sds((pairs, 2, size), F32)),
        out_specs=(
            tile,
            pl.BlockSpec((128, size), lambda i, n: (i, 0)),
            pl.BlockSpec((1, 2, size), lambda i, n: (i, 0, 0)),
        ),
        grid=(pairs,),
        prefetch=1,
        limit=16,
    )


def normed(values):
    centred = values - jnp.mean(values, axis=-1, keepdims=True)
    scale = lax.rsqrt(jnp.mean(centred * centred, axis=-1, keepdims=True) + EPSILON)
    return centred * scale, scale


def norm_back(grad, unit, scale):
    return scale * (
        grad - jnp.mean(grad, axis=-1, keepdims=True) - unit * jnp.mean(grad * unit, axis=-1, keepdims=True)
    )


def mix_kernel(at_ref, tokens, mixed, mixed_t, lines, w_out, unit_out, scale_out, normed_out, keep, send):
    group = at_ref[0] // 4
    normed_out[...] = mixed[...]
    step = 128

    def rows(i, carry):
        part = pl.ds(pl.multiple_of(i * step, step), step)
        resid = tokens[part, :].astype(F32) + dot(mixed[part, :], w_out[...]) + lines[2:3]
        unit, scale = normed(resid)
        unit_out[part, :] = unit
        scale_out[part, :] = jnp.broadcast_to(scale, (step, scale_out.shape[1]))
        normed_out[part, :] = (unit * lines[3:4] + lines[4:5]).astype(BF16)
        return carry

    lax.fori_loop(0, tokens.shape[0] // step, rows, 0)
    store_halves(group, mixed_t[...], keep, send, (0,))
    store_halves(group, turned(normed_out[...]), keep, send, (1,))


def mix_stage(at, tokens, mixed, mixed_t, lines, w_out):
    size, width = tokens.shape
    half = sds((2, 4, width // 8, size))
    return call(
        mix_kernel,
        "mix",
        [at, tokens, mixed, mixed_t, lines, w_out],
        [smem()] + [vmem()] * 5,
        (sds((size, width), F32), sds((size, 128), F32), sds((size, width)), half, half),
        limit=16,
    )


def inner_kernel(at_ref, values, bias, *refs):
    pieces = refs[:PIECES]
    (activ, slope, weights, keep, send, scr, sems, out_sem) = refs[PIECES:]
    part = activ.shape[1] // 8
    group = at_ref[0] // 4
    core = lax.rem(group, 2)
    fetch_all(at_ref, pieces, scr, sems)
    copy = pltpu.make_async_copy(scr, weights, out_sem)
    copy.start()

    def step(b, carry):
        at = pl.multiple_of(b * part, 128)
        inner = dot(values[...], scr[:, pl.ds(at, part)]) + bias[:, pl.ds(at, part)]
        share = 0.5 * (1.0 + lax.erf(inner * 0.7071067811865476))
        result = inner * share
        activ[:, pl.ds(at, part)] = result.astype(BF16)
        slope[:, pl.ds(at, part)] = (share + inner * (0.3989422804014327 * jnp.exp(-0.5 * inner * inner))).astype(BF16)
        across = result.T.astype(BF16)
        slot = (group ^ b) // 2

        @pl.when(core == lax.rem(b, 2))
        def _():
            keep[pl.ds(slot, 1)] = across[None]

        @pl.when(core != lax.rem(b, 2))
        def _():
            send[pl.ds(slot, 1)] = across[None]

        return carry

    lax.fori_loop(0, 8, step, 0)
    copy.wait()


def inner_stage(at, values, bias, blocks):
    size, width = values.shape
    hidden = bias.shape[1]
    args = [at, values, bias] + flat_blocks(blocks)
    half = sds((4, hidden // 8, size))
    return call(
        inner_kernel,
        "inner",
        args,
        [smem()] + [vmem()] * 2 + [hbm()] * PIECES,
        (sds((size, hidden)), sds((size, hidden)), sds((width, hidden)), half, half),
        out_specs=(vmem(),) * 2 + (hbm(),) + (vmem(),) * 2,
        scratch=[
            pltpu.VMEM((width, hidden), BF16),
            pltpu.SemaphoreType.DMA((PIECES,)),
            pltpu.SemaphoreType.DMA,
        ],
        limit=32,
    )


def outer_kernel(at_ref, len_ref, activ, values, lines, cot, *refs):
    pieces, (output, resid_grad, outer_grad, sums, scr, acc, sems) = refs[:PIECES], refs[PIECES:]
    size = values.shape[0]
    part = activ.shape[1] // 8
    group = at_ref[0] // 4
    lists = block_copies(at_ref, pieces, scr, sems)
    for mine in lists:
        for copy in mine:
            copy.start()
    resid = values[...].astype(F32) + lines[5:6]
    for m, mine in enumerate(lists):
        for copy in mine:
            copy.wait()
        at = pl.multiple_of((group ^ m) * part, 128)
        resid += dot(activ[:, pl.ds(at, part)], scr[pl.ds(at, part), :])
    acc[...] = resid
    gain, shift = lines[6:7], lines[7:8]
    sums[...] = jnp.zeros_like(sums)
    step = 128

    def rows(i, carry):
        part = pl.ds(pl.multiple_of(i * step, step), step)
        unit, scale = normed(acc[part, :])
        valid = lax.broadcasted_iota(jnp.int32, (step, 1), 0) + i * step < len_ref[0]
        output[part, :] = jnp.where(valid, unit * gain + shift, 0.0).astype(BF16)
        grad = jnp.where(valid, cot[part, :].astype(F32), 0.0)
        sums[6:7] += jnp.sum(grad * unit, axis=0, keepdims=True)
        sums[7:8] += jnp.sum(grad, axis=0, keepdims=True)
        grad = norm_back(grad * gain, unit, scale)
        resid_grad[part, :] = grad
        rounded = grad.astype(BF16)
        outer_grad[part, :] = rounded
        sums[5:6] += jnp.sum(rounded.astype(F32), axis=0, keepdims=True)
        return carry

    lax.fori_loop(0, size // step, rows, 0)


def outer_stage(at, lengths, activ, values, lines, cot, blocks):
    size, width = values.shape
    hidden = activ.shape[1]
    args = [at, lengths, activ, values, lines, cot] + flat_blocks(blocks)
    return call(
        outer_kernel,
        "outer",
        args,
        [smem(), smem()] + [vmem()] * 4 + [hbm()] * PIECES,
        (sds((size, width)), sds((size, width), F32), sds((size, width)), sds((8, width), F32)),
        scratch=[
            pltpu.VMEM((hidden, width), BF16),
            pltpu.VMEM((size, width), F32),
            pltpu.SemaphoreType.DMA((PIECES,)),
        ],
        limit=32,
    )


def slope_kernel(at_ref, outer_grad, slope, *refs):
    pieces, (inner_grad, sums, scr, sems) = refs[:PIECES], refs[PIECES:]
    part = slope.shape[1] // 8
    group = at_ref[0] // 4
    lists = block_copies(at_ref, pieces, scr, sems)
    for mine in lists:
        for copy in mine:
            copy.start()
    grad = outer_grad[...]
    for m, mine in enumerate(lists):
        for copy in mine:
            copy.wait()
        at = pl.multiple_of((group ^ m) * part, 128)
        back = dot(grad, scr[pl.ds(at, part), :], NT) * slope[:, pl.ds(at, part)].astype(F32)
        rounded = back.astype(BF16)
        inner_grad[:, pl.ds(at, part)] = rounded
        sums[:, pl.ds(at, part)] = jnp.sum(rounded.astype(F32), axis=0, keepdims=True)


def slope_stage(at, outer_grad, slope, blocks):
    size, width = outer_grad.shape
    hidden = slope.shape[1]
    args = [at, outer_grad, slope] + flat_blocks(blocks)
    return call(
        slope_kernel,
        "slope",
        args,
        [smem()] + [vmem()] * 2 + [hbm()] * PIECES,
        (sds((size, hidden)), sds((1, hidden), F32)),
        scratch=[pltpu.VMEM((hidden, width), BF16), pltpu.SemaphoreType.DMA((PIECES,))],
        limit=32,
    )


def normed_back_kernel(inner_grad, resid_two, unit_ref, scale_ref, lines, w_out, weights, resid_grad, attn_low, attn_high, mixed_grad, sums):
    width = unit_ref.shape[1]
    hidden = inner_grad.shape[1]
    grad = resid_two[...]
    for c in range(0, hidden, width):
        grad += dot(inner_grad[:, c : c + width], weights[:, c : c + width], NT)
    half = attn_low.shape[1]
    resid_grad[...] = grad
    sums[...] = jnp.zeros_like(sums)
    step = 128

    def rows(i, carry):
        part = pl.ds(pl.multiple_of(i * step, step), step)
        unit = unit_ref[part, :]
        grad = resid_grad[part, :]
        sums[3:4] += jnp.sum(grad * unit, axis=0, keepdims=True)
        sums[4:5] += jnp.sum(grad, axis=0, keepdims=True)
        grad = norm_back(grad * lines[3:4], unit, scale_ref[part, 0:1])
        resid_grad[part, :] = grad
        rounded = grad.astype(BF16)
        attn_low[part, :] = rounded[:, :half]
        attn_high[part, :] = rounded[:, half:]
        sums[2:3] += jnp.sum(rounded.astype(F32), axis=0, keepdims=True)
        return carry

    lax.fori_loop(0, grad.shape[0] // step, rows, 0)
    back = dot(attn_low[...], w_out[:, :half], NT) + dot(attn_high[...], w_out[:, half:], NT)
    mixed_grad[...] = back.astype(BF16)


def normed_back(inner_grad, resid_two, unit, scale, lines, w_out, weights):
    size, width = unit.shape
    hidden = inner_grad.shape[1]
    args = [inner_grad, resid_two, unit, scale, lines, w_out, weights]
    return call(
        normed_back_kernel,
        "normed_back",
        args,
        [vmem()] * 7,
        (sds((size, width), F32),)
        + (sds((size, width // 2)),) * 2
        + (sds((size, width)), sds((8, width), F32)),
        limit=32,
    )


def attend_back_kernel(len_ref, q_ref, k_ref, v_ref, mixed_ref, grad_ref, lse_ref, grads_ref, qs_ref, vs_ref):
    length = len_ref[0]
    q, k, v, grad = q_ref[...], k_ref[...], v_ref[...], grad_ref[...]
    size = q.shape[0]
    keep = lax.broadcasted_iota(jnp.int32, (size, 1), 0) < length
    k_t = turned(k)
    prod_t = turned(grad).astype(F32) * mixed_ref[...].astype(F32)
    q_grad, k_grad, v_grad = [], 0.0, 0.0
    for h in range(2):
        mine = head_lanes(h)
        q_head = jnp.where(mine, q.astype(F32) * SCALE, 0.0).astype(BF16)
        g_head = jnp.where(mine, grad, jnp.zeros_like(grad))
        scores = jnp.where(keep, dot(k, q_head, NT), -1e30)
        probs = jnp.exp(scores - lse_ref[0, h : h + 1, :])
        delta = jnp.sum(prod_t[h * HEAD_DIM : (h + 1) * HEAD_DIM], axis=0, keepdims=True)
        prob_grad = dot(v, g_head, NT)
        score_grad = (probs * (prob_grad - delta)).astype(BF16)
        v_grad += dot(probs.astype(BF16), g_head)
        k_grad += dot(score_grad, q_head)
        q_grad.append(dot(k_t[h * HEAD_DIM : (h + 1) * HEAD_DIM], score_grad))
    q_rounded = (jnp.concatenate(q_grad, axis=0) * SCALE).T.astype(BF16)
    v_rounded = v_grad.astype(BF16)
    grads_ref[0] = q_rounded
    grads_ref[1] = k_grad.astype(BF16)
    grads_ref[2] = v_rounded
    qs_ref[...] = jnp.sum(q_rounded.astype(F32), axis=0, keepdims=True)
    vs_ref[...] = jnp.sum(v_rounded.astype(F32), axis=0, keepdims=True)


def attend_back(lengths, q, k, v, mixed_t, grad, lse):
    size, width = q.shape
    pairs = width // 128
    tile = pl.BlockSpec((size, 128), lambda i, n: (0, i))
    out = pl.BlockSpec((3, size, 128), lambda i, n: (0, 0, i))
    line = pl.BlockSpec((1, 128), lambda i, n: (0, i))
    return call(
        attend_back_kernel,
        "attend_back",
        [lengths, q, k, v, mixed_t, grad, lse],
        [tile] * 3
        + [
            pl.BlockSpec((128, size), lambda i, n: (i, 0)),
            tile,
            pl.BlockSpec((1, 2, size), lambda i, n: (i, 0, 0)),
        ],
        (sds((3, size, width)),) + (sds((1, width), F32),) * 2,
        out_specs=(out,) + (line,) * 2,
        grid=(pairs,),
        prefetch=1,
        limit=16,
    )


def tokens_kernel(at_ref, resid_grad, *refs):
    grads, pieces, (out, scr, sems) = refs[0], refs[1 : 1 + PIECES], refs[1 + PIECES :]
    width = resid_grad.shape[1]
    fetch_all(at_ref, pieces, scr, sems)
    total = resid_grad[...]
    for i in range(3):
        total += dot(grads[i], scr[:, i * width : (i + 1) * width], NT)
    out[...] = total.astype(BF16)


def tokens_back(at, resid_grad, grads, blocks):
    size, width = resid_grad.shape
    cols = blocks[0][0].shape[1]
    args = [at, resid_grad, grads] + flat_blocks(blocks)
    return call(
        tokens_kernel,
        "tokens_back",
        args,
        [smem()] + [vmem()] * 2 + [hbm()] * PIECES,
        sds((size, width)),
        scratch=[pltpu.VMEM((width, cols), BF16), pltpu.SemaphoreType.DMA((PIECES,))],
        limit=24,
    )


def small_kernel(one, two, q_sum, v_sum, bias, out):
    width = one.shape[1]
    out[0:8] = one[...] + two[...]
    out[8:16] = jnp.zeros((8, width), F32)
    out[0:1], out[1:2] = q_sum[...], v_sum[...]
    for r in range(4):
        out[12 + r : 13 + r] = bias[:, r * width : (r + 1) * width]


def stack_small(*args):
    one = args[0]
    return call(small_kernel, "stack_small", list(args), [vmem()] * 5, sds((16, one.shape[1]), F32), limit=4)


def put_slots(value, col, outs):
    s0, s1, s2, s3a, s3b = outs
    part, cols = s0.shape
    half = s3a.shape[1]
    width = value.shape[1]
    for s, out in enumerate((s0, s1, s2)):
        out[:, col : col + width] = value[s * part : (s + 1) * part]
    last = value[3 * part : 4 * part]
    cut = min(max(half - col, 0), width)
    if cut > 0:
        s3a[:, col : col + cut] = last[:, :cut]
    if cut < width:
        s3b[:, col + cut - half : col + width - half] = last[:, cut:]


def slot_shapes(part, cols):
    half = cols // 256 * 128
    return (sds((part, cols)),) * 3 + (sds((part, half)), sds((part, cols - half)))


def grad_kernel(plan, small, *refs):
    outs = refs[-5:]
    if small:
        outs, scr = refs[-6:-1], refs[-1]
    part = outs[0].shape[0]
    col = 0
    for left, lead, mine, came, which in plan:
        rows = 4 * part
        size = refs[left].shape[-1]
        a = refs[left][lead] if lead is not None else refs[left][...]
        b = refs[left + 1][lead] if lead is not None else refs[left + 1][...]
        a, b = a.reshape(rows, size), b.reshape(rows, size)
        total = refs[mine].shape[-1]
        step = min(total, 768)
        for start in range(0, total, step):
            at = which + (slice(None), slice(start, start + step))
            value = dot(a, refs[mine][at]) + dot(b, refs[came][at])
            put_slots(value.astype(BF16), col, outs)
            col += step
    if small:
        at_ref, own, came = refs[small], refs[small + 1], refs[small + 2]
        both = own[...] + came[...]
        padded = jnp.concatenate([both, jnp.zeros((SMALL - both.shape[0], both.shape[1]), F32)], axis=0)
        scr[...] = padded.T
        each = 4 * scr.shape[0] // 32
        wide = scr.shape[0]
        for d in range(32):
            row, lane = 12 + each * d // wide, each * d % wide
            scr[wide // 32 * d : wide // 32 * d + 1, BIAS_AT : BIAS_AT + each] = both[row : row + 1, lane : lane + each]
        group = at_ref[0] // 4
        value = jnp.concatenate(
            [scr[pl.ds(pl.multiple_of((group ^ (2 * s)) * part, 8), part), :] for s in range(4)], axis=0
        )
        put_slots(value.astype(BF16), col, outs)


def weight_grad(name, args, plan, part, cols, small=None):
    specs = [vmem()] * len(args)
    scratch = []
    if small:
        specs[small] = smem()
        scratch = [pltpu.VMEM((8 * part, SMALL), F32)]
    return call(
        functools.partial(grad_kernel, plan, small),
        name,
        args,
        specs,
        slot_shapes(part, cols),
        scratch=scratch,
        limit=32,
    )


def add_kernel(x_ref, p_ref, y_ref, q_ref, x_out, y_out):
    x_out[...] = (x_ref[...].astype(F32) + p_ref[...].astype(F32)).astype(BF16)
    y_out[...] = (y_ref[...].astype(F32) + q_ref[...].astype(F32)).astype(BF16)


def add_halves(x, p, y, q):
    part, cols = x.shape
    half = p.shape[1]
    rest = cols - half
    if half != rest:
        return add_uneven(x, p, y, q)
    low = pl.BlockSpec((part, half), lambda i: (0, 0))
    high = pl.BlockSpec((part, half), lambda i: (0, 1))
    return call(
        add_kernel,
        "add_halves",
        [x, p, y, q],
        [low, low, high, low],
        (sds(x.shape), sds(y.shape)),
        out_specs=(low, high),
        grid=(1,),
        alias={0: 0, 2: 1},
        limit=16,
    )


def uneven_kernel(x_ref, p_ref, y_ref, q_ref, x_out, y_out):
    half = p_ref.shape[1]
    x_out[...] = x_ref[...]
    y_out[...] = y_ref[...]
    x_out[:, :half] = (x_ref[:, :half].astype(F32) + p_ref[...].astype(F32)).astype(BF16)
    y_out[:, half:] = (y_ref[:, half:].astype(F32) + q_ref[...].astype(F32)).astype(BF16)


def add_uneven(x, p, y, q):
    return call(
        uneven_kernel,
        "add_halves",
        [x, p, y, q],
        [vmem()] * 4,
        (sds(x.shape), sds(y.shape)),
        limit=16,
    )


def plane_sum_kernel(at_ref, a0, a1, a2, keep, send, total):
    total[...] = a0[...].astype(F32) + (a1[...].astype(F32) + a2[...].astype(F32))
    rows = keep.shape[0] // 2
    z = lax.rem(at_ref[0], 4)
    for m in range(4):
        out = (keep, send)[m // 2]
        part = total[pl.ds(pl.multiple_of((z ^ m) * rows, 8), rows), :]
        out[m % 2 * rows : (m % 2 + 1) * rows] = part.astype(BF16)


def plane_sum(at, pieces):
    part, cols = pieces[0].shape
    return call(
        plane_sum_kernel,
        "plane_sum",
        [at] + pieces,
        [smem()] + [vmem()] * 3,
        (sds((part // 2, cols)),) * 2,
        scratch=[pltpu.VMEM((part, cols), F32)],
        limit=16,
    )


def pair_sum_kernel(keep, came, own, send):
    rows = own.shape[0]
    total = keep[...].astype(F32) + came[...].astype(F32)
    own[...] = total[:rows]
    send[...] = total[rows:].astype(BF16)


def pair_sum(keep, came):
    rows, cols = keep.shape[0] // 2, keep.shape[1]
    return call(
        pair_sum_kernel,
        "pair_sum",
        [keep, came],
        [vmem()] * 2,
        (sds((rows, cols), F32), sds((rows, cols))),
        limit=8,
    )


def finish_kernel(widths, tail, own, came, *outs):
    total = own[...] + came[...].astype(F32)
    rows = total.shape[0]
    col = 0
    for width, out in zip(widths, outs):
        blocks = width // 128
        for c in range(blocks):
            out[pl.ds(c, rows, stride=blocks), :] = total[:, col + c * 128 : col + (c + 1) * 128]
        col += width
    if tail:
        block = jnp.concatenate([total[:, col : col + SMALL], jnp.zeros((SMALL - rows, SMALL), F32)], axis=0).T
        for i in range(8):
            outs[len(widths) + i][...] = block[i : i + 1, :rows].reshape(rows)
        outs[len(widths) + 8][...] = total[0:1, col + BIAS_AT : col + BIAS_AT + 4 * rows].reshape(4 * rows)


def finish(pieces, widths, tail=False):
    rows = pieces[0].shape[0]
    shapes = [sds((rows * w // 128, 128), F32) for w in widths]
    if tail:
        shapes += [sds((rows,), F32)] * 8 + [sds((4 * rows,), F32)]
    outs = call(
        functools.partial(finish_kernel, widths, tail),
        "finish",
        pieces,
        [vmem()] * 2,
        tuple(shapes),
        limit=16,
    )
    return [o.reshape(-1) for o in outs]


def scatter_plane(slots, *done):
    s0, s1, s2, s3a, s3b = slots
    p, q = swap(s3a, 16), swap(s3b, 8)
    s1 = after(s1, *done)
    x, y = add_halves(s1, p, s2, q)
    return [s0, swap(x, 8), swap(y, 16), x]


def first_z(sums, *done):
    keep, send = sums
    return pair_sum(after(keep, *done), swap(send, 2))


def blocked_layer(
    tokens,
    lengths,
    query_weight,
    query_bias,
    key_weight,
    value_weight,
    value_bias,
    output_weight,
    output_bias,
    attn_gain,
    attn_shift,
    inner_weight,
    inner_bias,
    outer_weight,
    outer_bias,
    ffn_gain,
    ffn_shift,
    cotangent,
):
    size, width = tokens.shape
    rows = query_weight.shape[0] // width
    hidden = inner_weight.shape[0] // rows
    ratio = hidden // width
    at = lax.axis_index(AXES).astype(jnp.int32).reshape(1)

    first, second, third = pack(
        [query_weight, key_weight, value_weight, output_weight, inner_weight, outer_weight],
        [query_bias, value_bias, output_bias, attn_gain, attn_shift, outer_bias, ffn_gain, ffn_shift, inner_bias],
        rows,
        width,
        hidden,
    )
    z_first = z_join(at, z_swaps(first))
    x_first, y_first = swap(z_first, 8), swap(z_first, 16)
    second_swaps = z_swaps(after(second, z_first))
    f_first = forward_halves(x_first, y_first)
    first_blocks = row_blocks(z_first, x_first, y_first, f_first)
    z_second = z_join(at, second_swaps)
    x_second, y_second = swap(z_second, 8), swap(z_second, 16)
    third_swaps = z_swaps(after(third, z_second))
    tok_keep, tok_send = turn_tokens(at, tokens)
    tok_came = swap(tok_send, 4)
    queries, key_rows, value_rows, lines, bias, w_out = project(at, tokens, first_blocks)
    mixed, mixed_t, lse = attend(lengths, queries, key_rows, value_rows)
    mixed, x_second, y_second, *third_swaps = lax.optimization_barrier((mixed, x_second, y_second, *third_swaps))
    f_second = forward_halves(x_second, y_second)
    unit, scale, values, b_keep, b_send = mix_stage(at, tokens, after(mixed, tok_came), mixed_t, lines, w_out)
    b_came = swap(b_send, 4)
    second_blocks = row_blocks(z_second, x_second, y_second, [after(f, values) for f in f_second])
    z_third = z_join(at, [after(third_swaps[0], *f_second)] + third_swaps[1:])
    x_third, y_third = swap(z_third, 8), swap(z_third, 16)
    activ, slope, w_inner, a_keep, a_send = inner_stage(at, after(values, z_third), bias, second_blocks)
    activ, x_third, y_third = lax.optimization_barrier((activ, x_third, y_third))
    f_third = forward_halves(x_third, y_third)
    third_blocks = row_blocks(z_third, x_third, y_third, f_third)
    a_came = swap(after(a_send, x_third), 4)
    activ = after(activ, a_came)
    output, resid_two_grad, outer_grad, sums_two = outer_stage(at, lengths, activ, values, lines, cotangent, third_blocks)

    outer_came = swap(outer_grad, 4)
    slots_a = weight_grad(
        "grad_outer",
        [a_keep, a_came, outer_grad, outer_came],
        [(0, None, 2, 3, ())],
        hidden // 8,
        width,
    )
    inner_grad, bias_grad = slope_stage(at, after(outer_grad, slots_a[0]), slope, third_blocks)
    plane_a = scatter_plane(slots_a, inner_grad)
    inner_came = swap(after(inner_grad, plane_a[3]), 4)
    resid_one_grad, attn_low, attn_high, mixed_grad, sums_one = normed_back(
        after(inner_grad, plane_a[3]), resid_two_grad, unit, scale, lines, w_out, w_inner
    )
    low_came, high_came = swap(attn_low, 4), swap(attn_high, 4)
    slots_b = weight_grad(
        "grad_inner",
        [b_keep, b_came, attn_low, low_came, attn_high, high_came, inner_grad, inner_came],
        [(0, 0, 2, 3, ()), (0, 0, 4, 5, ()), (0, 1, 6, 7, ())],
        width // 8,
        width + hidden,
    )
    sums_a = plane_sum(at, [after(plane_a[0], slots_b[0])] + plane_a[1:3])
    grads, q_sum, v_sum = attend_back(
        lengths, queries, key_rows, value_rows, mixed_t, after(mixed_grad, sums_a[0]), lse
    )
    own_a, last_a = first_z(sums_a, grads)
    plane_b = scatter_plane(slots_b, own_a)
    grads_came = swap(after(grads, plane_b[3]), 4)
    (own_u,) = finish([own_a, swap(last_a, 1)], [width])
    small = stack_small(sums_one, sums_two, q_sum, v_sum, bias_grad)
    small_came = swap(small, 4)
    args = [tok_keep, tok_came, grads, grads_came]
    plan = [(0, None, 2, 3, (i,)) for i in range(3)]
    slots_c = weight_grad(
        "grad_first",
        args + [at, small, small_came],
        plan,
        width // 8,
        3 * width + SMALL,
        small=len(args),
    )
    slots_c = list(slots_c)
    slots_c[3], slots_c[4], _ = lax.optimization_barrier((slots_c[3], slots_c[4], own_u))
    tokens_grad = tokens_back(at, after(resid_one_grad, slots_c[3]), grads, first_blocks)
    sums_b = plane_sum(at, [after(plane_b[0], tokens_grad)] + plane_b[1:3])
    plane_c = scatter_plane(slots_c, sums_b[0])
    own_b, last_b = first_z(sums_b)
    sums_c = plane_sum(at, [after(plane_c[0], own_b)] + plane_c[1:3])
    own_o, own_i = finish([own_b, swap(last_b, 1)], [width, hidden])
    own_c, last_c = first_z(sums_c)
    own_q, own_k, own_v, qb, vb, ob, ag, ash, ub, fg, fs, ib = finish(
        [own_c, swap(last_c, 1)], [width] * 3, tail=True
    )
    return (output, tokens_grad, own_q, qb, own_k, own_v, vb, own_o, ob, ag, ash, own_i, ib, own_u, ub, fg, fs)


def layer_norm(values, norm_gain, norm_shift):
    row_mean = jnp.mean(values, axis=-1, keepdims=True)
    centred = values - row_mean
    row_var = jnp.mean(centred * centred, axis=-1, keepdims=True)
    return centred * lax.rsqrt(row_var + EPSILON) * norm_gain + norm_shift


def gelu_exact(values):
    return jax.nn.gelu(values, approximate=False)


def matmul(left, right):
    return jnp.dot(left, right, preferred_element_type=jnp.float32)


def left_product(left, right):
    return jnp.einsum("rd,rf->df", left, right, preferred_element_type=jnp.float32)


def right_product(left, right):
    return jnp.einsum("rf,df->rd", left, right, preferred_element_type=jnp.float32)


def column_sums(values):
    return jnp.sum(values.astype(jnp.float32), axis=0)


def unpack(gathered, model_width):
    (
        query_weight,
        query_bias,
        key_weight,
        value_weight,
        value_bias,
        output_weight,
        output_bias,
        attn_gain,
        attn_shift,
        inner_weight,
        inner_bias,
        outer_weight,
        outer_bias,
        ffn_gain,
        ffn_shift,
    ) = gathered
    hidden_width = inner_bias.shape[0]
    return (
        query_weight.reshape(model_width, model_width),
        query_bias,
        key_weight.reshape(model_width, model_width),
        value_weight.reshape(model_width, model_width),
        value_bias,
        output_weight.reshape(model_width, model_width),
        output_bias,
        attn_gain.astype(jnp.float32),
        attn_shift.astype(jnp.float32),
        inner_weight.reshape(model_width, hidden_width),
        inner_bias,
        outer_weight.reshape(hidden_width, model_width),
        outer_bias,
        ffn_gain.astype(jnp.float32),
        ffn_shift.astype(jnp.float32),
    )


def scores_of(query_seq, key_seq, keep_row):
    scores = (
        jnp.einsum("qhd,khd->hqk", query_seq, key_seq, preferred_element_type=jnp.float32) * SCALE
    )
    return jnp.where(keep_row[None, None, :], scores, -1e30)


def attend_forward(seq_item):
    query_seq, key_seq, value_seq, keep_row = seq_item
    scores = scores_of(query_seq, key_seq, keep_row)
    top = jnp.max(scores, axis=-1, keepdims=True)
    shifted_exp = jnp.exp(scores - top)
    total = jnp.sum(shifted_exp, axis=-1, keepdims=True)
    probs = (shifted_exp / total).astype(jnp.bfloat16)
    mixed = jnp.einsum("hqk,khd->qhd", probs, value_seq, preferred_element_type=jnp.float32)
    return (mixed.astype(jnp.bfloat16), (top + jnp.log(total))[..., 0])


def attend_backward(seq_item):
    query_seq, key_seq, value_seq, keep_row, log_total, mixed_grad = seq_item
    scores = scores_of(query_seq, key_seq, keep_row)
    probs = jnp.exp(scores - log_total[..., None])
    value_grad = jnp.einsum(
        "hqk,qhd->khd", probs.astype(jnp.bfloat16), mixed_grad, preferred_element_type=jnp.float32
    )
    prob_grad = jnp.einsum(
        "qhd,khd->hqk", mixed_grad, value_seq, preferred_element_type=jnp.float32
    )
    row_delta = jnp.sum(probs * prob_grad, axis=-1, keepdims=True)
    score_grad = (probs * (prob_grad - row_delta)).astype(jnp.bfloat16)
    query_grad = (
        jnp.einsum("hqk,khd->qhd", score_grad, key_seq, preferred_element_type=jnp.float32) * SCALE
    )
    key_grad = (
        jnp.einsum("hqk,qhd->khd", score_grad, query_seq, preferred_element_type=jnp.float32)
        * SCALE
    )
    return (
        query_grad.astype(jnp.bfloat16),
        key_grad.astype(jnp.bfloat16),
        value_grad.astype(jnp.bfloat16),
    )


def plain_layer(
    tokens,
    lengths,
    query_weight,
    query_bias,
    key_weight,
    value_weight,
    value_bias,
    output_weight,
    output_bias,
    attn_gain,
    attn_shift,
    inner_weight,
    inner_bias,
    outer_weight,
    outer_bias,
    ffn_gain,
    ffn_shift,
    cotangent,
):
    row_count = tokens.shape[0]
    model_width = tokens.shape[1]
    seq_count = lengths.shape[0]
    seq_len = row_count // seq_count
    gathered = (
        lax.all_gather(query_weight, ("wide", "narrow"), axis=0, tiled=True),
        lax.all_gather(query_bias, ("wide", "narrow"), axis=0, tiled=True),
        lax.all_gather(key_weight, ("wide", "narrow"), axis=0, tiled=True),
        lax.all_gather(value_weight, ("wide", "narrow"), axis=0, tiled=True),
        lax.all_gather(value_bias, ("wide", "narrow"), axis=0, tiled=True),
        lax.all_gather(output_weight, ("wide", "narrow"), axis=0, tiled=True),
        lax.all_gather(output_bias, ("wide", "narrow"), axis=0, tiled=True),
        lax.all_gather(attn_gain, ("wide", "narrow"), axis=0, tiled=True),
        lax.all_gather(attn_shift, ("wide", "narrow"), axis=0, tiled=True),
        lax.all_gather(inner_weight, ("wide", "narrow"), axis=0, tiled=True),
        lax.all_gather(inner_bias, ("wide", "narrow"), axis=0, tiled=True),
        lax.all_gather(outer_weight, ("wide", "narrow"), axis=0, tiled=True),
        lax.all_gather(outer_bias, ("wide", "narrow"), axis=0, tiled=True),
        lax.all_gather(ffn_gain, ("wide", "narrow"), axis=0, tiled=True),
        lax.all_gather(ffn_shift, ("wide", "narrow"), axis=0, tiled=True),
    )
    (
        full_qw,
        full_qb,
        full_kw,
        full_vw,
        full_vb,
        full_ow,
        full_ob,
        full_ag,
        full_as,
        full_iw,
        full_ib,
        full_uw,
        full_ub,
        full_fg,
        full_fs,
    ) = unpack(gathered, model_width)
    positions = jnp.arange(seq_len, dtype=jnp.int32)
    keep = positions[None, :] < lengths[:, None]
    row_valid = keep.reshape(row_count, 1).astype(jnp.float32)
    shape_four = (seq_count, seq_len, HEADS, HEAD_DIM)
    queries = (matmul(tokens, full_qw) + full_qb).astype(jnp.bfloat16)
    key_rows = matmul(tokens, full_kw).astype(jnp.bfloat16)
    value_rows = (matmul(tokens, full_vw) + full_vb).astype(jnp.bfloat16)
    query_four = queries.reshape(shape_four)
    key_four = key_rows.reshape(shape_four)
    value_four = value_rows.reshape(shape_four)
    mixed, log_total = lax.map(attend_forward, (query_four, key_four, value_four, keep))
    mixed_flat = mixed.reshape(row_count, model_width)
    resid_one = tokens.astype(jnp.float32) + matmul(mixed_flat, full_ow) + full_ob
    normed_one = layer_norm(resid_one, full_ag, full_as).astype(jnp.bfloat16)
    inner = matmul(normed_one, full_iw) + full_ib
    activ = gelu_exact(inner).astype(jnp.bfloat16)
    resid_two = normed_one.astype(jnp.float32) + matmul(activ, full_uw) + full_ub
    output = (layer_norm(resid_two, full_fg, full_fs) * row_valid).astype(jnp.bfloat16)
    (
        back_qw,
        back_qb,
        back_kw,
        back_vw,
        back_vb,
        back_ow,
        back_ob,
        back_ag,
        back_as,
        back_iw,
        back_ib,
        back_uw,
        back_ub,
        back_fg,
        back_fs,
    ) = unpack(gathered, model_width)
    out_grad = cotangent.astype(jnp.float32) * row_valid
    ignored, pull_two = jax.vjp(layer_norm, resid_two, back_fg, back_fs)
    resid_two_grad, ffn_gain_grad, ffn_shift_grad = pull_two(out_grad)
    outer_grad = resid_two_grad.astype(jnp.bfloat16)
    outer_weight_grad = left_product(activ, outer_grad)
    outer_bias_grad = column_sums(outer_grad)
    activ_grad = right_product(outer_grad, back_uw)
    ignored, pull_gelu = jax.vjp(gelu_exact, inner)
    inner_grad = pull_gelu(activ_grad)[0].astype(jnp.bfloat16)
    inner_weight_grad = left_product(normed_one, inner_grad)
    inner_bias_grad = column_sums(inner_grad)
    normed_grad = resid_two_grad + right_product(inner_grad, back_iw)
    ignored, pull_one = jax.vjp(layer_norm, resid_one, back_ag, back_as)
    resid_one_grad, attn_gain_grad, attn_shift_grad = pull_one(normed_grad)
    attn_grad = resid_one_grad.astype(jnp.bfloat16)
    output_weight_grad = left_product(mixed_flat, attn_grad)
    output_bias_grad = column_sums(attn_grad)
    mixed_grad = right_product(attn_grad, back_ow).astype(jnp.bfloat16)
    query_grad, key_grad, value_grad = lax.map(
        attend_backward,
        (query_four, key_four, value_four, keep, log_total, mixed_grad.reshape(shape_four)),
    )
    query_grad = query_grad.reshape(row_count, model_width)
    key_grad = key_grad.reshape(row_count, model_width)
    value_grad = value_grad.reshape(row_count, model_width)
    query_weight_grad = left_product(tokens, query_grad)
    key_weight_grad = left_product(tokens, key_grad)
    value_weight_grad = left_product(tokens, value_grad)
    query_bias_grad = column_sums(query_grad)
    value_bias_grad = column_sums(value_grad)
    tokens_grad = (
        resid_one_grad
        + right_product(query_grad, back_qw)
        + right_product(key_grad, back_kw)
        + right_product(value_grad, back_vw)
    ).astype(jnp.bfloat16)
    (
        own_qw,
        own_qb,
        own_kw,
        own_vw,
        own_vb,
        own_ow,
        own_ob,
        own_ag,
        own_as,
        own_iw,
        own_ib,
        own_uw,
        own_ub,
        own_fg,
        own_fs,
    ) = (
        lax.psum_scatter(
            query_weight_grad.reshape(-1), ("wide", "narrow"), scatter_dimension=0, tiled=True
        ),
        lax.psum_scatter(query_bias_grad, ("wide", "narrow"), scatter_dimension=0, tiled=True),
        lax.psum_scatter(
            key_weight_grad.reshape(-1), ("wide", "narrow"), scatter_dimension=0, tiled=True
        ),
        lax.psum_scatter(
            value_weight_grad.reshape(-1), ("wide", "narrow"), scatter_dimension=0, tiled=True
        ),
        lax.psum_scatter(value_bias_grad, ("wide", "narrow"), scatter_dimension=0, tiled=True),
        lax.psum_scatter(
            output_weight_grad.reshape(-1), ("wide", "narrow"), scatter_dimension=0, tiled=True
        ),
        lax.psum_scatter(output_bias_grad, ("wide", "narrow"), scatter_dimension=0, tiled=True),
        lax.psum_scatter(attn_gain_grad, ("wide", "narrow"), scatter_dimension=0, tiled=True),
        lax.psum_scatter(attn_shift_grad, ("wide", "narrow"), scatter_dimension=0, tiled=True),
        lax.psum_scatter(
            inner_weight_grad.reshape(-1), ("wide", "narrow"), scatter_dimension=0, tiled=True
        ),
        lax.psum_scatter(inner_bias_grad, ("wide", "narrow"), scatter_dimension=0, tiled=True),
        lax.psum_scatter(
            outer_weight_grad.reshape(-1), ("wide", "narrow"), scatter_dimension=0, tiled=True
        ),
        lax.psum_scatter(outer_bias_grad, ("wide", "narrow"), scatter_dimension=0, tiled=True),
        lax.psum_scatter(ffn_gain_grad, ("wide", "narrow"), scatter_dimension=0, tiled=True),
        lax.psum_scatter(ffn_shift_grad, ("wide", "narrow"), scatter_dimension=0, tiled=True),
    )
    return (
        output,
        tokens_grad,
        own_qw,
        own_qb,
        own_kw,
        own_vw,
        own_vb,
        own_ow,
        own_ob,
        own_ag,
        own_as,
        own_iw,
        own_ib,
        own_uw,
        own_ub,
        own_fg,
        own_fs,
    )


def solution(mesh):
    split = P(AXES)
    rows = P(AXES, None)
    blocked = mesh.shape["wide"] == 8 and mesh.shape["narrow"] == 4
    return jax.shard_map(
        blocked_layer if blocked else plain_layer,
        mesh=mesh,
        in_specs=(rows,) + (split,) * 16 + (rows,),
        out_specs=(rows, rows) + (split,) * 15,
        check_vma=False,
    )
```

profile of v0, /device:TPU:0, one launch (start us, length us, event | category | flops | bytes accessed | tf_op | source)
XLA Modules:
  0.0 224.2 jit_solution(8790151706447534477)
XLA Ops:
  2.0 5.1 %collective-permute-start.2 = (bf16[24,3200]{1,0:T(8,128)(2,1)S(1)}, bf16[24,3200]{1,0:T(8,128)(2,1)S(1)}, u32[]{:S(2)}, u32[]{:S(2)}) collective-permute-start(bf16[24,3200]{1,0:T(8,128)(2,1)S(1)} %get-tuple-element.135.a0), channel_id=1, source_target_pairs={{0,3},{1,2},{2,1},{3,0},{4,7},{5,6},{6,5},{7,4},{8,11},{9,10},{10,... | collective-permute-start | bytes 460808 | tf_op jit(solution)/shard_map/ppermute | solution.py:99
  7.8 4.3 %collective-permute-done.2.a3 = bf16[24,3200]{1,0:T(8,128)(2,1)S(1)} collective-permute-done((bf16[24,3200]{1,0:T(8,128)(2,1)S(1)}, bf16[24,3200]{1,0:T(8,128)(2,1)S(1)}, u32[]{:S(2)}, u32[]{:S(2)}) %collective-permute-start.2) | collective-permute-done | bytes 153632 | tf_op jit(solution)/shard_map/ppermute | solution.py:99
  12.1 8.1 %collective-permute-done.1.a2 = bf16[24,3200]{1,0:T(8,128)(2,1)S(1)} collective-permute-done((bf16[24,3200]{1,0:T(8,128)(2,1)S(1)}, bf16[24,3200]{1,0:T(8,128)(2,1)S(1)}, u32[]{:S(2)}, u32[]{:S(2)}) %collective-permute-start.1) | collective-permute-done | bytes 153632 | tf_op jit(solution)/shard_map/ppermute | solution.py:99
  23.3 2.5 %collective-permute-start.14 = (bf16[24,3072]{1,0:T(8,128)(2,1)S(1)}, bf16[24,3072]{1,0:T(8,128)(2,1)S(1)}, u32[]{:S(2)}, u32[]{:S(2)}) collective-permute-start(bf16[24,3072]{1,0:T(8,128)(2,1)S(1)} %get-tuple-element.141.a0), channel_id=1, source_target_pairs={{0,3},{1,2},{2,1},{3,0},{4,7},{5,6},{6,5},{7,4},{8,11},{9,10},{10,... | collective-permute-start | bytes 442376 | tf_op jit(solution)/shard_map/ppermute | solution.py:99
  25.8 1.9 collective-permute-start.12
  27.7 7.5 %collective-permute-done.6.refs_4_.refs_5_ = bf16[96,3200]{1,0:T(8,128)(2,1)S(1)} collective-permute-done((bf16[96,3200]{1,0:T(8,128)(2,1)S(1)}, bf16[96,3200]{1,0:T(8,128)(2,1)S(1)}, u32[]{:S(2)}, u32[]{:S(2)}) %collective-permute-start.6) | collective-permute-done | bytes 614432 | tf_op jit(solution)/shard_map/ppermute | solution.py:99
  39.0 4.3 %collective-permute-done.9.refs_7_.refs_8_ = bf16[96,1664]{1,0:T(8,128)(2,1)S(1)} collective-permute-done((bf16[96,1664]{1,0:T(8,128)(2,1)S(1)}, bf16[96,1664]{1,0:T(8,128)(2,1)S(1)}, u32[]{:S(2)}, u32[]{:S(2)}) %collective-permute-start.9) | collective-permute-done | bytes 319520 | tf_op jit(solution)/shard_map/ppermute | solution.py:99
  43.3 3.5 %collective-permute-done.8.refs_6_.refs_7_ = bf16[96,1536]{1,0:T(8,128)(2,1)S(1)} collective-permute-done((bf16[96,1536]{1,0:T(8,128)(2,1)S(1)}, bf16[96,1536]{1,0:T(8,128)(2,1)S(1)}, u32[]{:S(2)}, u32[]{:S(2)}) %collective-permute-start.8) | collective-permute-done | bytes 294944 | tf_op jit(solution)/shard_map/ppermute | solution.py:99
  48.6 2.3 %collective-permute-start.19 = (bf16[96,768]{1,0:T(8,128)(2,1)S(1)}, bf16[96,768]{1,0:T(8,128)(2,1)S(1)}, u32[]{:S(2)}, u32[]{:S(2)}) collective-permute-start(bf16[96,768]{1,0:T(8,128)(2,1)S(1)} %get-tuple-element.154.a0), channel_id=1, source_target_pairs={{0,3},{1,2},{2,1},{3,0},{4,7},{5,6},{6,5},{7,4},{8,11},{9,10},{10,... | collective-permute-start | bytes 442376 | tf_op jit(solution)/shard_map/ppermute | solution.py:99
  53.2 4.5 %project.1 = (bf16[512,768]{1,0:T(8,128)(2,1)S(1)}, bf16[512,768]{1,0:T(8,128)(2,1)S(1)}, bf16[512,768]{1,0:T(8,128)(2,1)S(1)}, f32[16,768]{1,0:T(8,128)S(1)}, f...) custom-call(s32[1]{0:T(128)} %bitcast.at_ref.refs_4_, bf16[512,768]{1,0:T(8,128)(2,1)S(1)} %copy-done.3, ...), custom_call_target="tpu_custom_call" | custom-call | flops 2200000000 | tf_op jit(solution)/shard_map/project/pallas_call | solution.py:87
  57.8 2.6 %collective-permute-start.17 = (bf16[96,768]{1,0:T(8,128)(2,1)S(1)}, bf16[96,768]{1,0:T(8,128)(2,1)S(1)}, u32[]{:S(2)}, u32[]{:S(2)}) collective-permute-start(bf16[96,768]{1,0:T(8,128)(2,1)S(1)} %get-tuple-element.154.a0), channel_id=1, source_target_pairs={{0,1},{1,0},{2,3},{3,2},{4,5},{5,4},{6,7},{7,6},{8,9},{9,8},{10,11... | collective-permute-start | bytes 442376 | tf_op jit(solution)/shard_map/ppermute | solution.py:99
  60.4 8.3 %attend.1 = (bf16[512,768]{1,0:T(8,128)(2,1)S(1)}, bf16[768,512]{1,0:T(8,128)(2,1)S(1)}, f32[6,2,512]{2,1,0:T(2,128)S(1)}) custom-call(s32[1]{0:T(128)S(6)} %copy.43.len_ref, bf16[512,768]{1,0:T(8,128)(2,1)S(1)} %get-tuple-element.136.q_ref, bf16[512,768]{1,0:T(8,128)(2,1)S(1)} %get-tuple-element.137.k_ref, bf16[512,768]{1,0:T(8,128)(2,1)S(1)} %get-tuple-element.138.v_ref), custom_call_target="tpu_custom_call" | custom-call | flops 4620000256 | tf_op jit(solution)/shard_map/attend/pallas_call | solution.py:87
  71.6 3.0 %mix.1 = (f32[512,768]{1,0:T(8,128)S(1)}, f32[512,128]{1,0:T(8,128)S(1)}, bf16[512,768]{1,0:T(8,128)(2,1)S(1)}, bf16[2,4,96,512]{3,2,1,0:T(8,128)(2,1)S(1)}, bf16[2,4,96,512]{3,2,1,0:T(8,128)(2,1)S(1)}) custom-call(s32[1]{0:T(128)} %bitcast.at_ref.refs_4_, bf16[512,768]{1,0:T(8,128)(2,1)S(1)} %copy-done.3, bf16[512,768]{1,0:T(8,128)(2,1)S(1)} %get-tuple-element.146.mixed, ...), custom_call_target="tpu_custom_call" | custom-call | flops 1650000000 | tf_op jit(solution)/shard_map/mix/pallas_call | solution.py:87
  76.3 3.6 %collective-permute-done.22.refs_7_ = bf16[96,1536]{1,0:T(8,128)(2,1)S(1)} collective-permute-done((bf16[96,1536]{1,0:T(8,128)(2,1)S(1)}, bf16[96,1536]{1,0:T(8,128)(2,1)S(1)}, u32[]{:S(2)}, u32[]{:S(2)}) %collective-permute-start.22) | collective-permute-done | bytes 294944 | tf_op jit(solution)/shard_map/ppermute | solution.py:99
  83.0 10.5 %inner.1 = (bf16[512,3072]{1,0:T(8,128)(2,1)S(1)}, bf16[512,3072]{1,0:T(8,128)(2,1)S(1)}, bf16[768,3072]{1,0:T(8,128)(2,1)S(1)}, bf16[4,384,512]{2,1,0:T(8,128)(2,1)S(1)}, bf16[4,384,512]{2,1,0:T(8,128)(2,1)S(1)}) custom-call(s32[1]{0:T(128)} %bitcast.at_ref.refs_4_, bf16[512,768]{1,0:T(8,128)(2,1)S(1)} %get-tuple-element.158.values, ...), custom_call_target="tpu_custom_call" | custom-call | flops 6049999872 | tf_op jit(solution)/shard_map/inner/pallas_call | solution.py:87
  93.5 2.2 copy-done.11
  98.8 6.7 %collective-permute-done.34.refs_6_ = bf16[384,384]{1,0:T(8,128)(2,1)S(1)} collective-permute-done((bf16[384,384]{1,0:T(8,128)(2,1)S(1)}, bf16[384,384]{1,0:T(8,128)(2,1)S(1)}, u32[]{:S(2)}, u32[]{:S(2)}) %collective-permute-start.34) | collective-permute-done | bytes 294944 | tf_op jit(solution)/shard_map/ppermute | solution.py:99
  110.7 8.8 %outer.1 = (bf16[512,768]{1,0:T(8,128)(2,1)}, f32[512,768]{1,0:T(8,128)S(1)}, bf16[512,768]{1,0:T(8,128)(2,1)S(1)}, f32[8,768]{1,0:T(8,128)S(1)}) custom-call(s32[1]{0:T(128)} %bitcast.at_ref.refs_4_, s32[1]{0:T(128)S(6)} %copy.43.len_ref, bf16[512,3072]{1,0:T(8,128)(2,1)S(1)} %get-tuple-element.167.activ, bf16[512,768]{1,0:T(8,128)(2,1)S(1)} %get-tuple-element.158.values, ...), custom_call_target="tpu_custom_call" | custom-call | flops 4400000000 | tf_op jit(solution)/shard_map/outer/pallas_call | solution.py:87
  119.8 2.1 collective-permute-done.38.refs_3_
  121.9 2.6 %grad_outer.1 = (bf16[384,768]{1,0:T(8,128)(2,1)S(1)}, bf16[384,768]{1,0:T(8,128)(2,1)S(1)}, bf16[384,768]{1,0:T(8,128)(2,1)S(1)}, bf16[384,384]{1,0:T(8,128)(2,1)S(1)}, bf16[384,384]{1,0:T(8,128)(2,1)S(1)}) custom-call(bf16[4,384,512]{2,1,0:T(8,128)(2,1)S(1)} %get-tuple-element.171.refs_0_, bf16[4,384,512]{2,1,0:T(8,128)(2,1)S(1)} %collective-permute-done.30.refs_1_, ...), custom_call_target="tpu_custom_call" | custom-call | flops 1430000000 | tf_op jit(solution)/shard_map/grad_outer/pallas_call | solution.py:87
  126.3 6.1 %slope.1 = (bf16[512,3072]{1,0:T(8,128)(2,1)S(1)}, f32[1,3072]{1,0:T(1,128)S(1)}) custom-call(s32[1]{0:T(128)} %bitcast.at_ref.refs_4_, bf16[512,768]{1,0:T(8,128)(2,1)S(1)} %get-tuple-element.173.refs_2_.outer_grad, bf16[512,3072]{1,0:T(8,128)(2,1)S(1)} %get-tuple-element.174.slope, bf16[384,768]{1,0:T(8,128)(2,1)} %copy-done.2, ...), custom_call_target="tpu_custom_call" | custom-call | flops 3300000000 | tf_op jit(solution)/shard_map/slope/pallas_call | solution.py:87
  137.0 6.6 %normed_back.1 = (f32[512,768]{1,0:T(8,128)S(1)}, bf16[512,384]{1,0:T(8,128)(2,1)S(1)}, bf16[512,384]{1,0:T(8,128)(2,1)S(1)}, bf16[512,768]{1,0:T(8,128)(2,1)S(1)}, f32[8,768]{1,0:T(8,128)S(1)}) custom-call(bf16[512,3072]{1,0:T(8,128)(2,1)S(1)} %get-tuple-element.182.inner_grad.refs_6_, f32[512,768]{1,0:T(8,128)S(1)} %get-tuple-element.183.resid_two, ...), custom_call_target="tpu_custom_call" | custom-call | flops 27499999232 | tf_op jit(solution)/shard_map/normed_back/pallas_call | solution.py:87
  146.0 3.4 %grad_inner.1 = (bf16[96,3840]{1,0:T(8,128)(2,1)S(1)}, bf16[96,3840]{1,0:T(8,128)(2,1)S(1)}, bf16[96,3840]{1,0:T(8,128)(2,1)S(1)}, bf16[96,1920]{1,0:T(8,128)(2,1)S(1)}, bf16[96,1920]{1,0:T(8,128)(2,1)S(1)}) custom-call(bf16[2,4,96,512]{3,2,1,0:T(8,128)(2,1)S(1)} %get-tuple-element.190.refs_0_, bf16[2,4,96,512]{3,2,1,0:T(8,128)(2,1)S(1)} %collective-permute-done.41.refs_1_, ...), custom_call_target="tpu_custom_call" | custom-call | flops 1760000000 | tf_op jit(solution)/shard_map/grad_inner/pallas_call | solution.py:87
  154.4 11.2 %attend_back.1 = (bf16[3,512,768]{2,1,0:T(8,128)(2,1)S(1)}, f32[1,768]{1,0:T(1,128)S(1)}, f32[1,768]{1,0:T(1,128)S(1)}) custom-call(s32[1]{0:T(128)S(6)} %copy.43.len_ref, bf16[512,768]{1,0:T(8,128)(2,1)S(1)} %get-tuple-element.136.q_ref, bf16[512,768]{1,0:T(8,128)(2,1)S(1)} %copy-done.6, bf16[512,768]{1,0:T(8,128)(2,1)S(1)} %copy-done.8, ...), custom_call_target="tpu_custom_call" | custom-call | flops 6270000128 | tf_op jit(solution)/shard_map/attend_back/pallas_call | solution.py:87
  170.1 4.6 %collective-permute-done.52.came = bf16[96,768]{1,0:T(8,128)(2,1)S(1)} collective-permute-done((bf16[96,768]{1,0:T(8,128)(2,1)S(1)}, bf16[96,768]{1,0:T(8,128)(2,1)S(1)}, u32[]{:S(2)}, u32[]{:S(2)}) %collective-permute-start.52) | collective-permute-done | bytes 147488 | tf_op jit(solution)/shard_map/ppermute | solution.py:99
  175.4 2.0 grad_first.1
  179.2 5.4 %tokens_back.1 = bf16[512,768]{1,0:T(8,128)(2,1)} custom-call(s32[1]{0:T(128)} %bitcast.at_ref.refs_4_, f32[512,768]{1,0:T(8,128)S(1)} %get-tuple-element.220.resid_grad, bf16[3,512,768]{2,1,0:T(8,128)(2,1)S(1)} %get-tuple-element.210.refs_2_.refs_0_, bf16[96,3200]{1,0:T(8,128)(2,1)} %copy-done, bf16[96,3200]{1,0:T(8,128)(2,1)} %copy-done.14, ...), custom_call_target="tpu_custom_call" | custom-call | flops 165000000 | tf_op jit(solution)/shard_map/tokens_back/pallas_call | solution.py:87
  187.6 2.1 collective-permute-start.55
  194.1 11.4 %collective-permute-done.55.came = bf16[48,3840]{1,0:T(8,128)(2,1)S(1)} collective-permute-done((bf16[48,3840]{1,0:T(8,128)(2,1)S(1)}, bf16[48,3840]{1,0:T(8,128)(2,1)S(1)}, u32[]{:S(2)}, u32[]{:S(2)}) %collective-permute-start.55) | collective-permute-done | bytes 368672 | tf_op jit(solution)/shard_map/ppermute | solution.py:99
  206.5 2.1 collective-permute-start.62
  208.6 9.4 %collective-permute-done.60.came = bf16[48,2432]{1,0:T(8,128)(2,1)S(1)} collective-permute-done((bf16[48,2432]{1,0:T(8,128)(2,1)S(1)}, bf16[48,2432]{1,0:T(8,128)(2,1)S(1)}, u32[]{:S(2)}, u32[]{:S(2)}) %collective-permute-start.60) | collective-permute-done | bytes 233504 | tf_op jit(solution)/shard_map/ppermute | solution.py:99
  219.0 4.3 %collective-permute-done.61.came = bf16[24,2432]{1,0:T(8,128)(2,1)S(1)} collective-permute-done((bf16[24,2432]{1,0:T(8,128)(2,1)S(1)}, bf16[24,2432]{1,0:T(8,128)(2,1)S(1)}, u32[]{:S(2)}, u32[]{:S(2)}) %collective-permute-start.61) | collective-permute-done | bytes 116768 | tf_op jit(solution)/shard_map/ppermute | solution.py:99
  (213 shorter events, 58.8 us)
Async XLA Ops:
  7.2 13.0 %collective-permute-start.1 = (bf16[24,3200]{1,0:T(8,128)(2,1)S(1)}, bf16[24,3200]{1,0:T(8,128)(2,1)S(1)}, u32[]{:S(2)}, u32[]{:S(2)}) collective-permute-start(bf16[24,3200]{1,0:T(8,128)(2,1)S(1)} %get-tuple-element.135.a0), channel_id=1, source_target_pairs={{0,2},{1,3},{2,0},{3,1},{4,6},{5,7},{6,4},{7,5},{8,10},{9,11},{10,... | collective-permute-start | bytes 460808 | tf_op jit(solution)/shard_map/ppermute | solution.py:99
  7.2 13.0 %collective-permute-start = (bf16[24,3200]{1,0:T(8,128)(2,1)S(1)}, bf16[24,3200]{1,0:T(8,128)(2,1)S(1)}, u32[]{:S(2)}, u32[]{:S(2)}) collective-permute-start(bf16[24,3200]{1,0:T(8,128)(2,1)S(1)} %get-tuple-element.135.a0), channel_id=1, source_target_pairs={{0,1},{1,0},{2,3},{3,2},{4,5},{5,4},{6,7},{7,6},{8,9},{9,8},{10,11... | collective-permute-start | bytes 460808 | tf_op jit(solution)/shard_map/ppermute | solution.py:99
  20.2 15.0 %collective-permute-start.6 = (bf16[96,3200]{1,0:T(8,128)(2,1)S(1)}, bf16[96,3200]{1,0:T(8,128)(2,1)S(1)}, u32[]{:S(2)}, u32[]{:S(2)}) collective-permute-start(bf16[96,3200]{1,0:T(8,128)(2,1)S(1)} %z_join.3.refs_0_.refs_1_), channel_id=1, source_target_pairs={{0,16},{1,17},{2,18},{3,19},{4,20},{5,21},{6,22},{7,23},{8,24},{9,... | collective-permute-start | bytes 1843208 | tf_op jit(solution)/shard_map/ppermute | solution.py:99
  21.8 15.5 %collective-permute-start.4 = (bf16[96,3200]{1,0:T(8,128)(2,1)S(1)}, bf16[96,3200]{1,0:T(8,128)(2,1)S(1)}, u32[]{:S(2)}, u32[]{:S(2)}) collective-permute-start(bf16[96,3200]{1,0:T(8,128)(2,1)S(1)} %z_join.3.refs_0_.refs_1_), channel_id=1, source_target_pairs={{0,8},{1,9},{2,10},{3,11},{4,12},{5,13},{6,14},{7,15},{8,0},{9,1},... | collective-permute-start | bytes 1843208 | tf_op jit(solution)/shard_map/ppermute | solution.py:99
  23.3 13.5 %collective-permute-start.14 = (bf16[24,3072]{1,0:T(8,128)(2,1)S(1)}, bf16[24,3072]{1,0:T(8,128)(2,1)S(1)}, u32[]{:S(2)}, u32[]{:S(2)}) collective-permute-start(bf16[24,3072]{1,0:T(8,128)(2,1)S(1)} %get-tuple-element.141.a0), channel_id=1, source_target_pairs={{0,3},{1,2},{2,1},{3,0},{4,7},{5,6},{6,5},{7,4},{8,11},{9,10},{10,... | collective-permute-start | bytes 442376 | tf_op jit(solution)/shard_map/ppermute | solution.py:99
  25.8 11.2 %collective-permute-start.13 = (bf16[24,3072]{1,0:T(8,128)(2,1)S(1)}, bf16[24,3072]{1,0:T(8,128)(2,1)S(1)}, u32[]{:S(2)}, u32[]{:S(2)}) collective-permute-start(bf16[24,3072]{1,0:T(8,128)(2,1)S(1)} %get-tuple-element.141.a0), channel_id=1, source_target_pairs={{0,2},{1,3},{2,0},{3,1},{4,6},{5,7},{6,4},{7,5},{8,10},{9,11},{10,... | collective-permute-start | bytes 442376 | tf_op jit(solution)/shard_map/ppermute | solution.py:99
  25.8 11.8 %collective-permute-start.12 = (bf16[24,3072]{1,0:T(8,128)(2,1)S(1)}, bf16[24,3072]{1,0:T(8,128)(2,1)S(1)}, u32[]{:S(2)}, u32[]{:S(2)}) collective-permute-start(bf16[24,3072]{1,0:T(8,128)(2,1)S(1)} %get-tuple-element.141.a0), channel_id=1, source_target_pairs={{0,1},{1,0},{2,3},{3,2},{4,5},{5,4},{6,7},{7,6},{8,9},{9,8},{10,11... | collective-permute-start | bytes 442376 | tf_op jit(solution)/shard_map/ppermute | solution.py:99
  36.8 11.2 %collective-permute-start.3 = (bf16[96,3200]{1,0:T(8,128)(2,1)S(1)}, bf16[96,3200]{1,0:T(8,128)(2,1)S(1)}, u32[]{:S(2)}, u32[]{:S(2)}) collective-permute-start(bf16[96,3200]{1,0:T(8,128)(2,1)S(1)} %z_join.3.refs_0_.refs_1_), channel_id=1, source_target_pairs={{0,4},{1,5},{2,6},{3,7},{4,0},{5,1},{6,2},{7,3},{8,12},{9,13},{10,... | collective-permute-start | bytes 1843208 | tf_op jit(solution)/shard_map/ppermute | solution.py:99
  37.0 13.9 %collective-permute-start.7 = (bf16[96,3200]{1,0:T(8,128)(2,1)S(1)}, bf16[96,3200]{1,0:T(8,128)(2,1)S(1)}, u32[]{:S(2)}, u32[]{:S(2)}) collective-permute-start(bf16[96,3200]{1,0:T(8,128)(2,1)S(1)} %collective-permute-done.6.refs_4_.refs_5_), channel_id=1, source_target_pairs={{0,4},{1,5},{2,6},{3,7},{4,0},{5,1},{6,2},{7,3},{8,12},{9,13},{10,... | collective-permute-start | bytes 1843208 | tf_op jit(solution)/shard_map/ppermute | solution.py:99
  37.3 13.6 %collective-permute-start.5 = (bf16[96,3200]{1,0:T(8,128)(2,1)S(1)}, bf16[96,3200]{1,0:T(8,128)(2,1)S(1)}, u32[]{:S(2)}, u32[]{:S(2)}) collective-permute-start(bf16[96,3200]{1,0:T(8,128)(2,1)S(1)} %collective-permute-done.4.refs_2_.refs_3_), channel_id=1, source_target_pairs={{0,4},{1,5},{2,6},{3,7},{4,0},{5,1},{6,2},{7,3},{8,12},{9,13},{10,... | collective-permute-start | bytes 1843208 | tf_op jit(solution)/shard_map/ppermute | solution.py:99
  48.0 23.2 %collective-permute-start.20 = (bf16[4,96,512]{2,1,0:T(8,128)(2,1)S(1)}, bf16[4,96,512]{2,1,0:T(8,128)(2,1)S(1)}, u32[]{:S(2)}, u32[]{:S(2)}) collective-permute-start(bf16[4,96,512]{2,1,0:T(8,128)(2,1)S(1)} %get-tuple-element.145), channel_id=1, source_target_pairs={{0,4},{1,5},{2,6},{3,7},{4,0},{5,1},{6,2},{7,3},{8,12},{9,13},{10,... | collective-permute-start | bytes 1179656 | tf_op jit(solution)/shard_map/ppermute | solution.py:99
  50.9 17.8 %collective-permute-start.18 = (bf16[96,768]{1,0:T(8,128)(2,1)S(1)}, bf16[96,768]{1,0:T(8,128)(2,1)S(1)}, u32[]{:S(2)}, u32[]{:S(2)}) collective-permute-start(bf16[96,768]{1,0:T(8,128)(2,1)S(1)} %get-tuple-element.154.a0), channel_id=1, source_target_pairs={{0,2},{1,3},{2,0},{3,1},{4,6},{5,7},{6,4},{7,5},{8,10},{9,11},{10,... | collective-permute-start | bytes 442376 | tf_op jit(solution)/shard_map/ppermute | solution.py:99
  50.9 17.8 %collective-permute-start.16 = (bf16[96,3072]{1,0:T(8,128)(2,1)S(1)}, bf16[96,3072]{1,0:T(8,128)(2,1)S(1)}, u32[]{:S(2)}, u32[]{:S(2)}) collective-permute-start(bf16[96,3072]{1,0:T(8,128)(2,1)S(1)} %z_join.4.refs_0_), channel_id=1, source_target_pairs={{0,16},{1,17},{2,18},{3,19},{4,20},{5,21},{6,22},{7,23},{8,24},{9,... | collective-permute-start | bytes 1769480 | tf_op jit(solution)/shard_map/ppermute | solution.py:99
  52.5 16.3 %collective-permute-start.15 = (bf16[96,3072]{1,0:T(8,128)(2,1)S(1)}, bf16[96,3072]{1,0:T(8,128)(2,1)S(1)}, u32[]{:S(2)}, u32[]{:S(2)}) collective-permute-start(bf16[96,3072]{1,0:T(8,128)(2,1)S(1)} %z_join.4.refs_0_), channel_id=1, source_target_pairs={{0,8},{1,9},{2,10},{3,11},{4,12},{5,13},{6,14},{7,15},{8,0},{9,1},... | collective-permute-start | bytes 1769480 | tf_op jit(solution)/shard_map/ppermute | solution.py:99
  57.8 11.0 %collective-permute-start.17 = (bf16[96,768]{1,0:T(8,128)(2,1)S(1)}, bf16[96,768]{1,0:T(8,128)(2,1)S(1)}, u32[]{:S(2)}, u32[]{:S(2)}) collective-permute-start(bf16[96,768]{1,0:T(8,128)(2,1)S(1)} %get-tuple-element.154.a0), channel_id=1, source_target_pairs={{0,1},{1,0},{2,3},{3,2},{4,5},{5,4},{6,7},{7,6},{8,9},{9,8},{10,11... | collective-permute-start | bytes 442376 | tf_op jit(solution)/shard_map/ppermute | solution.py:99
  80.0 15.8 %collective-permute-start.29 = (bf16[384,768]{1,0:T(8,128)(2,1)S(1)}, bf16[384,768]{1,0:T(8,128)(2,1)S(1)}, u32[]{:S(2)}, u32[]{:S(2)}) collective-permute-start(bf16[384,768]{1,0:T(8,128)(2,1)S(1)} %z_join.5.refs_0_), channel_id=1, source_target_pairs={{0,16},{1,17},{2,18},{3,19},{4,20},{5,21},{6,22},{7,23},{8,24},{9,... | collective-permute-start | bytes 1769480 | tf_op jit(solution)/shard_map/ppermute | solution.py:99
  80.6 15.5 %collective-permute-start.28 = (bf16[384,768]{1,0:T(8,128)(2,1)S(1)}, bf16[384,768]{1,0:T(8,128)(2,1)S(1)}, u32[]{:S(2)}, u32[]{:S(2)}) collective-permute-start(bf16[384,768]{1,0:T(8,128)(2,1)S(1)} %z_join.5.refs_0_), channel_id=1, source_target_pairs={{0,8},{1,9},{2,10},{3,11},{4,12},{5,13},{6,14},{7,15},{8,0},{9,1},... | collective-permute-start | bytes 1769480 | tf_op jit(solution)/shard_map/ppermute | solution.py:99
  134.7 11.3 %collective-permute-start.44 = (bf16[512,3072]{1,0:T(8,128)(2,1)S(1)}, bf16[512,3072]{1,0:T(8,128)(2,1)S(1)}, u32[]{:S(2)}, u32[]{:S(2)}) collective-permute-start(bf16[512,3072]{1,0:T(8,128)(2,1)S(1)} %get-tuple-element.182.inner_grad.refs_6_), channel_id=1, source_target_pairs={{0,4},{1,5},{2,6},{3,7},{4,0},{5,1},{6,2},{7,3},{8,12},{9,13},{10,... | collective-permute-start | bytes 9437192 | tf_op jit(solution)/shard_map/ppermute | solution.py:99
  135.3 15.7 %collective-permute-start.45 = (bf16[384,768]{1,0:T(8,128)(2,1)S(1)}, bf16[384,768]{1,0:T(8,128)(2,1)S(1)}, u32[]{:S(2)}, u32[]{:S(2)}) collective-permute-start(bf16[384,768]{1,0:T(8,128)(2,1)S(1)} %get-tuple-element.181), channel_id=1, source_target_pairs={{0,8},{1,9},{2,10},{3,11},{4,12},{5,13},{6,14},{7,15},{8,0},{9,1},... | collective-permute-start | bytes 1769480 | tf_op jit(solution)/shard_map/ppermute | solution.py:99
  136.0 15.0 %collective-permute-start.46 = (bf16[384,768]{1,0:T(8,128)(2,1)S(1)}, bf16[384,768]{1,0:T(8,128)(2,1)S(1)}, u32[]{:S(2)}, u32[]{:S(2)}) collective-permute-start(bf16[384,768]{1,0:T(8,128)(2,1)S(1)} %get-tuple-element.196), channel_id=1, source_target_pairs={{0,16},{1,17},{2,18},{3,19},{4,20},{5,21},{6,22},{7,23},{8,24},{9,... | collective-permute-start | bytes 1769480 | tf_op jit(solution)/shard_map/ppermute | solution.py:99
  151.5 14.6 %collective-permute-start.47 = (bf16[192,768]{1,0:T(8,128)(2,1)S(1)}, bf16[192,768]{1,0:T(8,128)(2,1)S(1)}, u32[]{:S(2)}, u32[]{:S(2)}) collective-permute-start(bf16[192,768]{1,0:T(8,128)(2,1)S(1)} %get-tuple-element.203), channel_id=1, source_target_pairs={{0,2},{1,3},{2,0},{3,1},{4,6},{5,7},{6,4},{7,5},{8,10},{9,11},{10,... | collective-permute-start | bytes 884744 | tf_op jit(solution)/shard_map/ppermute | solution.py:99
  152.1 14.0 %collective-permute-start.48 = (bf16[96,1920]{1,0:T(8,128)(2,1)S(1)}, bf16[96,1920]{1,0:T(8,128)(2,1)S(1)}, u32[]{:S(2)}, u32[]{:S(2)}) collective-permute-start(bf16[96,1920]{1,0:T(8,128)(2,1)S(1)} %get-tuple-element.206), channel_id=1, source_target_pairs={{0,16},{1,17},{2,18},{3,19},{4,20},{5,21},{6,22},{7,23},{8,24},{9,... | collective-permute-start | bytes 1105928 | tf_op jit(solution)/shard_map/ppermute | solution.py:99
  153.2 13.0 %collective-permute-start.49 = (bf16[96,1920]{1,0:T(8,128)(2,1)S(1)}, bf16[96,1920]{1,0:T(8,128)(2,1)S(1)}, u32[]{:S(2)}, u32[]{:S(2)}) collective-permute-start(bf16[96,1920]{1,0:T(8,128)(2,1)S(1)} %get-tuple-element.208), channel_id=1, source_target_pairs={{0,8},{1,9},{2,10},{3,11},{4,12},{5,13},{6,14},{7,15},{8,0},{9,1},... | collective-permute-start | bytes 1105928 | tf_op jit(solution)/shard_map/ppermute | solution.py:99
  166.6 19.4 %collective-permute-start.54 = (bf16[96,3840]{1,0:T(8,128)(2,1)S(1)}, bf16[96,3840]{1,0:T(8,128)(2,1)S(1)}, u32[]{:S(2)}, u32[]{:S(2)}) collective-permute-start(bf16[96,3840]{1,0:T(8,128)(2,1)S(1)} %get-tuple-element.223), channel_id=1, source_target_pairs={{0,16},{1,17},{2,18},{3,19},{4,20},{5,21},{6,22},{7,23},{8,24},{9,... | collective-permute-start | bytes 2211848 | tf_op jit(solution)/shard_map/ppermute | solution.py:99
  167.7 19.3 %collective-permute-start.53 = (bf16[96,3840]{1,0:T(8,128)(2,1)S(1)}, bf16[96,3840]{1,0:T(8,128)(2,1)S(1)}, u32[]{:S(2)}, u32[]{:S(2)}) collective-permute-start(bf16[96,3840]{1,0:T(8,128)(2,1)S(1)} %get-tuple-element.209), channel_id=1, source_target_pairs={{0,8},{1,9},{2,10},{3,11},{4,12},{5,13},{6,14},{7,15},{8,0},{9,1},... | collective-permute-start | bytes 2211848 | tf_op jit(solution)/shard_map/ppermute | solution.py:99
  177.4 14.1 %collective-permute-start.57 = (bf16[96,1280]{1,0:T(8,128)(2,1)S(1)}, bf16[96,1280]{1,0:T(8,128)(2,1)S(1)}, u32[]{:S(2)}, u32[]{:S(2)}) collective-permute-start(bf16[96,1280]{1,0:T(8,128)(2,1)S(1)} %get-tuple-element.231), channel_id=1, source_target_pairs={{0,8},{1,9},{2,10},{3,11},{4,12},{5,13},{6,14},{7,15},{8,0},{9,1},... | collective-permute-start | bytes 737288 | tf_op jit(solution)/shard_map/ppermute | solution.py:99
  178.2 12.1 %collective-permute-start.56 = (bf16[96,1152]{1,0:T(8,128)(2,1)S(1)}, bf16[96,1152]{1,0:T(8,128)(2,1)S(1)}, u32[]{:S(2)}, u32[]{:S(2)}) collective-permute-start(bf16[96,1152]{1,0:T(8,128)(2,1)S(1)} %get-tuple-element.219), channel_id=1, source_target_pairs={{0,16},{1,17},{2,18},{3,19},{4,20},{5,21},{6,22},{7,23},{8,24},{9,... | collective-permute-start | bytes 663560 | tf_op jit(solution)/shard_map/ppermute | solution.py:99
  187.6 17.9 %collective-permute-start.55 = (bf16[48,3840]{1,0:T(8,128)(2,1)S(1)}, bf16[48,3840]{1,0:T(8,128)(2,1)S(1)}, u32[]{:S(2)}, u32[]{:S(2)}) collective-permute-start(bf16[48,3840]{1,0:T(8,128)(2,1)S(1)} %get-tuple-element.225), channel_id=1, source_target_pairs={{0,2},{1,3},{2,0},{3,1},{4,6},{5,7},{6,4},{7,5},{8,10},{9,11},{10,... | collective-permute-start | bytes 1105928 | tf_op jit(solution)/shard_map/ppermute | solution.py:99
  191.7 13.9 %collective-permute-start.58 = (bf16[96,2432]{1,0:T(8,128)(2,1)S(1)}, bf16[96,2432]{1,0:T(8,128)(2,1)S(1)}, u32[]{:S(2)}, u32[]{:S(2)}) collective-permute-start(bf16[96,2432]{1,0:T(8,128)(2,1)S(1)} %get-tuple-element.232), channel_id=1, source_target_pairs={{0,8},{1,9},{2,10},{3,11},{4,12},{5,13},{6,14},{7,15},{8,0},{9,1},... | collective-permute-start | bytes 1400840 | tf_op jit(solution)/shard_map/ppermute | solution.py:99
  193.1 12.6 %collective-permute-start.59 = (bf16[96,2432]{1,0:T(8,128)(2,1)S(1)}, bf16[96,2432]{1,0:T(8,128)(2,1)S(1)}, u32[]{:S(2)}, u32[]{:S(2)}) collective-permute-start(bf16[96,2432]{1,0:T(8,128)(2,1)S(1)} %get-tuple-element.233), channel_id=1, source_target_pairs={{0,16},{1,17},{2,18},{3,19},{4,20},{5,21},{6,22},{7,23},{8,24},{9,... | collective-permute-start | bytes 1400840 | tf_op jit(solution)/shard_map/ppermute | solution.py:99
  206.0 12.1 %collective-permute-start.60 = (bf16[48,2432]{1,0:T(8,128)(2,1)S(1)}, bf16[48,2432]{1,0:T(8,128)(2,1)S(1)}, u32[]{:S(2)}, u32[]{:S(2)}) collective-permute-start(bf16[48,2432]{1,0:T(8,128)(2,1)S(1)} %get-tuple-element.235), channel_id=1, source_target_pairs={{0,2},{1,3},{2,0},{3,1},{4,6},{5,7},{6,4},{7,5},{8,10},{9,11},{10,... | collective-permute-start | bytes 700424 | tf_op jit(solution)/shard_map/ppermute | solution.py:99
  206.5 11.7 %collective-permute-start.62 = (bf16[24,3840]{1,0:T(8,128)(2,1)S(1)}, bf16[24,3840]{1,0:T(8,128)(2,1)S(1)}, u32[]{:S(2)}, u32[]{:S(2)}) collective-permute-start(bf16[24,3840]{1,0:T(8,128)(2,1)S(1)} %get-tuple-element.243), channel_id=1, source_target_pairs={{0,1},{1,0},{2,3},{3,2},{4,5},{5,4},{6,7},{7,6},{8,9},{9,8},{10,11... | collective-permute-start | bytes 552968 | tf_op jit(solution)/shard_map/ppermute | solution.py:99
  (72 other events, 570.7 us)
where the time goes:
time: 224 us
  waiting for transfers between devices  85.2 us (38%)
  Pallas kernels  79.2 us (35%)
  starting transfers between devices  52.3 us (23%)
  local copies, waits for them, and re-layouts  5.31 us (2%)
    ppermute x63, waiting for transfers between devices, swap(): return lax.ppermute(value, AXES, [(i, i ^ mask) for i in range(32)])  85.2 us
    pallas_call x30, Pallas kernels, call(): pl.pallas_call(kernel, out_shape=out_shape, name=name, input_output_alias...  79.2 us
    ppermute x63, starting transfers between devices, swap(): return lax.ppermute(value, AXES, [(i, i ^ mask) for i in range(32)])  52.3 us
    unnamed x82, local copies, waits for them, and re-layouts  5.16 us
  transfers between devices with their start and end apart: 63, of which 29 were waited for; matrix products, arithmetic and copies ran while one was open for 0% of the time, Pallas kernels for 29%

commit v1 on v0

--- a/solution.py
+++ b/solution.py
@@ -24,22 +24,22 @@
     "pack": 1.3,
     "z_join": 0.3,
     "turn_tokens": 1.0,
-    "project": 4.0,
-    "attend": 8.4,
+    "project": 1.5,
+    "attend": 2.0,
     "mix": 3.0,
     "inner": 11.0,
-    "outer": 8.0,
-    "slope": 6.0,
+    "outer": 6.0,
+    "slope": 3.7,
     "grad_outer": 2.6,
-    "normed_back": 50.0,
+    "normed_back": 5.0,
     "add_halves": 0.5,
     "grad_inner": 3.2,
     "attend_back": 11.4,
     "plane_sum": 0.6,
     "pair_sum": 4.0,
     "stack_small": 0.1,
-    "grad_first": 0.3,
-    "tokens_back": 0.3,
+    "grad_first": 2.0,
+    "tokens_back": 5.6,
     "finish": 0.8,
 }
 
@@ -170,6 +170,31 @@
     return call(z_join_kernel, "z_join", [at] + pieces, [smem()] + [vmem()] * 4, sds((4 * rows, cols)), limit=8)
 
 
+def pair_join_kernel(a0, a1, out):
+    rows = a0.shape[0]
+    out[:rows] = a0[...]
+    out[rows:] = a1[...]
+
+
+def pair_join(own, came):
+    rows, cols = own.shape
+    return call(pair_join_kernel, "z_join", [own, came], [vmem()] * 2, sds((2 * rows, cols)), limit=4)
+
+
+def z_join_pairs_kernel(at_ref, a, b, out):
+    rows = a.shape[0] // 2
+    z = lax.rem(at_ref[0], 4)
+    for m in range(4):
+        piece = (a, b)[m % 2]
+        start = pl.multiple_of((z ^ m) * rows, 8)
+        out[pl.ds(start, rows), :] = piece[m // 2 * rows : (m // 2 + 1) * rows]
+
+
+def z_join_pairs(at, pair, came):
+    rows, cols = pair.shape
+    return call(z_join_pairs_kernel, "z_join", [at, pair, came], [smem()] + [vmem()] * 2, sds((2 * rows, cols)), limit=8)
+
+
 def forward_halves(x, y):
     half = x.shape[1] // 256 * 128
     return [swap(x[:, :half], 16), swap(y[:, half:], 8)]
@@ -187,6 +212,10 @@
 
 
 PIECES = 10
+
+
+def grouped(refs):
+    return [[r] for r in refs[:6]] + [list(refs[6:8]), list(refs[8:10])]
 
 
 def block_copies(at_ref, refs, scr, sems):
@@ -273,7 +302,7 @@
         [smem(), vmem()] + [hbm()] * PIECES,
         (sds((size, width)),) * 3 + (sds((16, width), F32), sds((1, 4 * width), F32), sds((width, width))),
         scratch=[pltpu.VMEM((width, cols), BF16), pltpu.SemaphoreType.DMA((PIECES,))],
-        limit=20,
+        limit=14,
     )
 
 
@@ -320,7 +349,7 @@
         ),
         grid=(pairs,),
         prefetch=1,
-        limit=16,
+        limit=12,
     )
 
 
@@ -364,19 +393,17 @@
         [at, tokens, mixed, mixed_t, lines, w_out],
         [smem()] + [vmem()] * 5,
         (sds((size, width), F32), sds((size, 128), F32), sds((size, width)), half, half),
-        limit=16,
+        limit=10,
     )
 
 
 def inner_kernel(at_ref, values, bias, *refs):
     pieces = refs[:PIECES]
-    (activ, slope, weights, keep, send, scr, sems, out_sem) = refs[PIECES:]
+    (activ, slope, scr, keep, send, sems) = refs[PIECES:]
     part = activ.shape[1] // 8
     group = at_ref[0] // 4
     core = lax.rem(group, 2)
     fetch_all(at_ref, pieces, scr, sems)
-    copy = pltpu.make_async_copy(scr, weights, out_sem)
-    copy.start()
 
     def step(b, carry):
         at = pl.multiple_of(b * part, 128)
@@ -399,7 +426,6 @@
         return carry
 
     lax.fori_loop(0, 8, step, 0)
-    copy.wait()
 
 
 def inner_stage(at, values, bias, blocks):
@@ -413,31 +439,21 @@
         args,
         [smem()] + [vmem()] * 2 + [hbm()] * PIECES,
         (sds((size, hidden)), sds((size, hidden)), sds((width, hidden)), half, half),
-        out_specs=(vmem(),) * 2 + (hbm(),) + (vmem(),) * 2,
-        scratch=[
-            pltpu.VMEM((width, hidden), BF16),
-            pltpu.SemaphoreType.DMA((PIECES,)),
-            pltpu.SemaphoreType.DMA,
-        ],
-        limit=32,
+        scratch=[pltpu.SemaphoreType.DMA((PIECES,))],
+        limit=14,
     )
 
 
 def outer_kernel(at_ref, len_ref, activ, values, lines, cot, *refs):
-    pieces, (output, resid_grad, outer_grad, sums, scr, acc, sems) = refs[:PIECES], refs[PIECES:]
+    pieces, (output, resid_grad, outer_grad, sums, acc) = refs[:PIECES], refs[PIECES:]
     size = values.shape[0]
     part = activ.shape[1] // 8
     group = at_ref[0] // 4
-    lists = block_copies(at_ref, pieces, scr, sems)
-    for mine in lists:
-        for copy in mine:
-            copy.start()
     resid = values[...].astype(F32) + lines[5:6]
-    for m, mine in enumerate(lists):
-        for copy in mine:
-            copy.wait()
-        at = pl.multiple_of((group ^ m) * part, 128)
-        resid += dot(activ[:, pl.ds(at, part)], scr[pl.ds(at, part), :])
+    for m, mine in enumerate(grouped(pieces)):
+        given = activ[:, pl.ds(pl.multiple_of((group ^ m) * part, 128), part)]
+        products = [dot(given, piece[...]) for piece in mine]
+        resid += products[0] if len(products) == 1 else jnp.concatenate(products, axis=1)
     acc[...] = resid
     gain, shift = lines[6:7], lines[7:8]
     sums[...] = jnp.zeros_like(sums)
@@ -469,32 +485,26 @@
         outer_kernel,
         "outer",
         args,
-        [smem(), smem()] + [vmem()] * 4 + [hbm()] * PIECES,
+        [smem(), smem()] + [vmem()] * (4 + PIECES),
         (sds((size, width)), sds((size, width), F32), sds((size, width)), sds((8, width), F32)),
-        scratch=[
-            pltpu.VMEM((hidden, width), BF16),
-            pltpu.VMEM((size, width), F32),
-            pltpu.SemaphoreType.DMA((PIECES,)),
-        ],
-        limit=32,
+        scratch=[pltpu.VMEM((size, width), F32)],
+        limit=10,
     )
 
 
 def slope_kernel(at_ref, outer_grad, slope, *refs):
-    pieces, (inner_grad, sums, scr, sems) = refs[:PIECES], refs[PIECES:]
+    pieces, (inner_grad, sums) = refs[:PIECES], refs[PIECES:]
     part = slope.shape[1] // 8
     group = at_ref[0] // 4
-    lists = block_copies(at_ref, pieces, scr, sems)
-    for mine in lists:
-        for copy in mine:
-            copy.start()
     grad = outer_grad[...]
-    for m, mine in enumerate(lists):
-        for copy in mine:
-            copy.wait()
+    for m, mine in enumerate(grouped(pieces)):
         at = pl.multiple_of((group ^ m) * part, 128)
-        back = dot(grad, scr[pl.ds(at, part), :], NT) * slope[:, pl.ds(at, part)].astype(F32)
-        rounded = back.astype(BF16)
+        back, col = 0.0, 0
+        for piece in mine:
+            cols = piece.shape[1]
+            back += dot(grad[:, col : col + cols], piece[...], NT)
+            col += cols
+        rounded = (back * slope[:, pl.ds(at, part)].astype(F32)).astype(BF16)
         inner_grad[:, pl.ds(at, part)] = rounded
         sums[:, pl.ds(at, part)] = jnp.sum(rounded.astype(F32), axis=0, keepdims=True)
 
@@ -507,10 +517,9 @@
         slope_kernel,
         "slope",
         args,
-        [smem()] + [vmem()] * 2 + [hbm()] * PIECES,
+        [smem()] + [vmem()] * (2 + PIECES),
         (sds((size, hidden)), sds((1, hidden), F32)),
-        scratch=[pltpu.VMEM((hidden, width), BF16), pltpu.SemaphoreType.DMA((PIECES,))],
-        limit=32,
+        limit=10,
     )
 
 
@@ -556,7 +565,7 @@
         (sds((size, width), F32),)
         + (sds((size, width // 2)),) * 2
         + (sds((size, width)), sds((8, width), F32)),
-        limit=32,
+        limit=12,
     )
 
 
@@ -609,7 +618,7 @@
         out_specs=(out,) + (line,) * 2,
         grid=(pairs,),
         prefetch=1,
-        limit=16,
+        limit=12,
     )
 
 
@@ -634,7 +643,7 @@
         [smem()] + [vmem()] * 2 + [hbm()] * PIECES,
         sds((size, width)),
         scratch=[pltpu.VMEM((width, cols), BF16), pltpu.SemaphoreType.DMA((PIECES,))],
-        limit=24,
+        limit=14,
     )
 
 
@@ -721,7 +730,7 @@
         specs,
         slot_shapes(part, cols),
         scratch=scratch,
-        limit=32,
+        limit=14,
     )
 
 
@@ -789,7 +798,7 @@
         [smem()] + [vmem()] * 3,
         (sds((part // 2, cols)),) * 2,
         scratch=[pltpu.VMEM((part, cols), F32)],
-        limit=16,
+        limit=6,
     )
 
 
@@ -839,7 +848,7 @@
         pieces,
         [vmem()] * 2,
         tuple(shapes),
-        limit=16,
+        limit=6,
     )
     return [o.reshape(-1) for o in outs]
 
@@ -892,22 +901,28 @@
     )
     z_first = z_join(at, z_swaps(first))
     x_first, y_first = swap(z_first, 8), swap(z_first, 16)
-    second_swaps = z_swaps(after(second, z_first))
+    second = after(second, z_first)
+    second = pair_join(second, swap(second, 2))
+    x_first, second = lax.optimization_barrier((x_first, second))
     f_first = forward_halves(x_first, y_first)
     first_blocks = row_blocks(z_first, x_first, y_first, f_first)
-    z_second = z_join(at, second_swaps)
+    z_second = z_join_pairs(at, second, swap(second, 1))
     x_second, y_second = swap(z_second, 8), swap(z_second, 16)
-    third_swaps = z_swaps(after(third, z_second))
+    third = after(third, z_second)
+    third_came = swap(third, 2)
+
     tok_keep, tok_send = turn_tokens(at, tokens)
     tok_came = swap(tok_send, 4)
     queries, key_rows, value_rows, lines, bias, w_out = project(at, tokens, first_blocks)
+    third = pair_join(third, after(third_came, queries))
+    queries = after(queries, third)
     mixed, mixed_t, lse = attend(lengths, queries, key_rows, value_rows)
-    mixed, x_second, y_second, *third_swaps = lax.optimization_barrier((mixed, x_second, y_second, *third_swaps))
+    mixed, x_second, y_second = lax.optimization_barrier((mixed, x_second, y_second))
     f_second = forward_halves(x_second, y_second)
     unit, scale, values, b_keep, b_send = mix_stage(at, tokens, after(mixed, tok_came), mixed_t, lines, w_out)
     b_came = swap(b_send, 4)
     second_blocks = row_blocks(z_second, x_second, y_second, [after(f, values) for f in f_second])
-    z_third = z_join(at, [after(third_swaps[0], *f_second)] + third_swaps[1:])
+    z_third = z_join_pairs(at, third, after(swap(third, 1), *f_second))
     x_third, y_third = swap(z_third, 8), swap(z_third, 16)
     activ, slope, w_inner, a_keep, a_send = inner_stage(at, after(values, z_third), bias, second_blocks)
     activ, x_third, y_third = lax.optimization_barrier((activ, x_third, y_third))
@@ -918,20 +933,20 @@
     output, resid_two_grad, outer_grad, sums_two = outer_stage(at, lengths, activ, values, lines, cotangent, third_blocks)
 
     outer_came = swap(outer_grad, 4)
+    inner_grad, bias_grad = slope_stage(at, outer_grad, slope, third_blocks)
+    inner_came = swap(after(inner_grad, outer_came), 4)
     slots_a = weight_grad(
         "grad_outer",
-        [a_keep, a_came, outer_grad, outer_came],
+        [a_keep, a_came, outer_grad, after(outer_came, inner_grad)],
         [(0, None, 2, 3, ())],
         hidden // 8,
         width,
     )
-    inner_grad, bias_grad = slope_stage(at, after(outer_grad, slots_a[0]), slope, third_blocks)
-    plane_a = scatter_plane(slots_a, inner_grad)
-    inner_came = swap(after(inner_grad, plane_a[3]), 4)
     resid_one_grad, attn_low, attn_high, mixed_grad, sums_one = normed_back(
-        after(inner_grad, plane_a[3]), resid_two_grad, unit, scale, lines, w_out, w_inner
-    )
-    low_came, high_came = swap(attn_low, 4), swap(attn_high, 4)
+        after(inner_grad, slots_a[0]), resid_two_grad, unit, scale, lines, w_out, w_inner
+    )
+    plane_a = scatter_plane(slots_a, attn_low)
+    low_came, high_came = (swap(after(g, plane_a[3]), 4) for g in (attn_low, attn_high))
     slots_b = weight_grad(
         "grad_inner",
         [b_keep, b_came, attn_low, low_came, attn_high, high_came, inner_grad, inner_came],
@@ -939,14 +954,12 @@
         width // 8,
         width + hidden,
     )
-    sums_a = plane_sum(at, [after(plane_a[0], slots_b[0])] + plane_a[1:3])
     grads, q_sum, v_sum = attend_back(
-        lengths, queries, key_rows, value_rows, mixed_t, after(mixed_grad, sums_a[0]), lse
-    )
-    own_a, last_a = first_z(sums_a, grads)
-    plane_b = scatter_plane(slots_b, own_a)
-    grads_came = swap(after(grads, plane_b[3]), 4)
-    (own_u,) = finish([own_a, swap(last_a, 1)], [width])
+        lengths, queries, key_rows, value_rows, mixed_t, after(mixed_grad, slots_b[0]), lse
+    )
+    plane_b = scatter_plane(slots_b, grads)
+    sums_a = plane_sum(at, [after(plane_a[0], plane_b[3])] + plane_a[1:3])
+    grads_came = swap(after(grads, sums_a[0]), 4)
     small = stack_small(sums_one, sums_two, q_sum, v_sum, bias_grad)
     small_came = swap(small, 4)
     args = [tok_keep, tok_came, grads, grads_came]
@@ -959,11 +972,13 @@
         3 * width + SMALL,
         small=len(args),
     )
+    tokens_grad = tokens_back(at, after(resid_one_grad, slots_c[0]), grads, first_blocks)
+    own_a, last_a = first_z(sums_a, tokens_grad)
     slots_c = list(slots_c)
-    slots_c[3], slots_c[4], _ = lax.optimization_barrier((slots_c[3], slots_c[4], own_u))
-    tokens_grad = tokens_back(at, after(resid_one_grad, slots_c[3]), grads, first_blocks)
-    sums_b = plane_sum(at, [after(plane_b[0], tokens_grad)] + plane_b[1:3])
+    slots_c[3], slots_c[4], _ = lax.optimization_barrier((slots_c[3], slots_c[4], own_a))
+    sums_b = plane_sum(at, [after(plane_b[0], own_a)] + plane_b[1:3])
     plane_c = scatter_plane(slots_c, sums_b[0])
+    (own_u,) = finish([own_a, swap(after(last_a, sums_b[0]), 1)], [width])
     own_b, last_b = first_z(sums_b)
     sums_c = plane_sum(at, [after(plane_c[0], own_b)] + plane_c[1:3])
     own_o, own_i = finish([own_b, swap(last_b, 1)], [width, hidden])

time: 224 us -> 214 us (0.955)
  starting transfers between devices: 52.3 us -> 41.4 us
  waiting for transfers between devices: 85.2 us -> 93.4 us
  Pallas kernels: 79.2 us -> 74.1 us
  local copies, waits for them, and re-layouts: 5.31 us -> 2.59 us
    ppermute x63 -> x61, starting transfers between devices: 52.3 us -> 41.4 us  [swap(): return lax.ppermute(value, AXES, [(i, i ^ mask) for i in range(32)])]
    ppermute x63 -> x61, waiting for transfers between devices: 85.2 us -> 93.4 us  [swap(): return lax.ppermute(value, AXES, [(i, i ^ mask) for i in range(32)])]
    pallas_call x30 -> x32, Pallas kernels: 79.2 us -> 74.1 us  [call(): pl.pallas_call(kernel, out_shape=out_shape, name=name, input_output_alias...]
    unnamed x82 -> x44, local copies, waits for them, and re-layouts: 5.16 us -> 2.44 us
  transfers between devices with their start and end apart: 63 -> 61, of which waited for: 29 -> 27; matrix products, arithmetic and copies ran while one was open for 0% -> 0% of each run, Pallas kernels for 29% -> 30%
where the time goes in v1:
time: 214 us
  waiting for transfers between devices  93.4 us (44%)
  Pallas kernels  74.1 us (35%)
  starting transfers between devices  41.4 us (19%)
  local copies, waits for them, and re-layouts  2.59 us (1%)
    ppermute x61, waiting for transfers between devices, swap(): return lax.ppermute(value, AXES, [(i, i ^ mask) for i in range(32)])  93.4 us
    pallas_call x32, Pallas kernels, call(): pl.pallas_call(kernel, out_shape=out_shape, name=name, input_output_alias...  74.1 us
    ppermute x61, starting transfers between devices, swap(): return lax.ppermute(value, AXES, [(i, i ^ mask) for i in range(32)])  41.4 us
  transfers between devices with their start and end apart: 61, of which 27 were waited for; matrix products, arithmetic and copies ran while one was open for 0% of the time, Pallas kernels for 30%

profile of v1, /device:TPU:0, one launch (start us, length us, event | category | flops | bytes accessed | tf_op | source)
XLA Modules:
  0.0 213.6 jit_solution(18156870578050798412)
XLA Ops:
  2.0 5.1 %collective-permute-start.2 = (bf16[24,3200]{1,0:T(8,128)(2,1)S(1)}, bf16[24,3200]{1,0:T(8,128)(2,1)S(1)}, u32[]{:S(2)}, u32[]{:S(2)}) collective-permute-start(bf16[24,3200]{1,0:T(8,128)(2,1)S(1)} %get-tuple-element.139.a0), channel_id=1, source_target_pairs={{0,3},{1,2},{2,1},{3,0},{4,7},{5,6},{6,5},{7,4},{8,11},{9,10},{10,... | collective-permute-start | bytes 460808 | tf_op jit(solution)/shard_map/ppermute | solution.py:99
  7.7 4.3 %collective-permute-done.2.a3 = bf16[24,3200]{1,0:T(8,128)(2,1)S(1)} collective-permute-done((bf16[24,3200]{1,0:T(8,128)(2,1)S(1)}, bf16[24,3200]{1,0:T(8,128)(2,1)S(1)}, u32[]{:S(2)}, u32[]{:S(2)}) %collective-permute-start.2) | collective-permute-done | bytes 153632 | tf_op jit(solution)/shard_map/ppermute | solution.py:99
  12.0 8.1 %collective-permute-done.1.a2 = bf16[24,3200]{1,0:T(8,128)(2,1)S(1)} collective-permute-done((bf16[24,3200]{1,0:T(8,128)(2,1)S(1)}, bf16[24,3200]{1,0:T(8,128)(2,1)S(1)}, u32[]{:S(2)}, u32[]{:S(2)}) %collective-permute-start.1) | collective-permute-done | bytes 153632 | tf_op jit(solution)/shard_map/ppermute | solution.py:99
  20.2 1.6 collective-permute-start.4
  23.3 8.0 %collective-permute-done.5.a1 = bf16[24,3072]{1,0:T(8,128)(2,1)S(1)} collective-permute-done((bf16[24,3072]{1,0:T(8,128)(2,1)S(1)}, bf16[24,3072]{1,0:T(8,128)(2,1)S(1)}, u32[]{:S(2)}, u32[]{:S(2)}) %collective-permute-start.5) | collective-permute-done | bytes 147488 | tf_op jit(solution)/shard_map/ppermute | solution.py:99
  31.3 3.8 %collective-permute-done.4.refs_2_.refs_3_ = bf16[96,3200]{1,0:T(8,128)(2,1)S(1)} collective-permute-done((bf16[96,3200]{1,0:T(8,128)(2,1)S(1)}, bf16[96,3200]{1,0:T(8,128)(2,1)S(1)}, u32[]{:S(2)}, u32[]{:S(2)}) %collective-permute-start.4) | collective-permute-done | bytes 614432 | tf_op jit(solution)/shard_map/ppermute | solution.py:99
  35.2 1.6 collective-permute-start.9
  36.8 1.6 collective-permute-start.10
  38.4 4.3 %collective-permute-done.9.refs_6_.refs_7_ = bf16[96,1536]{1,0:T(8,128)(2,1)S(1)} collective-permute-done((bf16[96,1536]{1,0:T(8,128)(2,1)S(1)}, bf16[96,1536]{1,0:T(8,128)(2,1)S(1)}, u32[]{:S(2)}, u32[]{:S(2)}) %collective-permute-start.9) | collective-permute-done | bytes 294944 | tf_op jit(solution)/shard_map/ppermute | solution.py:99
  46.1 2.2 %collective-permute-start.14 = (bf16[96,768]{1,0:T(8,128)(2,1)S(1)}, bf16[96,768]{1,0:T(8,128)(2,1)S(1)}, u32[]{:S(2)}, u32[]{:S(2)}) collective-permute-start(bf16[96,768]{1,0:T(8,128)(2,1)S(1)} %get-tuple-element.146.a0), channel_id=1, source_target_pairs={{0,2},{1,3},{2,0},{3,1},{4,6},{5,7},{6,4},{7,5},{8,10},{9,11},{10,... | collective-permute-start | bytes 442376 | tf_op jit(solution)/shard_map/ppermute | solution.py:99
  51.0 4.5 %project.1 = (bf16[512,768]{1,0:T(8,128)(2,1)S(1)}, bf16[512,768]{1,0:T(8,128)(2,1)S(1)}, bf16[512,768]{1,0:T(8,128)(2,1)S(1)}, f32[16,768]{1,0:T(8,128)S(1)}, f...) custom-call(s32[1]{0:T(128)} %bitcast.at_ref.refs_4_, bf16[512,768]{1,0:T(8,128)(2,1)S(1)} %copy-done.1, ...), custom_call_target="tpu_custom_call" | custom-call | flops 825000000 | tf_op jit(solution)/shard_map/project/pallas_call | solution.py:87
  56.4 8.4 %attend.1 = (bf16[512,768]{1,0:T(8,128)(2,1)S(1)}, bf16[768,512]{1,0:T(8,128)(2,1)S(1)}, f32[6,2,512]{2,1,0:T(2,128)S(1)}) custom-call(s32[1]{0:T(128)S(6)} %copy.43.len_ref, bf16[512,768]{1,0:T(8,128)(2,1)S(1)} %get-tuple-element.148.q_ref, bf16[512,768]{1,0:T(8,128)(2,1)S(1)} %get-tuple-element.149.k_ref, bf16[512,768]{1,0:T(8,128)(2,1)S(1)} %get-tuple-element.150.v_ref), custom_call_target="tpu_custom_call" | custom-call | flops 1100000000 | tf_op jit(solution)/shard_map/attend/pallas_call | solution.py:87
  67.1 6.5 %collective-permute-done.19.refs_6_ = bf16[96,1536]{1,0:T(8,128)(2,1)S(1)} collective-permute-done((bf16[96,1536]{1,0:T(8,128)(2,1)S(1)}, bf16[96,1536]{1,0:T(8,128)(2,1)S(1)}, u32[]{:S(2)}, u32[]{:S(2)}) %collective-permute-start.19) | collective-permute-done | bytes 294944 | tf_op jit(solution)/shard_map/ppermute | solution.py:99
  73.5 3.0 %mix.1 = (f32[512,768]{1,0:T(8,128)S(1)}, f32[512,128]{1,0:T(8,128)S(1)}, bf16[512,768]{1,0:T(8,128)(2,1)S(1)}, bf16[2,4,96,512]{3,2,1,0:T(8,128)(2,1)S(1)}, bf16[2,4,96,512]{3,2,1,0:T(8,128)(2,1)S(1)}) custom-call(s32[1]{0:T(128)} %bitcast.at_ref.refs_4_, bf16[512,768]{1,0:T(8,128)(2,1)S(1)} %copy-done.1, bf16[512,768]{1,0:T(8,128)(2,1)S(1)} %get-tuple-element.154.mixed, ...), custom_call_target="tpu_custom_call" | custom-call | flops 1650000000 | tf_op jit(solution)/shard_map/mix/pallas_call | solution.py:87
  80.5 10.2 %inner.1 = (bf16[512,3072]{1,0:T(8,128)(2,1)S(1)}, bf16[512,3072]{1,0:T(8,128)(2,1)S(1)}, bf16[768,3072]{1,0:T(8,128)(2,1)S(1)}, bf16[4,384,512]{2,1,0:T(8,128)(2,1)S(1)}, bf16[4,384,512]{2,1,0:T(8,128)(2,1)S(1)}) custom-call(s32[1]{0:T(128)} %bitcast.at_ref.refs_4_, bf16[512,768]{1,0:T(8,128)(2,1)S(1)} %get-tuple-element.162.values, ...), custom_call_target="tpu_custom_call" | custom-call | flops 6049999872 | tf_op jit(solution)/shard_map/inner/pallas_call | solution.py:87
  90.7 2.3 %collective-permute-done.27.refs_4_ = bf16[384,768]{1,0:T(8,128)(2,1)S(1)} collective-permute-done((bf16[384,768]{1,0:T(8,128)(2,1)S(1)}, bf16[384,768]{1,0:T(8,128)(2,1)S(1)}, u32[]{:S(2)}, u32[]{:S(2)}) %collective-permute-start.27) | collective-permute-done | bytes 589856 | tf_op jit(solution)/shard_map/ppermute | solution.py:99
  96.7 7.1 %collective-permute-done.32.refs_6_ = bf16[384,384]{1,0:T(8,128)(2,1)S(1)} collective-permute-done((bf16[384,384]{1,0:T(8,128)(2,1)S(1)}, bf16[384,384]{1,0:T(8,128)(2,1)S(1)}, u32[]{:S(2)}, u32[]{:S(2)}) %collective-permute-start.32) | collective-permute-done | bytes 294944 | tf_op jit(solution)/shard_map/ppermute | solution.py:99
  106.8 6.2 %outer.1 = (bf16[512,768]{1,0:T(8,128)(2,1)}, f32[512,768]{1,0:T(8,128)S(1)}, bf16[512,768]{1,0:T(8,128)(2,1)S(1)}, f32[8,768]{1,0:T(8,128)S(1)}) custom-call(s32[1]{0:T(128)} %bitcast.at_ref.refs_4_, s32[1]{0:T(128)S(6)} %copy.43.len_ref, bf16[512,3072]{1,0:T(8,128)(2,1)S(1)} %get-tuple-element.171.activ, bf16[512,768]{1,0:T(8,128)(2,1)S(1)} %get-tuple-element.162.values, ...), custom_call_target="tpu_custom_call" | custom-call | flops 3300000000 | tf_op jit(solution)/shard_map/outer/pallas_call | solution.py:87
  113.1 3.7 %slope.1 = (bf16[512,3072]{1,0:T(8,128)(2,1)S(1)}, f32[1,3072]{1,0:T(1,128)S(1)}) custom-call(s32[1]{0:T(128)} %bitcast.at_ref.refs_4_, bf16[512,768]{1,0:T(8,128)(2,1)S(1)} %get-tuple-element.174.outer_grad.refs_2_, bf16[512,3072]{1,0:T(8,128)(2,1)S(1)} %get-tuple-element.175.slope, bf16[384,768]{1,0:T(8,128)(2,1)S(1)} %z_join.9.refs_0_, ...), custom_call_target="tpu_custom_call" | custom-call | flops 2035000064 | tf_op jit(solution)/shard_map/slope/pallas_call | solution.py:87
  117.3 2.6 %grad_outer.1 = (bf16[384,768]{1,0:T(8,128)(2,1)S(1)}, bf16[384,768]{1,0:T(8,128)(2,1)S(1)}, bf16[384,768]{1,0:T(8,128)(2,1)S(1)}, bf16[384,384]{1,0:T(8,128)(2,1)S(1)}, bf16[384,384]{1,0:T(8,128)(2,1)S(1)}) custom-call(bf16[4,384,512]{2,1,0:T(8,128)(2,1)S(1)} %get-tuple-element.177.refs_0_, bf16[4,384,512]{2,1,0:T(8,128)(2,1)S(1)} %collective-permute-done.28.refs_1_, ...), custom_call_target="tpu_custom_call" | custom-call | flops 1430000000 | tf_op jit(solution)/shard_map/grad_outer/pallas_call | solution.py:87
  121.6 6.7 %normed_back.1 = (f32[512,768]{1,0:T(8,128)S(1)}, bf16[512,384]{1,0:T(8,128)(2,1)S(1)}, bf16[512,384]{1,0:T(8,128)(2,1)S(1)}, bf16[512,768]{1,0:T(8,128)(2,1)S(1)}, f32[8,768]{1,0:T(8,128)S(1)}) custom-call(bf16[512,3072]{1,0:T(8,128)(2,1)S(1)} %get-tuple-element.200.inner_grad.refs_6_, f32[512,768]{1,0:T(8,128)S(1)} %get-tuple-element.181.resid_two, ...), custom_call_target="tpu_custom_call" | custom-call | flops 2750000128 | tf_op jit(solution)/shard_map/normed_back/pallas_call | solution.py:87
  132.7 3.4 %grad_inner.1 = (bf16[96,3840]{1,0:T(8,128)(2,1)S(1)}, bf16[96,3840]{1,0:T(8,128)(2,1)S(1)}, bf16[96,3840]{1,0:T(8,128)(2,1)S(1)}, bf16[96,1920]{1,0:T(8,128)(2,1)S(1)}, bf16[96,1920]{1,0:T(8,128)(2,1)S(1)}) custom-call(bf16[2,4,96,512]{3,2,1,0:T(8,128)(2,1)S(1)} %get-tuple-element.188.refs_0_, bf16[2,4,96,512]{3,2,1,0:T(8,128)(2,1)S(1)} %collective-permute-done.37.refs_1_, ...), custom_call_target="tpu_custom_call" | custom-call | flops 1760000000 | tf_op jit(solution)/shard_map/grad_inner/pallas_call | solution.py:87
  138.5 11.5 %attend_back.1 = (bf16[3,512,768]{2,1,0:T(8,128)(2,1)S(1)}, f32[1,768]{1,0:T(1,128)S(1)}, f32[1,768]{1,0:T(1,128)S(1)}) custom-call(s32[1]{0:T(128)S(6)} %copy.43.len_ref, bf16[512,768]{1,0:T(8,128)(2,1)S(1)} %get-tuple-element.148.q_ref, bf16[512,768]{1,0:T(8,128)(2,1)S(1)} %get-tuple-element.149.k_ref, bf16[512,768]{1,0:T(8,128)(2,1)S(1)} %get-tuple-element.150.v_ref, ...), custom_call_target="tpu_custom_call" | custom-call | flops 6270000128 | tf_op jit(solution)/shard_map/attend_back/pallas_call | solution.py:87
  150.0 4.4 %collective-permute-done.43.p_ref = bf16[96,1920]{1,0:T(8,128)(2,1)S(1)} collective-permute-done((bf16[96,1920]{1,0:T(8,128)(2,1)S(1)}, bf16[96,1920]{1,0:T(8,128)(2,1)S(1)}, u32[]{:S(2)}, u32[]{:S(2)}) %collective-permute-start.43) | collective-permute-done | bytes 368672 | tf_op jit(solution)/shard_map/ppermute | solution.py:99
  160.0 2.0 grad_first.1
  162.0 5.4 %tokens_back.1 = bf16[512,768]{1,0:T(8,128)(2,1)} custom-call(s32[1]{0:T(128)} %bitcast.at_ref.refs_4_, f32[512,768]{1,0:T(8,128)S(1)} %get-tuple-element.221.resid_grad, bf16[3,512,768]{2,1,0:T(8,128)(2,1)S(1)} %get-tuple-element.214.refs_2_.refs_0_, bf16[96,3200]{1,0:T(8,128)(2,1)} %copy-done, bf16[96,3200]{1,0:T(8,128)(2,1)} %copy-done.6, ...), custom_call_target="tpu_custom_call" | custom-call | flops 3080000000 | tf_op jit(solution)/shard_map/tokens_back/pallas_call | solution.py:87
  167.4 6.2 %collective-permute-done.49.came = bf16[192,768]{1,0:T(8,128)(2,1)S(1)} collective-permute-done((bf16[192,768]{1,0:T(8,128)(2,1)S(1)}, bf16[192,768]{1,0:T(8,128)(2,1)S(1)}, u32[]{:S(2)}, u32[]{:S(2)}) %collective-permute-start.49) | collective-permute-done | bytes 294944 | tf_op jit(solution)/shard_map/ppermute | solution.py:99
  176.1 5.4 %collective-permute-done.53.p_ref = bf16[96,1152]{1,0:T(8,128)(2,1)S(1)} collective-permute-done((bf16[96,1152]{1,0:T(8,128)(2,1)S(1)}, bf16[96,1152]{1,0:T(8,128)(2,1)S(1)}, u32[]{:S(2)}, u32[]{:S(2)}) %collective-permute-start.53) | collective-permute-done | bytes 221216 | tf_op jit(solution)/shard_map/ppermute | solution.py:99
  184.1 9.6 %collective-permute-done.52.came = bf16[48,3840]{1,0:T(8,128)(2,1)S(1)} collective-permute-done((bf16[48,3840]{1,0:T(8,128)(2,1)S(1)}, bf16[48,3840]{1,0:T(8,128)(2,1)S(1)}, u32[]{:S(2)}, u32[]{:S(2)}) %collective-permute-start.52) | collective-permute-done | bytes 368672 | tf_op jit(solution)/shard_map/ppermute | solution.py:99
  194.6 2.4 %collective-permute-start.60 = (bf16[96,768]{1,0:T(8,128)(2,1)S(1)}, bf16[96,768]{1,0:T(8,128)(2,1)S(1)}, u32[]{:S(2)}, u32[]{:S(2)}) collective-permute-start(bf16[96,768]{1,0:T(8,128)(2,1)S(1)} %get-tuple-element.257), channel_id=1, source_target_pairs={{0,1},{1,0},{2,3},{3,2},{4,5},{5,4},{6,7},{7,6},{8,9},{9,8},{10,11... | collective-permute-start | bytes 442376 | tf_op jit(solution)/shard_map/ppermute | solution.py:99
  197.1 10.4 %collective-permute-done.57.came = bf16[48,2432]{1,0:T(8,128)(2,1)S(1)} collective-permute-done((bf16[48,2432]{1,0:T(8,128)(2,1)S(1)}, bf16[48,2432]{1,0:T(8,128)(2,1)S(1)}, u32[]{:S(2)}, u32[]{:S(2)}) %collective-permute-start.57) | collective-permute-done | bytes 233504 | tf_op jit(solution)/shard_map/ppermute | solution.py:99
  210.6 2.1 collective-permute-done.58.came
  (172 shorter events, 47.0 us)
Async XLA Ops:
  7.1 13.0 %collective-permute-start.1 = (bf16[24,3200]{1,0:T(8,128)(2,1)S(1)}, bf16[24,3200]{1,0:T(8,128)(2,1)S(1)}, u32[]{:S(2)}, u32[]{:S(2)}) collective-permute-start(bf16[24,3200]{1,0:T(8,128)(2,1)S(1)} %get-tuple-element.139.a0), channel_id=1, source_target_pairs={{0,2},{1,3},{2,0},{3,1},{4,6},{5,7},{6,4},{7,5},{8,10},{9,11},{10,... | collective-permute-start | bytes 460808 | tf_op jit(solution)/shard_map/ppermute | solution.py:99
  7.1 13.0 %collective-permute-start = (bf16[24,3200]{1,0:T(8,128)(2,1)S(1)}, bf16[24,3200]{1,0:T(8,128)(2,1)S(1)}, u32[]{:S(2)}, u32[]{:S(2)}) collective-permute-start(bf16[24,3200]{1,0:T(8,128)(2,1)S(1)} %get-tuple-element.139.a0), channel_id=1, source_target_pairs={{0,1},{1,0},{2,3},{3,2},{4,5},{5,4},{6,7},{7,6},{8,9},{9,8},{10,11... | collective-permute-start | bytes 460808 | tf_op jit(solution)/shard_map/ppermute | solution.py:99
  20.2 15.0 %collective-permute-start.4 = (bf16[96,3200]{1,0:T(8,128)(2,1)S(1)}, bf16[96,3200]{1,0:T(8,128)(2,1)S(1)}, u32[]{:S(2)}, u32[]{:S(2)}) collective-permute-start(bf16[96,3200]{1,0:T(8,128)(2,1)S(1)} %z_join.5.refs_0_.refs_1_), channel_id=1, source_target_pairs={{0,8},{1,9},{2,10},{3,11},{4,12},{5,13},{6,14},{7,15},{8,0},{9,1},... | collective-permute-start | bytes 1843208 | tf_op jit(solution)/shard_map/ppermute | solution.py:99
  21.7 15.0 %collective-permute-start.7 = (bf16[96,3200]{1,0:T(8,128)(2,1)S(1)}, bf16[96,3200]{1,0:T(8,128)(2,1)S(1)}, u32[]{:S(2)}, u32[]{:S(2)}) collective-permute-start(bf16[96,3200]{1,0:T(8,128)(2,1)S(1)} %z_join.5.refs_0_.refs_1_), channel_id=1, source_target_pairs={{0,16},{1,17},{2,18},{3,19},{4,20},{5,21},{6,22},{7,23},{8,24},{9,... | collective-permute-start | bytes 1843208 | tf_op jit(solution)/shard_map/ppermute | solution.py:99
  23.3 20.4 %collective-permute-start.3 = (bf16[96,3200]{1,0:T(8,128)(2,1)S(1)}, bf16[96,3200]{1,0:T(8,128)(2,1)S(1)}, u32[]{:S(2)}, u32[]{:S(2)}) collective-permute-start(bf16[96,3200]{1,0:T(8,128)(2,1)S(1)} %z_join.5.refs_0_.refs_1_), channel_id=1, source_target_pairs={{0,4},{1,5},{2,6},{3,7},{4,0},{5,1},{6,2},{7,3},{8,12},{9,13},{10,... | collective-permute-start | bytes 1843208 | tf_op jit(solution)/shard_map/ppermute | solution.py:99
  43.7 21.1 %collective-permute-start.16 = (bf16[96,3072]{1,0:T(8,128)(2,1)S(1)}, bf16[96,3072]{1,0:T(8,128)(2,1)S(1)}, u32[]{:S(2)}, u32[]{:S(2)}) collective-permute-start(bf16[96,3072]{1,0:T(8,128)(2,1)S(1)} %z_join.7.refs_0_), channel_id=1, source_target_pairs={{0,16},{1,17},{2,18},{3,19},{4,20},{5,21},{6,22},{7,23},{8,24},{9,... | collective-permute-start | bytes 1769480 | tf_op jit(solution)/shard_map/ppermute | solution.py:99
  44.9 20.0 %collective-permute-start.15 = (bf16[96,3072]{1,0:T(8,128)(2,1)S(1)}, bf16[96,3072]{1,0:T(8,128)(2,1)S(1)}, u32[]{:S(2)}, u32[]{:S(2)}) collective-permute-start(bf16[96,3072]{1,0:T(8,128)(2,1)S(1)} %z_join.7.refs_0_), channel_id=1, source_target_pairs={{0,8},{1,9},{2,10},{3,11},{4,12},{5,13},{6,14},{7,15},{8,0},{9,1},... | collective-permute-start | bytes 1769480 | tf_op jit(solution)/shard_map/ppermute | solution.py:99
  46.1 10.3 %collective-permute-start.14 = (bf16[96,768]{1,0:T(8,128)(2,1)S(1)}, bf16[96,768]{1,0:T(8,128)(2,1)S(1)}, u32[]{:S(2)}, u32[]{:S(2)}) collective-permute-start(bf16[96,768]{1,0:T(8,128)(2,1)S(1)} %get-tuple-element.146.a0), channel_id=1, source_target_pairs={{0,2},{1,3},{2,0},{3,1},{4,6},{5,7},{6,4},{7,5},{8,10},{9,11},{10,... | collective-permute-start | bytes 442376 | tf_op jit(solution)/shard_map/ppermute | solution.py:99
  49.4 17.4 %collective-permute-start.17 = (bf16[4,96,512]{2,1,0:T(8,128)(2,1)S(1)}, bf16[4,96,512]{2,1,0:T(8,128)(2,1)S(1)}, u32[]{:S(2)}, u32[]{:S(2)}) collective-permute-start(bf16[4,96,512]{2,1,0:T(8,128)(2,1)S(1)} %get-tuple-element.153), channel_id=1, source_target_pairs={{0,4},{1,5},{2,6},{3,7},{4,0},{5,1},{6,2},{7,3},{8,12},{9,13},{10,... | collective-permute-start | bytes 1179656 | tf_op jit(solution)/shard_map/ppermute | solution.py:99
  66.2 11.1 %collective-permute-start.21 = (bf16[96,3072]{1,0:T(8,128)(2,1)S(1)}, bf16[96,3072]{1,0:T(8,128)(2,1)S(1)}, u32[]{:S(2)}, u32[]{:S(2)}) collective-permute-start(bf16[96,3072]{1,0:T(8,128)(2,1)S(1)} %z_join.7.refs_0_), channel_id=1, source_target_pairs={{0,4},{1,5},{2,6},{3,7},{4,0},{5,1},{6,2},{7,3},{8,12},{9,13},{10,... | collective-permute-start | bytes 1769480 | tf_op jit(solution)/shard_map/ppermute | solution.py:99
  66.2 10.3 %collective-permute-start.20 = (bf16[96,1536]{1,0:T(8,128)(2,1)S(1)}, bf16[96,1536]{1,0:T(8,128)(2,1)S(1)}, u32[]{:S(2)}, u32[]{:S(2)}) collective-permute-start(bf16[96,1536]{1,0:T(8,128)(2,1)S(1)} %slice.21), channel_id=1, source_target_pairs={{0,8},{1,9},{2,10},{3,11},{4,12},{5,13},{6,14},{7,15},{8,0},{9,1},... | collective-permute-start | bytes 884744 | tf_op jit(solution)/shard_map/ppermute | solution.py:99
  66.8 10.3 %collective-permute-start.18 = (bf16[192,768]{1,0:T(8,128)(2,1)S(1)}, bf16[192,768]{1,0:T(8,128)(2,1)S(1)}, u32[]{:S(2)}, u32[]{:S(2)}) collective-permute-start(bf16[192,768]{1,0:T(8,128)(2,1)S(1)} %z_join.8.a), channel_id=1, source_target_pairs={{0,1},{1,0},{2,3},{3,2},{4,5},{5,4},{6,7},{7,6},{8,9},{9,8},{10,11... | collective-permute-start | bytes 884744 | tf_op jit(solution)/shard_map/ppermute | solution.py:99
  66.8 12.6 %collective-permute-start.22 = (bf16[96,3072]{1,0:T(8,128)(2,1)S(1)}, bf16[96,3072]{1,0:T(8,128)(2,1)S(1)}, u32[]{:S(2)}, u32[]{:S(2)}) collective-permute-start(bf16[96,3072]{1,0:T(8,128)(2,1)S(1)} %collective-permute-done.15.refs_2_), channel_id=1, source_target_pairs={{0,4},{1,5},{2,6},{3,7},{4,0},{5,1},{6,2},{7,3},{8,12},{9,13},{10,... | collective-permute-start | bytes 1769480 | tf_op jit(solution)/shard_map/ppermute | solution.py:99
  77.3 15.7 %collective-permute-start.27 = (bf16[384,768]{1,0:T(8,128)(2,1)S(1)}, bf16[384,768]{1,0:T(8,128)(2,1)S(1)}, u32[]{:S(2)}, u32[]{:S(2)}) collective-permute-start(bf16[384,768]{1,0:T(8,128)(2,1)S(1)} %z_join.9.refs_0_), channel_id=1, source_target_pairs={{0,16},{1,17},{2,18},{3,19},{4,20},{5,21},{6,22},{7,23},{8,24},{9,... | collective-permute-start | bytes 1769480 | tf_op jit(solution)/shard_map/ppermute | solution.py:99
  78.8 15.4 %collective-permute-start.26 = (bf16[384,768]{1,0:T(8,128)(2,1)S(1)}, bf16[384,768]{1,0:T(8,128)(2,1)S(1)}, u32[]{:S(2)}, u32[]{:S(2)}) collective-permute-start(bf16[384,768]{1,0:T(8,128)(2,1)S(1)} %z_join.9.refs_0_), channel_id=1, source_target_pairs={{0,8},{1,9},{2,10},{3,11},{4,12},{5,13},{6,14},{7,15},{8,0},{9,1},... | collective-permute-start | bytes 1769480 | tf_op jit(solution)/shard_map/ppermute | solution.py:99
  94.2 10.5 %collective-permute-start.28 = (bf16[4,384,512]{2,1,0:T(8,128)(2,1)S(1)}, bf16[4,384,512]{2,1,0:T(8,128)(2,1)S(1)}, u32[]{:S(2)}, u32[]{:S(2)}) collective-permute-start(bf16[4,384,512]{2,1,0:T(8,128)(2,1)S(1)} %get-tuple-element.170), channel_id=1, source_target_pairs={{0,4},{1,5},{2,6},{3,7},{4,0},{5,1},{6,2},{7,3},{8,12},{9,13},{10,... | collective-permute-start | bytes 4718600 | tf_op jit(solution)/shard_map/ppermute | solution.py:99
  96.2 10.6 %collective-permute-start.31 = (bf16[384,768]{1,0:T(8,128)(2,1)S(1)}, bf16[384,768]{1,0:T(8,128)(2,1)S(1)}, u32[]{:S(2)}, u32[]{:S(2)}) collective-permute-start(bf16[384,768]{1,0:T(8,128)(2,1)S(1)} %collective-permute-done.27.refs_4_), channel_id=1, source_target_pairs={{0,4},{1,5},{2,6},{3,7},{4,0},{5,1},{6,2},{7,3},{8,12},{9,13},{10,... | collective-permute-start | bytes 1769480 | tf_op jit(solution)/shard_map/ppermute | solution.py:99
  116.8 16.0 %collective-permute-start.42 = (bf16[512,3072]{1,0:T(8,128)(2,1)S(1)}, bf16[512,3072]{1,0:T(8,128)(2,1)S(1)}, u32[]{:S(2)}, u32[]{:S(2)}) collective-permute-start(bf16[512,3072]{1,0:T(8,128)(2,1)S(1)} %get-tuple-element.200.inner_grad.refs_6_), channel_id=1, source_target_pairs={{0,4},{1,5},{2,6},{3,7},{4,0},{5,1},{6,2},{7,3},{8,12},{9,13},{10,... | collective-permute-start | bytes 9437192 | tf_op jit(solution)/shard_map/ppermute | solution.py:99
  117.2 14.3 %collective-permute-start.37 = (bf16[2,4,96,512]{3,2,1,0:T(8,128)(2,1)S(1)}, bf16[2,4,96,512]{3,2,1,0:T(8,128)(2,1)S(1)}, u32[]{:S(2)}, u32[]{:S(2)}) collective-permute-start(bf16[2,4,96,512]{3,2,1,0:T(8,128)(2,1)S(1)} %get-tuple-element.189), channel_id=1, source_target_pairs={{0,4},{1,5},{2,6},{3,7},{4,0},{5,1},{6,2},{7,3},{8,12},{9,13},{10,... | collective-permute-start | bytes 2359304 | tf_op jit(solution)/shard_map/ppermute | solution.py:99
  131.0 23.9 %collective-permute-start.45 = (bf16[384,768]{1,0:T(8,128)(2,1)S(1)}, bf16[384,768]{1,0:T(8,128)(2,1)S(1)}, u32[]{:S(2)}, u32[]{:S(2)}) collective-permute-start(bf16[384,768]{1,0:T(8,128)(2,1)S(1)} %get-tuple-element.196), channel_id=1, source_target_pairs={{0,8},{1,9},{2,10},{3,11},{4,12},{5,13},{6,14},{7,15},{8,0},{9,1},... | collective-permute-start | bytes 1769480 | tf_op jit(solution)/shard_map/ppermute | solution.py:99
  131.5 23.3 %collective-permute-start.46 = (bf16[384,768]{1,0:T(8,128)(2,1)S(1)}, bf16[384,768]{1,0:T(8,128)(2,1)S(1)}, u32[]{:S(2)}, u32[]{:S(2)}) collective-permute-start(bf16[384,768]{1,0:T(8,128)(2,1)S(1)} %get-tuple-element.212), channel_id=1, source_target_pairs={{0,16},{1,17},{2,18},{3,19},{4,20},{5,21},{6,22},{7,23},{8,24},{9,... | collective-permute-start | bytes 1769480 | tf_op jit(solution)/shard_map/ppermute | solution.py:99
  136.2 18.3 %collective-permute-start.43 = (bf16[96,1920]{1,0:T(8,128)(2,1)S(1)}, bf16[96,1920]{1,0:T(8,128)(2,1)S(1)}, u32[]{:S(2)}, u32[]{:S(2)}) collective-permute-start(bf16[96,1920]{1,0:T(8,128)(2,1)S(1)} %get-tuple-element.207), channel_id=1, source_target_pairs={{0,16},{1,17},{2,18},{3,19},{4,20},{5,21},{6,22},{7,23},{8,24},{9,... | collective-permute-start | bytes 1105928 | tf_op jit(solution)/shard_map/ppermute | solution.py:99
  137.2 17.2 %collective-permute-start.44 = (bf16[96,1920]{1,0:T(8,128)(2,1)S(1)}, bf16[96,1920]{1,0:T(8,128)(2,1)S(1)}, u32[]{:S(2)}, u32[]{:S(2)}) collective-permute-start(bf16[96,1920]{1,0:T(8,128)(2,1)S(1)} %get-tuple-element.209), channel_id=1, source_target_pairs={{0,8},{1,9},{2,10},{3,11},{4,12},{5,13},{6,14},{7,15},{8,0},{9,1},... | collective-permute-start | bytes 1105928 | tf_op jit(solution)/shard_map/ppermute | solution.py:99
  156.0 19.5 %collective-permute-start.51 = (bf16[96,3840]{1,0:T(8,128)(2,1)S(1)}, bf16[96,3840]{1,0:T(8,128)(2,1)S(1)}, u32[]{:S(2)}, u32[]{:S(2)}) collective-permute-start(bf16[96,3840]{1,0:T(8,128)(2,1)S(1)} %get-tuple-element.226), channel_id=1, source_target_pairs={{0,16},{1,17},{2,18},{3,19},{4,20},{5,21},{6,22},{7,23},{8,24},{9,... | collective-permute-start | bytes 2211848 | tf_op jit(solution)/shard_map/ppermute | solution.py:99
  157.0 18.4 %collective-permute-start.50 = (bf16[96,3840]{1,0:T(8,128)(2,1)S(1)}, bf16[96,3840]{1,0:T(8,128)(2,1)S(1)}, u32[]{:S(2)}, u32[]{:S(2)}) collective-permute-start(bf16[96,3840]{1,0:T(8,128)(2,1)S(1)} %get-tuple-element.210), channel_id=1, source_target_pairs={{0,8},{1,9},{2,10},{3,11},{4,12},{5,13},{6,14},{7,15},{8,0},{9,1},... | collective-permute-start | bytes 2211848 | tf_op jit(solution)/shard_map/ppermute | solution.py:99
  158.5 15.1 %collective-permute-start.49 = (bf16[192,768]{1,0:T(8,128)(2,1)S(1)}, bf16[192,768]{1,0:T(8,128)(2,1)S(1)}, u32[]{:S(2)}, u32[]{:S(2)}) collective-permute-start(bf16[192,768]{1,0:T(8,128)(2,1)S(1)} %get-tuple-element.223), channel_id=1, source_target_pairs={{0,2},{1,3},{2,0},{3,1},{4,6},{5,7},{6,4},{7,5},{8,10},{9,11},{10,... | collective-permute-start | bytes 884744 | tf_op jit(solution)/shard_map/ppermute | solution.py:99
  176.0 17.7 %collective-permute-start.52 = (bf16[48,3840]{1,0:T(8,128)(2,1)S(1)}, bf16[48,3840]{1,0:T(8,128)(2,1)S(1)}, u32[]{:S(2)}, u32[]{:S(2)}) collective-permute-start(bf16[48,3840]{1,0:T(8,128)(2,1)S(1)} %get-tuple-element.228), channel_id=1, source_target_pairs={{0,2},{1,3},{2,0},{3,1},{4,6},{5,7},{6,4},{7,5},{8,10},{9,11},{10,... | collective-permute-start | bytes 1105928 | tf_op jit(solution)/shard_map/ppermute | solution.py:99
  181.8 12.0 %collective-permute-start.55 = (bf16[96,2432]{1,0:T(8,128)(2,1)S(1)}, bf16[96,2432]{1,0:T(8,128)(2,1)S(1)}, u32[]{:S(2)}, u32[]{:S(2)}) collective-permute-start(bf16[96,2432]{1,0:T(8,128)(2,1)S(1)} %get-tuple-element.238), channel_id=1, source_target_pairs={{0,8},{1,9},{2,10},{3,11},{4,12},{5,13},{6,14},{7,15},{8,0},{9,1},... | collective-permute-start | bytes 1400840 | tf_op jit(solution)/shard_map/ppermute | solution.py:99
  183.0 11.2 %collective-permute-start.56 = (bf16[96,2432]{1,0:T(8,128)(2,1)S(1)}, bf16[96,2432]{1,0:T(8,128)(2,1)S(1)}, u32[]{:S(2)}, u32[]{:S(2)}) collective-permute-start(bf16[96,2432]{1,0:T(8,128)(2,1)S(1)} %get-tuple-element.239), channel_id=1, source_target_pairs={{0,16},{1,17},{2,18},{3,19},{4,20},{5,21},{6,22},{7,23},{8,24},{9,... | collective-permute-start | bytes 1400840 | tf_op jit(solution)/shard_map/ppermute | solution.py:99
  194.6 12.9 %collective-permute-start.57 = (bf16[48,2432]{1,0:T(8,128)(2,1)S(1)}, bf16[48,2432]{1,0:T(8,128)(2,1)S(1)}, u32[]{:S(2)}, u32[]{:S(2)}) collective-permute-start(bf16[48,2432]{1,0:T(8,128)(2,1)S(1)} %get-tuple-element.241), channel_id=1, source_target_pairs={{0,2},{1,3},{2,0},{3,1},{4,6},{5,7},{6,4},{7,5},{8,10},{9,11},{10,... | collective-permute-start | bytes 700424 | tf_op jit(solution)/shard_map/ppermute | solution.py:99
  194.6 13.0 %collective-permute-start.60 = (bf16[96,768]{1,0:T(8,128)(2,1)S(1)}, bf16[96,768]{1,0:T(8,128)(2,1)S(1)}, u32[]{:S(2)}, u32[]{:S(2)}) collective-permute-start(bf16[96,768]{1,0:T(8,128)(2,1)S(1)} %get-tuple-element.257), channel_id=1, source_target_pairs={{0,1},{1,0},{2,3},{3,2},{4,5},{5,4},{6,7},{7,6},{8,9},{9,8},{10,11... | collective-permute-start | bytes 442376 | tf_op jit(solution)/shard_map/ppermute | solution.py:99
  197.1 12.7 %collective-permute-start.59 = (bf16[24,3840]{1,0:T(8,128)(2,1)S(1)}, bf16[24,3840]{1,0:T(8,128)(2,1)S(1)}, u32[]{:S(2)}, u32[]{:S(2)}) collective-permute-start(bf16[24,3840]{1,0:T(8,128)(2,1)S(1)} %get-tuple-element.249), channel_id=1, source_target_pairs={{0,1},{1,0},{2,3},{3,2},{4,5},{5,4},{6,7},{7,6},{8,9},{9,8},{10,11... | collective-permute-start | bytes 552968 | tf_op jit(solution)/shard_map/ppermute | solution.py:99
  (51 other events, 384.1 us)

commit v2 on v1

--- a/solution.py
+++ b/solution.py
@@ -27,7 +27,7 @@
     "project": 1.5,
     "attend": 2.0,
     "mix": 3.0,
-    "inner": 11.0,
+    "inner": 9.0,
     "outer": 6.0,
     "slope": 3.7,
     "grad_outer": 2.6,
@@ -299,7 +299,7 @@
         qkv_kernel,
         "project",
         args,
-        [smem(), vmem()] + [hbm()] * PIECES,
+        [smem(), vmem()] + [vmem()] * PIECES,
         (sds((size, width)),) * 3 + (sds((16, width), F32), sds((1, 4 * width), F32), sds((width, width))),
         scratch=[pltpu.VMEM((width, cols), BF16), pltpu.SemaphoreType.DMA((PIECES,))],
         limit=14,
@@ -437,7 +437,7 @@
         inner_kernel,
         "inner",
         args,
-        [smem()] + [vmem()] * 2 + [hbm()] * PIECES,
+        [smem()] + [vmem()] * (2 + PIECES),
         (sds((size, hidden)), sds((size, hidden)), sds((width, hidden)), half, half),
         scratch=[pltpu.SemaphoreType.DMA((PIECES,))],
         limit=14,
@@ -908,20 +908,19 @@
     first_blocks = row_blocks(z_first, x_first, y_first, f_first)
     z_second = z_join_pairs(at, second, swap(second, 1))
     x_second, y_second = swap(z_second, 8), swap(z_second, 16)
-    third = after(third, z_second)
+    third = after(third, z_second, first_blocks[7][0], first_blocks[7][1])
     third_came = swap(third, 2)
 
     tok_keep, tok_send = turn_tokens(at, tokens)
     tok_came = swap(tok_send, 4)
     queries, key_rows, value_rows, lines, bias, w_out = project(at, tokens, first_blocks)
-    third = pair_join(third, after(third_came, queries))
-    queries = after(queries, third)
     mixed, mixed_t, lse = attend(lengths, queries, key_rows, value_rows)
-    mixed, x_second, y_second = lax.optimization_barrier((mixed, x_second, y_second))
+    third = pair_join(third, after(third_came, mixed))
+    mixed, x_second, y_second, third = lax.optimization_barrier((mixed, x_second, y_second, third))
     f_second = forward_halves(x_second, y_second)
     unit, scale, values, b_keep, b_send = mix_stage(at, tokens, after(mixed, tok_came), mixed_t, lines, w_out)
     b_came = swap(b_send, 4)
-    second_blocks = row_blocks(z_second, x_second, y_second, [after(f, values) for f in f_second])
+    second_blocks = row_blocks(z_second, x_second, y_second, f_second)
     z_third = z_join_pairs(at, third, after(swap(third, 1), *f_second))
     x_third, y_third = swap(z_third, 8), swap(z_third, 16)
     activ, slope, w_inner, a_keep, a_send = inner_stage(at, after(values, z_third), bias, second_blocks)

time: 214 us -> 209 us (0.977)
  starting transfers between devices: 41.4 us -> 46.2 us
  waiting for transfers between devices: 93.4 us -> 88.9 us
  Pallas kernels: 74.1 us -> 71.4 us
  local copies, waits for them, and re-layouts: 2.59 us -> 0.2 us
    ppermute x61, starting transfers between devices: 41.4 us -> 46.2 us  [swap(): return lax.ppermute(value, AXES, [(i, i ^ mask) for i in range(32)])]
    ppermute x61, waiting for transfers between devices: 93.4 us -> 88.9 us  [swap(): return lax.ppermute(value, AXES, [(i, i ^ mask) for i in range(32)])]
    pallas_call x32, Pallas kernels: 74.1 us -> 71.4 us  [call(): pl.pallas_call(kernel, out_shape=out_shape, name=name, input_output_alias...]
    unnamed x44 -> x24, local copies, waits for them, and re-layouts: 2.44 us -> 0.05 us
where the time goes in v2:
time: 209 us
  waiting for transfers between devices  88.9 us (43%)
  Pallas kernels  71.4 us (34%)
  starting transfers between devices  46.2 us (22%)
    ppermute x61, waiting for transfers between devices, swap(): return lax.ppermute(value, AXES, [(i, i ^ mask) for i in range(32)])  88.9 us
    pallas_call x32, Pallas kernels, call(): pl.pallas_call(kernel, out_shape=out_shape, name=name, input_output_alias...  71.4 us
    ppermute x61, starting transfers between devices, swap(): return lax.ppermute(value, AXES, [(i, i ^ mask) for i in range(32)])  46.2 us
  transfers between devices with their start and end apart: 61, of which 27 were waited for; matrix products, arithmetic and copies ran while one was open for 0% of the time, Pallas kernels for 30%

profile of v2, /device:TPU:0, one launch (start us, length us, event | category | flops | bytes accessed | tf_op | source)
XLA Modules:
  0.0 208.8 jit_solution(11975947853241435106)
XLA Ops:
  2.0 5.1 %collective-permute-start.2 = (bf16[24,3200]{1,0:T(8,128)(2,1)S(1)}, bf16[24,3200]{1,0:T(8,128)(2,1)S(1)}, u32[]{:S(2)}, u32[]{:S(2)}) collective-permute-start(bf16[24,3200]{1,0:T(8,128)(2,1)S(1)} %get-tuple-element.137.a0), channel_id=1, source_target_pairs={{0,3},{1,2},{2,1},{3,0},{4,7},{5,6},{6,5},{7,4},{8,11},{9,10},{10,... | collective-permute-start | bytes 460808 | tf_op jit(solution)/shard_map/ppermute | solution.py:99
  7.7 4.3 %collective-permute-done.2.a3 = bf16[24,3200]{1,0:T(8,128)(2,1)S(1)} collective-permute-done((bf16[24,3200]{1,0:T(8,128)(2,1)S(1)}, bf16[24,3200]{1,0:T(8,128)(2,1)S(1)}, u32[]{:S(2)}, u32[]{:S(2)}) %collective-permute-start.2) | collective-permute-done | bytes 153632 | tf_op jit(solution)/shard_map/ppermute | solution.py:99
  12.0 8.1 %collective-permute-done.1.a2 = bf16[24,3200]{1,0:T(8,128)(2,1)S(1)} collective-permute-done((bf16[24,3200]{1,0:T(8,128)(2,1)S(1)}, bf16[24,3200]{1,0:T(8,128)(2,1)S(1)}, u32[]{:S(2)}, u32[]{:S(2)}) %collective-permute-start.1) | collective-permute-done | bytes 153632 | tf_op jit(solution)/shard_map/ppermute | solution.py:99
  20.2 1.6 collective-permute-start.7
  23.3 11.9 %collective-permute-done.7.refs_4_.refs_5_ = bf16[96,3200]{1,0:T(8,128)(2,1)S(1)} collective-permute-done((bf16[96,3200]{1,0:T(8,128)(2,1)S(1)}, bf16[96,3200]{1,0:T(8,128)(2,1)S(1)}, u32[]{:S(2)}, u32[]{:S(2)}) %collective-permute-start.7) | collective-permute-done | bytes 614432 | tf_op jit(solution)/shard_map/ppermute | solution.py:99
  36.8 1.6 collective-permute-start.9
  38.4 4.8 %collective-permute-done.10.refs_7_.refs_8_ = bf16[96,1664]{1,0:T(8,128)(2,1)S(1)} collective-permute-done((bf16[96,1664]{1,0:T(8,128)(2,1)S(1)}, bf16[96,1664]{1,0:T(8,128)(2,1)S(1)}, u32[]{:S(2)}, u32[]{:S(2)}) %collective-permute-start.10) | collective-permute-done | bytes 319520 | tf_op jit(solution)/shard_map/ppermute | solution.py:99
  49.4 3.3 %project.1 = (bf16[512,768]{1,0:T(8,128)(2,1)S(1)}, bf16[512,768]{1,0:T(8,128)(2,1)S(1)}, bf16[512,768]{1,0:T(8,128)(2,1)S(1)}, f32[16,768]{1,0:T(8,128)S(1)}, f...) custom-call(s32[1]{0:T(128)} %bitcast.at_ref.refs_4_, bf16[512,768]{1,0:T(8,128)(2,1)S(1)} %copy-done.3, ...), custom_call_target="tpu_custom_call" | custom-call | flops 825000000 | tf_op jit(solution)/shard_map/project/pallas_call | solution.py:87
  52.8 8.4 %attend.1 = (bf16[512,768]{1,0:T(8,128)(2,1)S(1)}, bf16[768,512]{1,0:T(8,128)(2,1)S(1)}, f32[6,2,512]{2,1,0:T(2,128)S(1)}) custom-call(s32[1]{0:T(128)S(6)} %copy.43.len_ref, bf16[512,768]{1,0:T(8,128)(2,1)S(1)} %get-tuple-element.141.q_ref, bf16[512,768]{1,0:T(8,128)(2,1)S(1)} %get-tuple-element.142.k_ref, bf16[512,768]{1,0:T(8,128)(2,1)S(1)} %get-tuple-element.143.v_ref), custom_call_target="tpu_custom_call" | custom-call | flops 1100000000 | tf_op jit(solution)/shard_map/attend/pallas_call | solution.py:87
  65.5 5.1 %collective-permute-done.20.refs_7_ = bf16[96,1536]{1,0:T(8,128)(2,1)S(1)} collective-permute-done((bf16[96,1536]{1,0:T(8,128)(2,1)S(1)}, bf16[96,1536]{1,0:T(8,128)(2,1)S(1)}, u32[]{:S(2)}, u32[]{:S(2)}) %collective-permute-start.20) | collective-permute-done | bytes 294944 | tf_op jit(solution)/shard_map/ppermute | solution.py:99
  70.5 2.1 %collective-permute-done.19.refs_6_ = bf16[96,1536]{1,0:T(8,128)(2,1)S(1)} collective-permute-done((bf16[96,1536]{1,0:T(8,128)(2,1)S(1)}, bf16[96,1536]{1,0:T(8,128)(2,1)S(1)}, u32[]{:S(2)}, u32[]{:S(2)}) %collective-permute-start.19) | collective-permute-done | bytes 294944 | tf_op jit(solution)/shard_map/ppermute | solution.py:99
  75.5 3.0 %mix.1 = (f32[512,768]{1,0:T(8,128)S(1)}, f32[512,128]{1,0:T(8,128)S(1)}, bf16[512,768]{1,0:T(8,128)(2,1)S(1)}, bf16[2,4,96,512]{3,2,1,0:T(8,128)(2,1)S(1)}, bf16[2,4,96,512]{3,2,1,0:T(8,128)(2,1)S(1)}) custom-call(s32[1]{0:T(128)} %bitcast.at_ref.refs_4_, bf16[512,768]{1,0:T(8,128)(2,1)S(1)} %copy-done.3, bf16[512,768]{1,0:T(8,128)(2,1)S(1)} %get-tuple-element.151.mixed, ...), custom_call_target="tpu_custom_call" | custom-call | flops 1650000000 | tf_op jit(solution)/shard_map/mix/pallas_call | solution.py:87
  78.5 8.8 %inner.1 = (bf16[512,3072]{1,0:T(8,128)(2,1)S(1)}, bf16[512,3072]{1,0:T(8,128)(2,1)S(1)}, bf16[768,3072]{1,0:T(8,128)(2,1)S(1)}, bf16[4,384,512]{2,1,0:T(8,128)(2,1)S(1)}, bf16[4,384,512]{2,1,0:T(8,128)(2,1)S(1)}) custom-call(s32[1]{0:T(128)} %bitcast.at_ref.refs_4_, bf16[512,768]{1,0:T(8,128)(2,1)S(1)} %get-tuple-element.160.values, ...), custom_call_target="tpu_custom_call" | custom-call | flops 4950000128 | tf_op jit(solution)/shard_map/inner/pallas_call | solution.py:87
  87.3 1.8 collective-permute-done.27.refs_4_
  92.7 6.8 %collective-permute-done.32.refs_6_ = bf16[384,384]{1,0:T(8,128)(2,1)S(1)} collective-permute-done((bf16[384,384]{1,0:T(8,128)(2,1)S(1)}, bf16[384,384]{1,0:T(8,128)(2,1)S(1)}, u32[]{:S(2)}, u32[]{:S(2)}) %collective-permute-start.32) | collective-permute-done | bytes 294944 | tf_op jit(solution)/shard_map/ppermute | solution.py:99
  102.4 6.1 %outer.1 = (bf16[512,768]{1,0:T(8,128)(2,1)}, f32[512,768]{1,0:T(8,128)S(1)}, bf16[512,768]{1,0:T(8,128)(2,1)S(1)}, f32[8,768]{1,0:T(8,128)S(1)}) custom-call(s32[1]{0:T(128)} %bitcast.at_ref.refs_4_, s32[1]{0:T(128)S(6)} %copy.43.len_ref, bf16[512,3072]{1,0:T(8,128)(2,1)S(1)} %get-tuple-element.167.activ, bf16[512,768]{1,0:T(8,128)(2,1)S(1)} %get-tuple-element.160.values, ...), custom_call_target="tpu_custom_call" | custom-call | flops 3300000000 | tf_op jit(solution)/shard_map/outer/pallas_call | solution.py:87
  108.6 3.7 %slope.1 = (bf16[512,3072]{1,0:T(8,128)(2,1)S(1)}, f32[1,3072]{1,0:T(1,128)S(1)}) custom-call(s32[1]{0:T(128)} %bitcast.at_ref.refs_4_, bf16[512,768]{1,0:T(8,128)(2,1)S(1)} %get-tuple-element.170.outer_grad.refs_2_, bf16[512,3072]{1,0:T(8,128)(2,1)S(1)} %get-tuple-element.171.slope, bf16[384,768]{1,0:T(8,128)(2,1)S(1)} %z_join.9.refs_0_, ...), custom_call_target="tpu_custom_call" | custom-call | flops 2035000064 | tf_op jit(solution)/shard_map/slope/pallas_call | solution.py:87
  112.9 2.6 %grad_outer.1 = (bf16[384,768]{1,0:T(8,128)(2,1)S(1)}, bf16[384,768]{1,0:T(8,128)(2,1)S(1)}, bf16[384,768]{1,0:T(8,128)(2,1)S(1)}, bf16[384,384]{1,0:T(8,128)(2,1)S(1)}, bf16[384,384]{1,0:T(8,128)(2,1)S(1)}) custom-call(bf16[4,384,512]{2,1,0:T(8,128)(2,1)S(1)} %get-tuple-element.173.refs_0_, bf16[4,384,512]{2,1,0:T(8,128)(2,1)S(1)} %collective-permute-done.28.refs_1_, ...), custom_call_target="tpu_custom_call" | custom-call | flops 1430000000 | tf_op jit(solution)/shard_map/grad_outer/pallas_call | solution.py:87
  117.6 6.6 %normed_back.1 = (f32[512,768]{1,0:T(8,128)S(1)}, bf16[512,384]{1,0:T(8,128)(2,1)S(1)}, bf16[512,384]{1,0:T(8,128)(2,1)S(1)}, bf16[512,768]{1,0:T(8,128)(2,1)S(1)}, f32[8,768]{1,0:T(8,128)S(1)}) custom-call(bf16[512,3072]{1,0:T(8,128)(2,1)S(1)} %get-tuple-element.196.inner_grad.refs_6_, f32[512,768]{1,0:T(8,128)S(1)} %get-tuple-element.177.resid_two, ...), custom_call_target="tpu_custom_call" | custom-call | flops 2750000128 | tf_op jit(solution)/shard_map/normed_back/pallas_call | solution.py:87
  128.6 3.5 %grad_inner.1 = (bf16[96,3840]{1,0:T(8,128)(2,1)S(1)}, bf16[96,3840]{1,0:T(8,128)(2,1)S(1)}, bf16[96,3840]{1,0:T(8,128)(2,1)S(1)}, bf16[96,1920]{1,0:T(8,128)(2,1)S(1)}, bf16[96,1920]{1,0:T(8,128)(2,1)S(1)}) custom-call(bf16[2,4,96,512]{3,2,1,0:T(8,128)(2,1)S(1)} %get-tuple-element.184.refs_0_, bf16[2,4,96,512]{3,2,1,0:T(8,128)(2,1)S(1)} %collective-permute-done.37.refs_1_, ...), custom_call_target="tpu_custom_call" | custom-call | flops 1760000000 | tf_op jit(solution)/shard_map/grad_inner/pallas_call | solution.py:87
  134.1 11.5 %attend_back.1 = (bf16[3,512,768]{2,1,0:T(8,128)(2,1)S(1)}, f32[1,768]{1,0:T(1,128)S(1)}, f32[1,768]{1,0:T(1,128)S(1)}) custom-call(s32[1]{0:T(128)S(6)} %copy.43.len_ref, bf16[512,768]{1,0:T(8,128)(2,1)S(1)} %get-tuple-element.141.q_ref, bf16[512,768]{1,0:T(8,128)(2,1)S(1)} %get-tuple-element.142.k_ref, bf16[512,768]{1,0:T(8,128)(2,1)S(1)} %get-tuple-element.143.v_ref, ...), custom_call_target="tpu_custom_call" | custom-call | flops 6270000128 | tf_op jit(solution)/shard_map/attend_back/pallas_call | solution.py:87
  145.6 4.9 %collective-permute-done.43.p_ref = bf16[96,1920]{1,0:T(8,128)(2,1)S(1)} collective-permute-done((bf16[96,1920]{1,0:T(8,128)(2,1)S(1)}, bf16[96,1920]{1,0:T(8,128)(2,1)S(1)}, u32[]{:S(2)}, u32[]{:S(2)}) %collective-permute-start.43) | collective-permute-done | bytes 368672 | tf_op jit(solution)/shard_map/ppermute | solution.py:99
  154.0 1.8 collective-permute-start.49
  156.0 2.0 grad_first.1
  158.0 5.4 %tokens_back.1 = bf16[512,768]{1,0:T(8,128)(2,1)} custom-call(s32[1]{0:T(128)} %bitcast.at_ref.refs_4_, f32[512,768]{1,0:T(8,128)S(1)} %get-tuple-element.217.resid_grad, bf16[3,512,768]{2,1,0:T(8,128)(2,1)S(1)} %get-tuple-element.210.refs_2_.refs_0_, bf16[96,3200]{1,0:T(8,128)(2,1)} %copy-done, bf16[96,3200]{1,0:T(8,128)(2,1)} %copy-done.4, ...), custom_call_target="tpu_custom_call" | custom-call | flops 3080000000 | tf_op jit(solution)/shard_map/tokens_back/pallas_call | solution.py:87
  163.4 6.3 %collective-permute-done.49.came = bf16[192,768]{1,0:T(8,128)(2,1)S(1)} collective-permute-done((bf16[192,768]{1,0:T(8,128)(2,1)S(1)}, bf16[192,768]{1,0:T(8,128)(2,1)S(1)}, u32[]{:S(2)}, u32[]{:S(2)}) %collective-permute-start.49) | collective-permute-done | bytes 294944 | tf_op jit(solution)/shard_map/ppermute | solution.py:99
  172.4 2.6 %collective-permute-start.52 = (bf16[48,3840]{1,0:T(8,128)(2,1)S(1)}, bf16[48,3840]{1,0:T(8,128)(2,1)S(1)}, u32[]{:S(2)}, u32[]{:S(2)}) collective-permute-start(bf16[48,3840]{1,0:T(8,128)(2,1)S(1)} %get-tuple-element.224), channel_id=1, source_target_pairs={{0,2},{1,3},{2,0},{3,1},{4,6},{5,7},{6,4},{7,5},{8,10},{9,11},{10,... | collective-permute-start | bytes 1105928 | tf_op jit(solution)/shard_map/ppermute | solution.py:99
  175.0 1.8 collective-permute-done.53.p_ref
  179.0 11.0 %collective-permute-done.52.came = bf16[48,3840]{1,0:T(8,128)(2,1)S(1)} collective-permute-done((bf16[48,3840]{1,0:T(8,128)(2,1)S(1)}, bf16[48,3840]{1,0:T(8,128)(2,1)S(1)}, u32[]{:S(2)}, u32[]{:S(2)}) %collective-permute-start.52) | collective-permute-done | bytes 368672 | tf_op jit(solution)/shard_map/ppermute | solution.py:99
  191.2 2.3 %collective-permute-start.60 = (bf16[96,768]{1,0:T(8,128)(2,1)S(1)}, bf16[96,768]{1,0:T(8,128)(2,1)S(1)}, u32[]{:S(2)}, u32[]{:S(2)}) collective-permute-start(bf16[96,768]{1,0:T(8,128)(2,1)S(1)} %get-tuple-element.253), channel_id=1, source_target_pairs={{0,1},{1,0},{2,3},{3,2},{4,5},{5,4},{6,7},{7,6},{8,9},{9,8},{10,11... | collective-permute-start | bytes 442376 | tf_op jit(solution)/shard_map/ppermute | solution.py:99
  193.5 9.4 %collective-permute-done.57.came = bf16[48,2432]{1,0:T(8,128)(2,1)S(1)} collective-permute-done((bf16[48,2432]{1,0:T(8,128)(2,1)S(1)}, bf16[48,2432]{1,0:T(8,128)(2,1)S(1)}, u32[]{:S(2)}, u32[]{:S(2)}) %collective-permute-start.57) | collective-permute-done | bytes 233504 | tf_op jit(solution)/shard_map/ppermute | solution.py:99
  205.9 2.0 collective-permute-done.58.came
  (152 shorter events, 46.8 us)
Async XLA Ops:
  2.0 10.0 %collective-permute-start.2 = (bf16[24,3200]{1,0:T(8,128)(2,1)S(1)}, bf16[24,3200]{1,0:T(8,128)(2,1)S(1)}, u32[]{:S(2)}, u32[]{:S(2)}) collective-permute-start(bf16[24,3200]{1,0:T(8,128)(2,1)S(1)} %get-tuple-element.137.a0), channel_id=1, source_target_pairs={{0,3},{1,2},{2,1},{3,0},{4,7},{5,6},{6,5},{7,4},{8,11},{9,10},{10,... | collective-permute-start | bytes 460808 | tf_op jit(solution)/shard_map/ppermute | solution.py:99
  7.1 13.0 %collective-permute-start.1 = (bf16[24,3200]{1,0:T(8,128)(2,1)S(1)}, bf16[24,3200]{1,0:T(8,128)(2,1)S(1)}, u32[]{:S(2)}, u32[]{:S(2)}) collective-permute-start(bf16[24,3200]{1,0:T(8,128)(2,1)S(1)} %get-tuple-element.137.a0), channel_id=1, source_target_pairs={{0,2},{1,3},{2,0},{3,1},{4,6},{5,7},{6,4},{7,5},{8,10},{9,11},{10,... | collective-permute-start | bytes 460808 | tf_op jit(solution)/shard_map/ppermute | solution.py:99
  7.1 13.0 %collective-permute-start = (bf16[24,3200]{1,0:T(8,128)(2,1)S(1)}, bf16[24,3200]{1,0:T(8,128)(2,1)S(1)}, u32[]{:S(2)}, u32[]{:S(2)}) collective-permute-start(bf16[24,3200]{1,0:T(8,128)(2,1)S(1)} %get-tuple-element.137.a0), channel_id=1, source_target_pairs={{0,1},{1,0},{2,3},{3,2},{4,5},{5,4},{6,7},{7,6},{8,9},{9,8},{10,11... | collective-permute-start | bytes 460808 | tf_op jit(solution)/shard_map/ppermute | solution.py:99
  20.2 15.0 %collective-permute-start.7 = (bf16[96,3200]{1,0:T(8,128)(2,1)S(1)}, bf16[96,3200]{1,0:T(8,128)(2,1)S(1)}, u32[]{:S(2)}, u32[]{:S(2)}) collective-permute-start(bf16[96,3200]{1,0:T(8,128)(2,1)S(1)} %z_join.5.refs_0_.refs_1_), channel_id=1, source_target_pairs={{0,16},{1,17},{2,18},{3,19},{4,20},{5,21},{6,22},{7,23},{8,24},{9,... | collective-permute-start | bytes 1843208 | tf_op jit(solution)/shard_map/ppermute | solution.py:99
  21.8 15.0 %collective-permute-start.4 = (bf16[96,3200]{1,0:T(8,128)(2,1)S(1)}, bf16[96,3200]{1,0:T(8,128)(2,1)S(1)}, u32[]{:S(2)}, u32[]{:S(2)}) collective-permute-start(bf16[96,3200]{1,0:T(8,128)(2,1)S(1)} %z_join.5.refs_0_.refs_1_), channel_id=1, source_target_pairs={{0,8},{1,9},{2,10},{3,11},{4,12},{5,13},{6,14},{7,15},{8,0},{9,1},... | collective-permute-start | bytes 1843208 | tf_op jit(solution)/shard_map/ppermute | solution.py:99
  23.3 13.5 %collective-permute-start.5 = (bf16[24,3072]{1,0:T(8,128)(2,1)S(1)}, bf16[24,3072]{1,0:T(8,128)(2,1)S(1)}, u32[]{:S(2)}, u32[]{:S(2)}) collective-permute-start(bf16[24,3072]{1,0:T(8,128)(2,1)S(1)} %get-tuple-element.139.a0), channel_id=1, source_target_pairs={{0,2},{1,3},{2,0},{3,1},{4,6},{5,7},{6,4},{7,5},{8,10},{9,11},{10,... | collective-permute-start | bytes 442376 | tf_op jit(solution)/shard_map/ppermute | solution.py:99
  45.3 15.9 %collective-permute-start.15 = (bf16[96,3072]{1,0:T(8,128)(2,1)S(1)}, bf16[96,3072]{1,0:T(8,128)(2,1)S(1)}, u32[]{:S(2)}, u32[]{:S(2)}) collective-permute-start(bf16[96,3072]{1,0:T(8,128)(2,1)S(1)} %z_join.7.refs_0_), channel_id=1, source_target_pairs={{0,16},{1,17},{2,18},{3,19},{4,20},{5,21},{6,22},{7,23},{8,24},{9,... | collective-permute-start | bytes 1769480 | tf_op jit(solution)/shard_map/ppermute | solution.py:99
  46.9 15.1 %collective-permute-start.14 = (bf16[96,3072]{1,0:T(8,128)(2,1)S(1)}, bf16[96,3072]{1,0:T(8,128)(2,1)S(1)}, u32[]{:S(2)}, u32[]{:S(2)}) collective-permute-start(bf16[96,3072]{1,0:T(8,128)(2,1)S(1)} %z_join.7.refs_0_), channel_id=1, source_target_pairs={{0,8},{1,9},{2,10},{3,11},{4,12},{5,13},{6,14},{7,15},{8,0},{9,1},... | collective-permute-start | bytes 1769480 | tf_op jit(solution)/shard_map/ppermute | solution.py:99
  49.1 16.4 %collective-permute-start.17 = (bf16[4,96,512]{2,1,0:T(8,128)(2,1)S(1)}, bf16[4,96,512]{2,1,0:T(8,128)(2,1)S(1)}, u32[]{:S(2)}, u32[]{:S(2)}) collective-permute-start(bf16[4,96,512]{2,1,0:T(8,128)(2,1)S(1)} %get-tuple-element.150), channel_id=1, source_target_pairs={{0,4},{1,5},{2,6},{3,7},{4,0},{5,1},{6,2},{7,3},{8,12},{9,13},{10,... | collective-permute-start | bytes 1179656 | tf_op jit(solution)/shard_map/ppermute | solution.py:99
  49.2 12.0 %collective-permute-start.16 = (bf16[96,768]{1,0:T(8,128)(2,1)S(1)}, bf16[96,768]{1,0:T(8,128)(2,1)S(1)}, u32[]{:S(2)}, u32[]{:S(2)}) collective-permute-start(bf16[96,768]{1,0:T(8,128)(2,1)S(1)} %get-tuple-element.147.a0), channel_id=1, source_target_pairs={{0,2},{1,3},{2,0},{3,1},{4,6},{5,7},{6,4},{7,5},{8,10},{9,11},{10,... | collective-permute-start | bytes 442376 | tf_op jit(solution)/shard_map/ppermute | solution.py:99
  63.2 10.1 %collective-permute-start.21 = (bf16[96,3072]{1,0:T(8,128)(2,1)S(1)}, bf16[96,3072]{1,0:T(8,128)(2,1)S(1)}, u32[]{:S(2)}, u32[]{:S(2)}) collective-permute-start(bf16[96,3072]{1,0:T(8,128)(2,1)S(1)} %z_join.7.refs_0_), channel_id=1, source_target_pairs={{0,4},{1,5},{2,6},{3,7},{4,0},{5,1},{6,2},{7,3},{8,12},{9,13},{10,... | collective-permute-start | bytes 1769480 | tf_op jit(solution)/shard_map/ppermute | solution.py:99
  63.2 9.5 %collective-permute-start.19 = (bf16[96,1536]{1,0:T(8,128)(2,1)S(1)}, bf16[96,1536]{1,0:T(8,128)(2,1)S(1)}, u32[]{:S(2)}, u32[]{:S(2)}) collective-permute-start(bf16[96,1536]{1,0:T(8,128)(2,1)S(1)} %slice.20), channel_id=1, source_target_pairs={{0,16},{1,17},{2,18},{3,19},{4,20},{5,21},{6,22},{7,23},{8,24},{9,... | collective-permute-start | bytes 884744 | tf_op jit(solution)/shard_map/ppermute | solution.py:99
  65.5 13.0 %collective-permute-start.22 = (bf16[96,3072]{1,0:T(8,128)(2,1)S(1)}, bf16[96,3072]{1,0:T(8,128)(2,1)S(1)}, u32[]{:S(2)}, u32[]{:S(2)}) collective-permute-start(bf16[96,3072]{1,0:T(8,128)(2,1)S(1)} %collective-permute-done.14.refs_2_), channel_id=1, source_target_pairs={{0,4},{1,5},{2,6},{3,7},{4,0},{5,1},{6,2},{7,3},{8,12},{9,13},{10,... | collective-permute-start | bytes 1769480 | tf_op jit(solution)/shard_map/ppermute | solution.py:99
  73.3 15.8 %collective-permute-start.27 = (bf16[384,768]{1,0:T(8,128)(2,1)S(1)}, bf16[384,768]{1,0:T(8,128)(2,1)S(1)}, u32[]{:S(2)}, u32[]{:S(2)}) collective-permute-start(bf16[384,768]{1,0:T(8,128)(2,1)S(1)} %z_join.9.refs_0_), channel_id=1, source_target_pairs={{0,16},{1,17},{2,18},{3,19},{4,20},{5,21},{6,22},{7,23},{8,24},{9,... | collective-permute-start | bytes 1769480 | tf_op jit(solution)/shard_map/ppermute | solution.py:99
  74.5 15.5 %collective-permute-start.26 = (bf16[384,768]{1,0:T(8,128)(2,1)S(1)}, bf16[384,768]{1,0:T(8,128)(2,1)S(1)}, u32[]{:S(2)}, u32[]{:S(2)}) collective-permute-start(bf16[384,768]{1,0:T(8,128)(2,1)S(1)} %z_join.9.refs_0_), channel_id=1, source_target_pairs={{0,8},{1,9},{2,10},{3,11},{4,12},{5,13},{6,14},{7,15},{8,0},{9,1},... | collective-permute-start | bytes 1769480 | tf_op jit(solution)/shard_map/ppermute | solution.py:99
  90.0 10.2 %collective-permute-start.28 = (bf16[4,384,512]{2,1,0:T(8,128)(2,1)S(1)}, bf16[4,384,512]{2,1,0:T(8,128)(2,1)S(1)}, u32[]{:S(2)}, u32[]{:S(2)}) collective-permute-start(bf16[4,384,512]{2,1,0:T(8,128)(2,1)S(1)} %get-tuple-element.166), channel_id=1, source_target_pairs={{0,4},{1,5},{2,6},{3,7},{4,0},{5,1},{6,2},{7,3},{8,12},{9,13},{10,... | collective-permute-start | bytes 4718600 | tf_op jit(solution)/shard_map/ppermute | solution.py:99
  92.2 10.2 %collective-permute-start.31 = (bf16[384,768]{1,0:T(8,128)(2,1)S(1)}, bf16[384,768]{1,0:T(8,128)(2,1)S(1)}, u32[]{:S(2)}, u32[]{:S(2)}) collective-permute-start(bf16[384,768]{1,0:T(8,128)(2,1)S(1)} %collective-permute-done.27.refs_4_), channel_id=1, source_target_pairs={{0,4},{1,5},{2,6},{3,7},{4,0},{5,1},{6,2},{7,3},{8,12},{9,13},{10,... | collective-permute-start | bytes 1769480 | tf_op jit(solution)/shard_map/ppermute | solution.py:99
  112.3 16.2 %collective-permute-start.42 = (bf16[512,3072]{1,0:T(8,128)(2,1)S(1)}, bf16[512,3072]{1,0:T(8,128)(2,1)S(1)}, u32[]{:S(2)}, u32[]{:S(2)}) collective-permute-start(bf16[512,3072]{1,0:T(8,128)(2,1)S(1)} %get-tuple-element.196.inner_grad.refs_6_), channel_id=1, source_target_pairs={{0,4},{1,5},{2,6},{3,7},{4,0},{5,1},{6,2},{7,3},{8,12},{9,13},{10,... | collective-permute-start | bytes 9437192 | tf_op jit(solution)/shard_map/ppermute | solution.py:99
  112.8 14.7 %collective-permute-start.37 = (bf16[2,4,96,512]{3,2,1,0:T(8,128)(2,1)S(1)}, bf16[2,4,96,512]{3,2,1,0:T(8,128)(2,1)S(1)}, u32[]{:S(2)}, u32[]{:S(2)}) collective-permute-start(bf16[2,4,96,512]{3,2,1,0:T(8,128)(2,1)S(1)} %get-tuple-element.185), channel_id=1, source_target_pairs={{0,4},{1,5},{2,6},{3,7},{4,0},{5,1},{6,2},{7,3},{8,12},{9,13},{10,... | collective-permute-start | bytes 2359304 | tf_op jit(solution)/shard_map/ppermute | solution.py:99
  126.5 24.3 %collective-permute-start.45 = (bf16[384,768]{1,0:T(8,128)(2,1)S(1)}, bf16[384,768]{1,0:T(8,128)(2,1)S(1)}, u32[]{:S(2)}, u32[]{:S(2)}) collective-permute-start(bf16[384,768]{1,0:T(8,128)(2,1)S(1)} %get-tuple-element.192), channel_id=1, source_target_pairs={{0,8},{1,9},{2,10},{3,11},{4,12},{5,13},{6,14},{7,15},{8,0},{9,1},... | collective-permute-start | bytes 1769480 | tf_op jit(solution)/shard_map/ppermute | solution.py:99
  127.5 23.3 %collective-permute-start.46 = (bf16[384,768]{1,0:T(8,128)(2,1)S(1)}, bf16[384,768]{1,0:T(8,128)(2,1)S(1)}, u32[]{:S(2)}, u32[]{:S(2)}) collective-permute-start(bf16[384,768]{1,0:T(8,128)(2,1)S(1)} %get-tuple-element.208), channel_id=1, source_target_pairs={{0,16},{1,17},{2,18},{3,19},{4,20},{5,21},{6,22},{7,23},{8,24},{9,... | collective-permute-start | bytes 1769480 | tf_op jit(solution)/shard_map/ppermute | solution.py:99
  132.0 18.4 %collective-permute-start.43 = (bf16[96,1920]{1,0:T(8,128)(2,1)S(1)}, bf16[96,1920]{1,0:T(8,128)(2,1)S(1)}, u32[]{:S(2)}, u32[]{:S(2)}) collective-permute-start(bf16[96,1920]{1,0:T(8,128)(2,1)S(1)} %get-tuple-element.203), channel_id=1, source_target_pairs={{0,16},{1,17},{2,18},{3,19},{4,20},{5,21},{6,22},{7,23},{8,24},{9,... | collective-permute-start | bytes 1105928 | tf_op jit(solution)/shard_map/ppermute | solution.py:99
  133.1 17.4 %collective-permute-start.44 = (bf16[96,1920]{1,0:T(8,128)(2,1)S(1)}, bf16[96,1920]{1,0:T(8,128)(2,1)S(1)}, u32[]{:S(2)}, u32[]{:S(2)}) collective-permute-start(bf16[96,1920]{1,0:T(8,128)(2,1)S(1)} %get-tuple-element.205), channel_id=1, source_target_pairs={{0,8},{1,9},{2,10},{3,11},{4,12},{5,13},{6,14},{7,15},{8,0},{9,1},... | collective-permute-start | bytes 1105928 | tf_op jit(solution)/shard_map/ppermute | solution.py:99
  152.0 19.9 %collective-permute-start.51 = (bf16[96,3840]{1,0:T(8,128)(2,1)S(1)}, bf16[96,3840]{1,0:T(8,128)(2,1)S(1)}, u32[]{:S(2)}, u32[]{:S(2)}) collective-permute-start(bf16[96,3840]{1,0:T(8,128)(2,1)S(1)} %get-tuple-element.222), channel_id=1, source_target_pairs={{0,16},{1,17},{2,18},{3,19},{4,20},{5,21},{6,22},{7,23},{8,24},{9,... | collective-permute-start | bytes 2211848 | tf_op jit(solution)/shard_map/ppermute | solution.py:99
  153.0 18.8 %collective-permute-start.50 = (bf16[96,3840]{1,0:T(8,128)(2,1)S(1)}, bf16[96,3840]{1,0:T(8,128)(2,1)S(1)}, u32[]{:S(2)}, u32[]{:S(2)}) collective-permute-start(bf16[96,3840]{1,0:T(8,128)(2,1)S(1)} %get-tuple-element.206), channel_id=1, source_target_pairs={{0,8},{1,9},{2,10},{3,11},{4,12},{5,13},{6,14},{7,15},{8,0},{9,1},... | collective-permute-start | bytes 2211848 | tf_op jit(solution)/shard_map/ppermute | solution.py:99
  154.0 15.7 %collective-permute-start.49 = (bf16[192,768]{1,0:T(8,128)(2,1)S(1)}, bf16[192,768]{1,0:T(8,128)(2,1)S(1)}, u32[]{:S(2)}, u32[]{:S(2)}) collective-permute-start(bf16[192,768]{1,0:T(8,128)(2,1)S(1)} %get-tuple-element.219), channel_id=1, source_target_pairs={{0,2},{1,3},{2,0},{3,1},{4,6},{5,7},{6,4},{7,5},{8,10},{9,11},{10,... | collective-permute-start | bytes 884744 | tf_op jit(solution)/shard_map/ppermute | solution.py:99
  172.4 17.6 %collective-permute-start.52 = (bf16[48,3840]{1,0:T(8,128)(2,1)S(1)}, bf16[48,3840]{1,0:T(8,128)(2,1)S(1)}, u32[]{:S(2)}, u32[]{:S(2)}) collective-permute-start(bf16[48,3840]{1,0:T(8,128)(2,1)S(1)} %get-tuple-element.224), channel_id=1, source_target_pairs={{0,2},{1,3},{2,0},{3,1},{4,6},{5,7},{6,4},{7,5},{8,10},{9,11},{10,... | collective-permute-start | bytes 1105928 | tf_op jit(solution)/shard_map/ppermute | solution.py:99
  176.9 13.2 %collective-permute-start.55 = (bf16[96,2432]{1,0:T(8,128)(2,1)S(1)}, bf16[96,2432]{1,0:T(8,128)(2,1)S(1)}, u32[]{:S(2)}, u32[]{:S(2)}) collective-permute-start(bf16[96,2432]{1,0:T(8,128)(2,1)S(1)} %get-tuple-element.234), channel_id=1, source_target_pairs={{0,8},{1,9},{2,10},{3,11},{4,12},{5,13},{6,14},{7,15},{8,0},{9,1},... | collective-permute-start | bytes 1400840 | tf_op jit(solution)/shard_map/ppermute | solution.py:99
  178.0 12.1 %collective-permute-start.56 = (bf16[96,2432]{1,0:T(8,128)(2,1)S(1)}, bf16[96,2432]{1,0:T(8,128)(2,1)S(1)}, u32[]{:S(2)}, u32[]{:S(2)}) collective-permute-start(bf16[96,2432]{1,0:T(8,128)(2,1)S(1)} %get-tuple-element.235), channel_id=1, source_target_pairs={{0,16},{1,17},{2,18},{3,19},{4,20},{5,21},{6,22},{7,23},{8,24},{9,... | collective-permute-start | bytes 1400840 | tf_op jit(solution)/shard_map/ppermute | solution.py:99
  190.5 12.4 %collective-permute-start.57 = (bf16[48,2432]{1,0:T(8,128)(2,1)S(1)}, bf16[48,2432]{1,0:T(8,128)(2,1)S(1)}, u32[]{:S(2)}, u32[]{:S(2)}) collective-permute-start(bf16[48,2432]{1,0:T(8,128)(2,1)S(1)} %get-tuple-element.237), channel_id=1, source_target_pairs={{0,2},{1,3},{2,0},{3,1},{4,6},{5,7},{6,4},{7,5},{8,10},{9,11},{10,... | collective-permute-start | bytes 700424 | tf_op jit(solution)/shard_map/ppermute | solution.py:99
  191.2 11.8 %collective-permute-start.60 = (bf16[96,768]{1,0:T(8,128)(2,1)S(1)}, bf16[96,768]{1,0:T(8,128)(2,1)S(1)}, u32[]{:S(2)}, u32[]{:S(2)}) collective-permute-start(bf16[96,768]{1,0:T(8,128)(2,1)S(1)} %get-tuple-element.253), channel_id=1, source_target_pairs={{0,1},{1,0},{2,3},{3,2},{4,5},{5,4},{6,7},{7,6},{8,9},{9,8},{10,11... | collective-permute-start | bytes 442376 | tf_op jit(solution)/shard_map/ppermute | solution.py:99
  193.5 11.6 %collective-permute-start.59 = (bf16[24,3840]{1,0:T(8,128)(2,1)S(1)}, bf16[24,3840]{1,0:T(8,128)(2,1)S(1)}, u32[]{:S(2)}, u32[]{:S(2)}) collective-permute-start(bf16[24,3840]{1,0:T(8,128)(2,1)S(1)} %get-tuple-element.245), channel_id=1, source_target_pairs={{0,1},{1,0},{2,3},{3,2},{4,5},{5,4},{6,7},{7,6},{8,9},{9,8},{10,11... | collective-permute-start | bytes 552968 | tf_op jit(solution)/shard_map/ppermute | solution.py:99
  (41 other events, 335.1 us)

commit v3 on v2

--- a/solution.py
+++ b/solution.py
@@ -36,7 +36,7 @@
     "grad_inner": 3.2,
     "attend_back": 11.4,
     "plane_sum": 0.6,
-    "pair_sum": 4.0,
+    "pair_sum": 0.1,
     "stack_small": 0.1,
     "grad_first": 2.0,
     "tokens_back": 5.6,
@@ -779,20 +779,21 @@
     )
 
 
-def plane_sum_kernel(at_ref, a0, a1, a2, keep, send, total):
+def plane_sum_kernel(near, at_ref, a0, a1, a2, keep, send, total):
     total[...] = a0[...].astype(F32) + (a1[...].astype(F32) + a2[...].astype(F32))
     rows = keep.shape[0] // 2
     z = lax.rem(at_ref[0], 4)
     for m in range(4):
-        out = (keep, send)[m // 2]
+        side, place = (m % 2, m // 2) if near else (m // 2, m % 2)
+        out = (keep, send)[side]
         part = total[pl.ds(pl.multiple_of((z ^ m) * rows, 8), rows), :]
-        out[m % 2 * rows : (m % 2 + 1) * rows] = part.astype(BF16)
-
-
-def plane_sum(at, pieces):
+        out[place * rows : (place + 1) * rows] = part.astype(BF16)
+
+
+def plane_sum(at, pieces, near=False):
     part, cols = pieces[0].shape
     return call(
-        plane_sum_kernel,
+        functools.partial(plane_sum_kernel, near),
         "plane_sum",
         [at] + pieces,
         [smem()] + [vmem()] * 3,
@@ -861,9 +862,9 @@
     return [s0, swap(x, 8), swap(y, 16), x]
 
 
-def first_z(sums, *done):
+def first_z(sums, *done, near=False):
     keep, send = sums
-    return pair_sum(after(keep, *done), swap(send, 2))
+    return pair_sum(after(keep, *done), swap(send, 1 if near else 2))
 
 
 def blocked_layer(
@@ -975,15 +976,15 @@
     own_a, last_a = first_z(sums_a, tokens_grad)
     slots_c = list(slots_c)
     slots_c[3], slots_c[4], _ = lax.optimization_barrier((slots_c[3], slots_c[4], own_a))
-    sums_b = plane_sum(at, [after(plane_b[0], own_a)] + plane_b[1:3])
+    sums_b = plane_sum(at, [after(plane_b[0], own_a)] + plane_b[1:3], True)
     plane_c = scatter_plane(slots_c, sums_b[0])
     (own_u,) = finish([own_a, swap(after(last_a, sums_b[0]), 1)], [width])
-    own_b, last_b = first_z(sums_b)
-    sums_c = plane_sum(at, [after(plane_c[0], own_b)] + plane_c[1:3])
-    own_o, own_i = finish([own_b, swap(last_b, 1)], [width, hidden])
-    own_c, last_c = first_z(sums_c)
+    own_b, last_b = first_z(sums_b, near=True)
+    own_o, own_i = finish([own_b, swap(last_b, 2)], [width, hidden])
+    sums_c = plane_sum(at, [after(plane_c[0], own_o, own_u)] + plane_c[1:3], True)
+    own_c, last_c = first_z(sums_c, near=True)
     own_q, own_k, own_v, qb, vb, ob, ag, ash, ub, fg, fs, ib = finish(
-        [own_c, swap(last_c, 1)], [width] * 3, tail=True
+        [own_c, swap(last_c, 2)], [width] * 3, tail=True
     )
     return (output, tokens_grad, own_q, qb, own_k, own_v, vb, own_o, ob, ag, ash, own_i, ib, own_u, ub, fg, fs)
 

time: 209 us -> 209 us (level)
  waiting for transfers between devices: 88.9 us -> 92.5 us
  starting transfers between devices: 46.2 us -> 42.7 us
    ppermute x61, waiting for transfers between devices: 88.9 us -> 92.5 us  [swap(): return lax.ppermute(value, AXES, [(i, i ^ mask) for i in range(32)])]
    ppermute x61, starting transfers between devices: 46.2 us -> 42.7 us  [swap(): return lax.ppermute(value, AXES, [(i, i ^ mask) for i in range(32)])]
  transfers between devices with their start and end apart: 61 -> 61, of which waited for: 27 -> 28; matrix products, arithmetic and copies ran while one was open for 0% -> 0% of each run, Pallas kernels for 30% -> 30%
where the time goes in v3:
time: 209 us
  waiting for transfers between devices  92.5 us (44%)
  Pallas kernels  71.4 us (34%)
  starting transfers between devices  42.7 us (20%)
    ppermute x61, waiting for transfers between devices, swap(): return lax.ppermute(value, AXES, [(i, i ^ mask) for i in range(32)])  92.5 us
    pallas_call x32, Pallas kernels, call(): pl.pallas_call(kernel, out_shape=out_shape, name=name, input_output_alias...  71.4 us
    ppermute x61, starting transfers between devices, swap(): return lax.ppermute(value, AXES, [(i, i ^ mask) for i in range(32)])  42.7 us
  transfers between devices with their start and end apart: 61, of which 28 were waited for; matrix products, arithmetic and copies ran while one was open for 0% of the time, Pallas kernels for 30%

profile of v3, /device:TPU:0, one launch (start us, length us, event | category | flops | bytes accessed | tf_op | source)
XLA Modules:
  0.0 208.8 jit_solution(11211148620276057840)
XLA Ops:
  2.0 5.1 %collective-permute-start.2 = (bf16[24,3200]{1,0:T(8,128)(2,1)S(1)}, bf16[24,3200]{1,0:T(8,128)(2,1)S(1)}, u32[]{:S(2)}, u32[]{:S(2)}) collective-permute-start(bf16[24,3200]{1,0:T(8,128)(2,1)S(1)} %get-tuple-element.137.a0), channel_id=1, source_target_pairs={{0,3},{1,2},{2,1},{3,0},{4,7},{5,6},{6,5},{7,4},{8,11},{9,10},{10,... | collective-permute-start | bytes 460808 | tf_op jit(solution)/shard_map/ppermute | solution.py:99
  7.7 4.3 %collective-permute-done.2.a3 = bf16[24,3200]{1,0:T(8,128)(2,1)S(1)} collective-permute-done((bf16[24,3200]{1,0:T(8,128)(2,1)S(1)}, bf16[24,3200]{1,0:T(8,128)(2,1)S(1)}, u32[]{:S(2)}, u32[]{:S(2)}) %collective-permute-start.2) | collective-permute-done | bytes 153632 | tf_op jit(solution)/shard_map/ppermute | solution.py:99
  12.0 8.1 %collective-permute-done.1.a2 = bf16[24,3200]{1,0:T(8,128)(2,1)S(1)} collective-permute-done((bf16[24,3200]{1,0:T(8,128)(2,1)S(1)}, bf16[24,3200]{1,0:T(8,128)(2,1)S(1)}, u32[]{:S(2)}, u32[]{:S(2)}) %collective-permute-start.1) | collective-permute-done | bytes 153632 | tf_op jit(solution)/shard_map/ppermute | solution.py:99
  20.2 1.6 collective-permute-start.7
  23.3 11.9 %collective-permute-done.7.refs_4_.refs_5_ = bf16[96,3200]{1,0:T(8,128)(2,1)S(1)} collective-permute-done((bf16[96,3200]{1,0:T(8,128)(2,1)S(1)}, bf16[96,3200]{1,0:T(8,128)(2,1)S(1)}, u32[]{:S(2)}, u32[]{:S(2)}) %collective-permute-start.7) | collective-permute-done | bytes 614432 | tf_op jit(solution)/shard_map/ppermute | solution.py:99
  36.8 1.6 collective-permute-start.9
  38.4 4.8 %collective-permute-done.10.refs_7_.refs_8_ = bf16[96,1664]{1,0:T(8,128)(2,1)S(1)} collective-permute-done((bf16[96,1664]{1,0:T(8,128)(2,1)S(1)}, bf16[96,1664]{1,0:T(8,128)(2,1)S(1)}, u32[]{:S(2)}, u32[]{:S(2)}) %collective-permute-start.10) | collective-permute-done | bytes 319520 | tf_op jit(solution)/shard_map/ppermute | solution.py:99
  49.4 3.3 %project.1 = (bf16[512,768]{1,0:T(8,128)(2,1)S(1)}, bf16[512,768]{1,0:T(8,128)(2,1)S(1)}, bf16[512,768]{1,0:T(8,128)(2,1)S(1)}, f32[16,768]{1,0:T(8,128)S(1)}, f...) custom-call(s32[1]{0:T(128)} %bitcast.at_ref.refs_4_, bf16[512,768]{1,0:T(8,128)(2,1)S(1)} %copy-done.3, ...), custom_call_target="tpu_custom_call" | custom-call | flops 825000000 | tf_op jit(solution)/shard_map/project/pallas_call | solution.py:87
  52.8 8.4 %attend.1 = (bf16[512,768]{1,0:T(8,128)(2,1)S(1)}, bf16[768,512]{1,0:T(8,128)(2,1)S(1)}, f32[6,2,512]{2,1,0:T(2,128)S(1)}) custom-call(s32[1]{0:T(128)S(6)} %copy.43.len_ref, bf16[512,768]{1,0:T(8,128)(2,1)S(1)} %get-tuple-element.141.q_ref, bf16[512,768]{1,0:T(8,128)(2,1)S(1)} %get-tuple-element.142.k_ref, bf16[512,768]{1,0:T(8,128)(2,1)S(1)} %get-tuple-element.143.v_ref), custom_call_target="tpu_custom_call" | custom-call | flops 1100000000 | tf_op jit(solution)/shard_map/attend/pallas_call | solution.py:87
  65.5 5.1 %collective-permute-done.20.refs_7_ = bf16[96,1536]{1,0:T(8,128)(2,1)S(1)} collective-permute-done((bf16[96,1536]{1,0:T(8,128)(2,1)S(1)}, bf16[96,1536]{1,0:T(8,128)(2,1)S(1)}, u32[]{:S(2)}, u32[]{:S(2)}) %collective-permute-start.20) | collective-permute-done | bytes 294944 | tf_op jit(solution)/shard_map/ppermute | solution.py:99
  70.5 2.1 %collective-permute-done.19.refs_6_ = bf16[96,1536]{1,0:T(8,128)(2,1)S(1)} collective-permute-done((bf16[96,1536]{1,0:T(8,128)(2,1)S(1)}, bf16[96,1536]{1,0:T(8,128)(2,1)S(1)}, u32[]{:S(2)}, u32[]{:S(2)}) %collective-permute-start.19) | collective-permute-done | bytes 294944 | tf_op jit(solution)/shard_map/ppermute | solution.py:99
  75.5 3.0 %mix.1 = (f32[512,768]{1,0:T(8,128)S(1)}, f32[512,128]{1,0:T(8,128)S(1)}, bf16[512,768]{1,0:T(8,128)(2,1)S(1)}, bf16[2,4,96,512]{3,2,1,0:T(8,128)(2,1)S(1)}, bf16[2,4,96,512]{3,2,1,0:T(8,128)(2,1)S(1)}) custom-call(s32[1]{0:T(128)} %bitcast.at_ref.refs_4_, bf16[512,768]{1,0:T(8,128)(2,1)S(1)} %copy-done.3, bf16[512,768]{1,0:T(8,128)(2,1)S(1)} %get-tuple-element.151.mixed, ...), custom_call_target="tpu_custom_call" | custom-call | flops 1650000000 | tf_op jit(solution)/shard_map/mix/pallas_call | solution.py:87
  78.5 8.8 %inner.1 = (bf16[512,3072]{1,0:T(8,128)(2,1)S(1)}, bf16[512,3072]{1,0:T(8,128)(2,1)S(1)}, bf16[768,3072]{1,0:T(8,128)(2,1)S(1)}, bf16[4,384,512]{2,1,0:T(8,128)(2,1)S(1)}, bf16[4,384,512]{2,1,0:T(8,128)(2,1)S(1)}) custom-call(s32[1]{0:T(128)} %bitcast.at_ref.refs_4_, bf16[512,768]{1,0:T(8,128)(2,1)S(1)} %get-tuple-element.160.values, ...), custom_call_target="tpu_custom_call" | custom-call | flops 4950000128 | tf_op jit(solution)/shard_map/inner/pallas_call | solution.py:87
  87.3 1.8 collective-permute-done.27.refs_4_
  92.7 6.8 %collective-permute-done.32.refs_6_ = bf16[384,384]{1,0:T(8,128)(2,1)S(1)} collective-permute-done((bf16[384,384]{1,0:T(8,128)(2,1)S(1)}, bf16[384,384]{1,0:T(8,128)(2,1)S(1)}, u32[]{:S(2)}, u32[]{:S(2)}) %collective-permute-start.32) | collective-permute-done | bytes 294944 | tf_op jit(solution)/shard_map/ppermute | solution.py:99
  102.4 6.1 %outer.1 = (bf16[512,768]{1,0:T(8,128)(2,1)}, f32[512,768]{1,0:T(8,128)S(1)}, bf16[512,768]{1,0:T(8,128)(2,1)S(1)}, f32[8,768]{1,0:T(8,128)S(1)}) custom-call(s32[1]{0:T(128)} %bitcast.at_ref.refs_4_, s32[1]{0:T(128)S(6)} %copy.43.len_ref, bf16[512,3072]{1,0:T(8,128)(2,1)S(1)} %get-tuple-element.167.activ, bf16[512,768]{1,0:T(8,128)(2,1)S(1)} %get-tuple-element.160.values, ...), custom_call_target="tpu_custom_call" | custom-call | flops 3300000000 | tf_op jit(solution)/shard_map/outer/pallas_call | solution.py:87
  108.6 3.7 %slope.1 = (bf16[512,3072]{1,0:T(8,128)(2,1)S(1)}, f32[1,3072]{1,0:T(1,128)S(1)}) custom-call(s32[1]{0:T(128)} %bitcast.at_ref.refs_4_, bf16[512,768]{1,0:T(8,128)(2,1)S(1)} %get-tuple-element.170.outer_grad.refs_2_, bf16[512,3072]{1,0:T(8,128)(2,1)S(1)} %get-tuple-element.171.slope, bf16[384,768]{1,0:T(8,128)(2,1)S(1)} %z_join.9.refs_0_, ...), custom_call_target="tpu_custom_call" | custom-call | flops 2035000064 | tf_op jit(solution)/shard_map/slope/pallas_call | solution.py:87
  112.9 2.6 %grad_outer.1 = (bf16[384,768]{1,0:T(8,128)(2,1)S(1)}, bf16[384,768]{1,0:T(8,128)(2,1)S(1)}, bf16[384,768]{1,0:T(8,128)(2,1)S(1)}, bf16[384,384]{1,0:T(8,128)(2,1)S(1)}, bf16[384,384]{1,0:T(8,128)(2,1)S(1)}) custom-call(bf16[4,384,512]{2,1,0:T(8,128)(2,1)S(1)} %get-tuple-element.173.refs_0_, bf16[4,384,512]{2,1,0:T(8,128)(2,1)S(1)} %collective-permute-done.28.refs_1_, ...), custom_call_target="tpu_custom_call" | custom-call | flops 1430000000 | tf_op jit(solution)/shard_map/grad_outer/pallas_call | solution.py:87
  117.6 6.6 %normed_back.1 = (f32[512,768]{1,0:T(8,128)S(1)}, bf16[512,384]{1,0:T(8,128)(2,1)S(1)}, bf16[512,384]{1,0:T(8,128)(2,1)S(1)}, bf16[512,768]{1,0:T(8,128)(2,1)S(1)}, f32[8,768]{1,0:T(8,128)S(1)}) custom-call(bf16[512,3072]{1,0:T(8,128)(2,1)S(1)} %get-tuple-element.196.inner_grad.refs_6_, f32[512,768]{1,0:T(8,128)S(1)} %get-tuple-element.177.resid_two, ...), custom_call_target="tpu_custom_call" | custom-call | flops 2750000128 | tf_op jit(solution)/shard_map/normed_back/pallas_call | solution.py:87
  128.6 3.5 %grad_inner.1 = (bf16[96,3840]{1,0:T(8,128)(2,1)S(1)}, bf16[96,3840]{1,0:T(8,128)(2,1)S(1)}, bf16[96,3840]{1,0:T(8,128)(2,1)S(1)}, bf16[96,1920]{1,0:T(8,128)(2,1)S(1)}, bf16[96,1920]{1,0:T(8,128)(2,1)S(1)}) custom-call(bf16[2,4,96,512]{3,2,1,0:T(8,128)(2,1)S(1)} %get-tuple-element.184.refs_0_, bf16[2,4,96,512]{3,2,1,0:T(8,128)(2,1)S(1)} %collective-permute-done.37.refs_1_, ...), custom_call_target="tpu_custom_call" | custom-call | flops 1760000000 | tf_op jit(solution)/shard_map/grad_inner/pallas_call | solution.py:87
  134.1 11.5 %attend_back.1 = (bf16[3,512,768]{2,1,0:T(8,128)(2,1)S(1)}, f32[1,768]{1,0:T(1,128)S(1)}, f32[1,768]{1,0:T(1,128)S(1)}) custom-call(s32[1]{0:T(128)S(6)} %copy.43.len_ref, bf16[512,768]{1,0:T(8,128)(2,1)S(1)} %get-tuple-element.141.q_ref, bf16[512,768]{1,0:T(8,128)(2,1)S(1)} %get-tuple-element.142.k_ref, bf16[512,768]{1,0:T(8,128)(2,1)S(1)} %get-tuple-element.143.v_ref, ...), custom_call_target="tpu_custom_call" | custom-call | flops 6270000128 | tf_op jit(solution)/shard_map/attend_back/pallas_call | solution.py:87
  145.6 4.9 %collective-permute-done.43.p_ref = bf16[96,1920]{1,0:T(8,128)(2,1)S(1)} collective-permute-done((bf16[96,1920]{1,0:T(8,128)(2,1)S(1)}, bf16[96,1920]{1,0:T(8,128)(2,1)S(1)}, u32[]{:S(2)}, u32[]{:S(2)}) %collective-permute-start.43) | collective-permute-done | bytes 368672 | tf_op jit(solution)/shard_map/ppermute | solution.py:99
  153.6 1.9 collective-permute-start.49
  156.0 2.0 grad_first.1
  158.0 5.4 %tokens_back.1 = bf16[512,768]{1,0:T(8,128)(2,1)} custom-call(s32[1]{0:T(128)} %bitcast.at_ref.refs_4_, f32[512,768]{1,0:T(8,128)S(1)} %get-tuple-element.217.resid_grad, bf16[3,512,768]{2,1,0:T(8,128)(2,1)S(1)} %get-tuple-element.210.refs_2_.refs_0_, bf16[96,3200]{1,0:T(8,128)(2,1)} %copy-done, bf16[96,3200]{1,0:T(8,128)(2,1)} %copy-done.4, ...), custom_call_target="tpu_custom_call" | custom-call | flops 3080000000 | tf_op jit(solution)/shard_map/tokens_back/pallas_call | solution.py:87
  163.4 6.9 %collective-permute-done.49.came = bf16[192,768]{1,0:T(8,128)(2,1)S(1)} collective-permute-done((bf16[192,768]{1,0:T(8,128)(2,1)S(1)}, bf16[192,768]{1,0:T(8,128)(2,1)S(1)}, u32[]{:S(2)}, u32[]{:S(2)}) %collective-permute-start.49) | collective-permute-done | bytes 294944 | tf_op jit(solution)/shard_map/ppermute | solution.py:99
  174.2 3.9 %collective-permute-done.55.p_ref = bf16[96,1152]{1,0:T(8,128)(2,1)S(1)} collective-permute-done((bf16[96,1152]{1,0:T(8,128)(2,1)S(1)}, bf16[96,1152]{1,0:T(8,128)(2,1)S(1)}, u32[]{:S(2)}, u32[]{:S(2)}) %collective-permute-start.55) | collective-permute-done | bytes 221216 | tf_op jit(solution)/shard_map/ppermute | solution.py:99
  180.4 3.8 %collective-permute-done.52.came = bf16[48,3840]{1,0:T(8,128)(2,1)S(1)} collective-permute-done((bf16[48,3840]{1,0:T(8,128)(2,1)S(1)}, bf16[48,3840]{1,0:T(8,128)(2,1)S(1)}, u32[]{:S(2)}, u32[]{:S(2)}) %collective-permute-start.52) | collective-permute-done | bytes 368672 | tf_op jit(solution)/shard_map/ppermute | solution.py:99
  185.2 2.0 collective-permute-done.54.came
  188.0 4.9 %collective-permute-done.53.came = bf16[24,3840]{1,0:T(8,128)(2,1)S(1)} collective-permute-done((bf16[24,3840]{1,0:T(8,128)(2,1)S(1)}, bf16[24,3840]{1,0:T(8,128)(2,1)S(1)}, u32[]{:S(2)}, u32[]{:S(2)}) %collective-permute-start.53) | collective-permute-done | bytes 184352 | tf_op jit(solution)/shard_map/ppermute | solution.py:99
  194.1 7.3 %collective-permute-done.59.came = bf16[48,2432]{1,0:T(8,128)(2,1)S(1)} collective-permute-done((bf16[48,2432]{1,0:T(8,128)(2,1)S(1)}, bf16[48,2432]{1,0:T(8,128)(2,1)S(1)}, u32[]{:S(2)}, u32[]{:S(2)}) %collective-permute-start.59) | collective-permute-done | bytes 233504 | tf_op jit(solution)/shard_map/ppermute | solution.py:99
  201.7 6.1 %collective-permute-done.60.came = bf16[24,2432]{1,0:T(8,128)(2,1)S(1)} collective-permute-done((bf16[24,2432]{1,0:T(8,128)(2,1)S(1)}, bf16[24,2432]{1,0:T(8,128)(2,1)S(1)}, u32[]{:S(2)}, u32[]{:S(2)}) %collective-permute-start.60) | collective-permute-done | bytes 116768 | tf_op jit(solution)/shard_map/ppermute | solution.py:99
  (152 shorter events, 47.2 us)
Async XLA Ops:
  2.0 10.0 %collective-permute-start.2 = (bf16[24,3200]{1,0:T(8,128)(2,1)S(1)}, bf16[24,3200]{1,0:T(8,128)(2,1)S(1)}, u32[]{:S(2)}, u32[]{:S(2)}) collective-permute-start(bf16[24,3200]{1,0:T(8,128)(2,1)S(1)} %get-tuple-element.137.a0), channel_id=1, source_target_pairs={{0,3},{1,2},{2,1},{3,0},{4,7},{5,6},{6,5},{7,4},{8,11},{9,10},{10,... | collective-permute-start | bytes 460808 | tf_op jit(solution)/shard_map/ppermute | solution.py:99
  7.1 13.0 %collective-permute-start.1 = (bf16[24,3200]{1,0:T(8,128)(2,1)S(1)}, bf16[24,3200]{1,0:T(8,128)(2,1)S(1)}, u32[]{:S(2)}, u32[]{:S(2)}) collective-permute-start(bf16[24,3200]{1,0:T(8,128)(2,1)S(1)} %get-tuple-element.137.a0), channel_id=1, source_target_pairs={{0,2},{1,3},{2,0},{3,1},{4,6},{5,7},{6,4},{7,5},{8,10},{9,11},{10,... | collective-permute-start | bytes 460808 | tf_op jit(solution)/shard_map/ppermute | solution.py:99
  7.1 13.0 %collective-permute-start = (bf16[24,3200]{1,0:T(8,128)(2,1)S(1)}, bf16[24,3200]{1,0:T(8,128)(2,1)S(1)}, u32[]{:S(2)}, u32[]{:S(2)}) collective-permute-start(bf16[24,3200]{1,0:T(8,128)(2,1)S(1)} %get-tuple-element.137.a0), channel_id=1, source_target_pairs={{0,1},{1,0},{2,3},{3,2},{4,5},{5,4},{6,7},{7,6},{8,9},{9,8},{10,11... | collective-permute-start | bytes 460808 | tf_op jit(solution)/shard_map/ppermute | solution.py:99
  20.2 15.0 %collective-permute-start.7 = (bf16[96,3200]{1,0:T(8,128)(2,1)S(1)}, bf16[96,3200]{1,0:T(8,128)(2,1)S(1)}, u32[]{:S(2)}, u32[]{:S(2)}) collective-permute-start(bf16[96,3200]{1,0:T(8,128)(2,1)S(1)} %z_join.5.refs_0_.refs_1_), channel_id=1, source_target_pairs={{0,16},{1,17},{2,18},{3,19},{4,20},{5,21},{6,22},{7,23},{8,24},{9,... | collective-permute-start | bytes 1843208 | tf_op jit(solution)/shard_map/ppermute | solution.py:99
  21.8 15.0 %collective-permute-start.4 = (bf16[96,3200]{1,0:T(8,128)(2,1)S(1)}, bf16[96,3200]{1,0:T(8,128)(2,1)S(1)}, u32[]{:S(2)}, u32[]{:S(2)}) collective-permute-start(bf16[96,3200]{1,0:T(8,128)(2,1)S(1)} %z_join.5.refs_0_.refs_1_), channel_id=1, source_target_pairs={{0,8},{1,9},{2,10},{3,11},{4,12},{5,13},{6,14},{7,15},{8,0},{9,1},... | collective-permute-start | bytes 1843208 | tf_op jit(solution)/shard_map/ppermute | solution.py:99
  23.3 13.5 %collective-permute-start.5 = (bf16[24,3072]{1,0:T(8,128)(2,1)S(1)}, bf16[24,3072]{1,0:T(8,128)(2,1)S(1)}, u32[]{:S(2)}, u32[]{:S(2)}) collective-permute-start(bf16[24,3072]{1,0:T(8,128)(2,1)S(1)} %get-tuple-element.139.a0), channel_id=1, source_target_pairs={{0,2},{1,3},{2,0},{3,1},{4,6},{5,7},{6,4},{7,5},{8,10},{9,11},{10,... | collective-permute-start | bytes 442376 | tf_op jit(solution)/shard_map/ppermute | solution.py:99
  45.3 15.9 %collective-permute-start.15 = (bf16[96,3072]{1,0:T(8,128)(2,1)S(1)}, bf16[96,3072]{1,0:T(8,128)(2,1)S(1)}, u32[]{:S(2)}, u32[]{:S(2)}) collective-permute-start(bf16[96,3072]{1,0:T(8,128)(2,1)S(1)} %z_join.7.refs_0_), channel_id=1, source_target_pairs={{0,16},{1,17},{2,18},{3,19},{4,20},{5,21},{6,22},{7,23},{8,24},{9,... | collective-permute-start | bytes 1769480 | tf_op jit(solution)/shard_map/ppermute | solution.py:99
  46.9 15.1 %collective-permute-start.14 = (bf16[96,3072]{1,0:T(8,128)(2,1)S(1)}, bf16[96,3072]{1,0:T(8,128)(2,1)S(1)}, u32[]{:S(2)}, u32[]{:S(2)}) collective-permute-start(bf16[96,3072]{1,0:T(8,128)(2,1)S(1)} %z_join.7.refs_0_), channel_id=1, source_target_pairs={{0,8},{1,9},{2,10},{3,11},{4,12},{5,13},{6,14},{7,15},{8,0},{9,1},... | collective-permute-start | bytes 1769480 | tf_op jit(solution)/shard_map/ppermute | solution.py:99
  49.1 16.4 %collective-permute-start.17 = (bf16[4,96,512]{2,1,0:T(8,128)(2,1)S(1)}, bf16[4,96,512]{2,1,0:T(8,128)(2,1)S(1)}, u32[]{:S(2)}, u32[]{:S(2)}) collective-permute-start(bf16[4,96,512]{2,1,0:T(8,128)(2,1)S(1)} %get-tuple-element.150), channel_id=1, source_target_pairs={{0,4},{1,5},{2,6},{3,7},{4,0},{5,1},{6,2},{7,3},{8,12},{9,13},{10,... | collective-permute-start | bytes 1179656 | tf_op jit(solution)/shard_map/ppermute | solution.py:99
  49.2 12.0 %collective-permute-start.16 = (bf16[96,768]{1,0:T(8,128)(2,1)S(1)}, bf16[96,768]{1,0:T(8,128)(2,1)S(1)}, u32[]{:S(2)}, u32[]{:S(2)}) collective-permute-start(bf16[96,768]{1,0:T(8,128)(2,1)S(1)} %get-tuple-element.147.a0), channel_id=1, source_target_pairs={{0,2},{1,3},{2,0},{3,1},{4,6},{5,7},{6,4},{7,5},{8,10},{9,11},{10,... | collective-permute-start | bytes 442376 | tf_op jit(solution)/shard_map/ppermute | solution.py:99
  63.2 10.1 %collective-permute-start.21 = (bf16[96,3072]{1,0:T(8,128)(2,1)S(1)}, bf16[96,3072]{1,0:T(8,128)(2,1)S(1)}, u32[]{:S(2)}, u32[]{:S(2)}) collective-permute-start(bf16[96,3072]{1,0:T(8,128)(2,1)S(1)} %z_join.7.refs_0_), channel_id=1, source_target_pairs={{0,4},{1,5},{2,6},{3,7},{4,0},{5,1},{6,2},{7,3},{8,12},{9,13},{10,... | collective-permute-start | bytes 1769480 | tf_op jit(solution)/shard_map/ppermute | solution.py:99
  63.2 9.5 %collective-permute-start.19 = (bf16[96,1536]{1,0:T(8,128)(2,1)S(1)}, bf16[96,1536]{1,0:T(8,128)(2,1)S(1)}, u32[]{:S(2)}, u32[]{:S(2)}) collective-permute-start(bf16[96,1536]{1,0:T(8,128)(2,1)S(1)} %slice.20), channel_id=1, source_target_pairs={{0,16},{1,17},{2,18},{3,19},{4,20},{5,21},{6,22},{7,23},{8,24},{9,... | collective-permute-start | bytes 884744 | tf_op jit(solution)/shard_map/ppermute | solution.py:99
  65.5 13.0 %collective-permute-start.22 = (bf16[96,3072]{1,0:T(8,128)(2,1)S(1)}, bf16[96,3072]{1,0:T(8,128)(2,1)S(1)}, u32[]{:S(2)}, u32[]{:S(2)}) collective-permute-start(bf16[96,3072]{1,0:T(8,128)(2,1)S(1)} %collective-permute-done.14.refs_2_), channel_id=1, source_target_pairs={{0,4},{1,5},{2,6},{3,7},{4,0},{5,1},{6,2},{7,3},{8,12},{9,13},{10,... | collective-permute-start | bytes 1769480 | tf_op jit(solution)/shard_map/ppermute | solution.py:99
  73.3 15.8 %collective-permute-start.27 = (bf16[384,768]{1,0:T(8,128)(2,1)S(1)}, bf16[384,768]{1,0:T(8,128)(2,1)S(1)}, u32[]{:S(2)}, u32[]{:S(2)}) collective-permute-start(bf16[384,768]{1,0:T(8,128)(2,1)S(1)} %z_join.9.refs_0_), channel_id=1, source_target_pairs={{0,16},{1,17},{2,18},{3,19},{4,20},{5,21},{6,22},{7,23},{8,24},{9,... | collective-permute-start | bytes 1769480 | tf_op jit(solution)/shard_map/ppermute | solution.py:99
  74.5 15.5 %collective-permute-start.26 = (bf16[384,768]{1,0:T(8,128)(2,1)S(1)}, bf16[384,768]{1,0:T(8,128)(2,1)S(1)}, u32[]{:S(2)}, u32[]{:S(2)}) collective-permute-start(bf16[384,768]{1,0:T(8,128)(2,1)S(1)} %z_join.9.refs_0_), channel_id=1, source_target_pairs={{0,8},{1,9},{2,10},{3,11},{4,12},{5,13},{6,14},{7,15},{8,0},{9,1},... | collective-permute-start | bytes 1769480 | tf_op jit(solution)/shard_map/ppermute | solution.py:99
  90.0 10.2 %collective-permute-start.28 = (bf16[4,384,512]{2,1,0:T(8,128)(2,1)S(1)}, bf16[4,384,512]{2,1,0:T(8,128)(2,1)S(1)}, u32[]{:S(2)}, u32[]{:S(2)}) collective-permute-start(bf16[4,384,512]{2,1,0:T(8,128)(2,1)S(1)} %get-tuple-element.166), channel_id=1, source_target_pairs={{0,4},{1,5},{2,6},{3,7},{4,0},{5,1},{6,2},{7,3},{8,12},{9,13},{10,... | collective-permute-start | bytes 4718600 | tf_op jit(solution)/shard_map/ppermute | solution.py:99
  90.0 9.5 %collective-permute-start.32 = (bf16[384,384]{1,0:T(8,128)(2,1)S(1)}, bf16[384,384]{1,0:T(8,128)(2,1)S(1)}, u32[]{:S(2)}, u32[]{:S(2)}) collective-permute-start(bf16[384,384]{1,0:T(8,128)(2,1)S(1)} %slice.22), channel_id=1, source_target_pairs={{0,16},{1,17},{2,18},{3,19},{4,20},{5,21},{6,22},{7,23},{8,24},{9,... | collective-permute-start | bytes 884744 | tf_op jit(solution)/shard_map/ppermute | solution.py:99
  91.0 9.2 %collective-permute-start.33 = (bf16[384,384]{1,0:T(8,128)(2,1)S(1)}, bf16[384,384]{1,0:T(8,128)(2,1)S(1)}, u32[]{:S(2)}, u32[]{:S(2)}) collective-permute-start(bf16[384,384]{1,0:T(8,128)(2,1)S(1)} %slice.23), channel_id=1, source_target_pairs={{0,8},{1,9},{2,10},{3,11},{4,12},{5,13},{6,14},{7,15},{8,0},{9,1},... | collective-permute-start | bytes 884744 | tf_op jit(solution)/shard_map/ppermute | solution.py:99
  92.2 10.2 %collective-permute-start.31 = (bf16[384,768]{1,0:T(8,128)(2,1)S(1)}, bf16[384,768]{1,0:T(8,128)(2,1)S(1)}, u32[]{:S(2)}, u32[]{:S(2)}) collective-permute-start(bf16[384,768]{1,0:T(8,128)(2,1)S(1)} %collective-permute-done.27.refs_4_), channel_id=1, source_target_pairs={{0,4},{1,5},{2,6},{3,7},{4,0},{5,1},{6,2},{7,3},{8,12},{9,13},{10,... | collective-permute-start | bytes 1769480 | tf_op jit(solution)/shard_map/ppermute | solution.py:99
  112.3 16.2 %collective-permute-start.42 = (bf16[512,3072]{1,0:T(8,128)(2,1)S(1)}, bf16[512,3072]{1,0:T(8,128)(2,1)S(1)}, u32[]{:S(2)}, u32[]{:S(2)}) collective-permute-start(bf16[512,3072]{1,0:T(8,128)(2,1)S(1)} %get-tuple-element.196.inner_grad.refs_6_), channel_id=1, source_target_pairs={{0,4},{1,5},{2,6},{3,7},{4,0},{5,1},{6,2},{7,3},{8,12},{9,13},{10,... | collective-permute-start | bytes 9437192 | tf_op jit(solution)/shard_map/ppermute | solution.py:99
  112.8 14.7 %collective-permute-start.37 = (bf16[2,4,96,512]{3,2,1,0:T(8,128)(2,1)S(1)}, bf16[2,4,96,512]{3,2,1,0:T(8,128)(2,1)S(1)}, u32[]{:S(2)}, u32[]{:S(2)}) collective-permute-start(bf16[2,4,96,512]{3,2,1,0:T(8,128)(2,1)S(1)} %get-tuple-element.185), channel_id=1, source_target_pairs={{0,4},{1,5},{2,6},{3,7},{4,0},{5,1},{6,2},{7,3},{8,12},{9,13},{10,... | collective-permute-start | bytes 2359304 | tf_op jit(solution)/shard_map/ppermute | solution.py:99
  115.6 9.3 %collective-permute-start.38 = (bf16[384,384]{1,0:T(8,128)(2,1)S(1)}, bf16[384,384]{1,0:T(8,128)(2,1)S(1)}, u32[]{:S(2)}, u32[]{:S(2)}) collective-permute-start(bf16[384,384]{1,0:T(8,128)(2,1)S(1)} %get-tuple-element.189), channel_id=1, source_target_pairs={{0,16},{1,17},{2,18},{3,19},{4,20},{5,21},{6,22},{7,23},{8,24},{9,... | collective-permute-start | bytes 884744 | tf_op jit(solution)/shard_map/ppermute | solution.py:99
  126.5 24.3 %collective-permute-start.45 = (bf16[384,768]{1,0:T(8,128)(2,1)S(1)}, bf16[384,768]{1,0:T(8,128)(2,1)S(1)}, u32[]{:S(2)}, u32[]{:S(2)}) collective-permute-start(bf16[384,768]{1,0:T(8,128)(2,1)S(1)} %get-tuple-element.192), channel_id=1, source_target_pairs={{0,8},{1,9},{2,10},{3,11},{4,12},{5,13},{6,14},{7,15},{8,0},{9,1},... | collective-permute-start | bytes 1769480 | tf_op jit(solution)/shard_map/ppermute | solution.py:99
  127.5 23.3 %collective-permute-start.46 = (bf16[384,768]{1,0:T(8,128)(2,1)S(1)}, bf16[384,768]{1,0:T(8,128)(2,1)S(1)}, u32[]{:S(2)}, u32[]{:S(2)}) collective-permute-start(bf16[384,768]{1,0:T(8,128)(2,1)S(1)} %get-tuple-element.208), channel_id=1, source_target_pairs={{0,16},{1,17},{2,18},{3,19},{4,20},{5,21},{6,22},{7,23},{8,24},{9,... | collective-permute-start | bytes 1769480 | tf_op jit(solution)/shard_map/ppermute | solution.py:99
  132.0 18.4 %collective-permute-start.43 = (bf16[96,1920]{1,0:T(8,128)(2,1)S(1)}, bf16[96,1920]{1,0:T(8,128)(2,1)S(1)}, u32[]{:S(2)}, u32[]{:S(2)}) collective-permute-start(bf16[96,1920]{1,0:T(8,128)(2,1)S(1)} %get-tuple-element.203), channel_id=1, source_target_pairs={{0,16},{1,17},{2,18},{3,19},{4,20},{5,21},{6,22},{7,23},{8,24},{9,... | collective-permute-start | bytes 1105928 | tf_op jit(solution)/shard_map/ppermute | solution.py:99
  133.1 17.4 %collective-permute-start.44 = (bf16[96,1920]{1,0:T(8,128)(2,1)S(1)}, bf16[96,1920]{1,0:T(8,128)(2,1)S(1)}, u32[]{:S(2)}, u32[]{:S(2)}) collective-permute-start(bf16[96,1920]{1,0:T(8,128)(2,1)S(1)} %get-tuple-element.205), channel_id=1, source_target_pairs={{0,8},{1,9},{2,10},{3,11},{4,12},{5,13},{6,14},{7,15},{8,0},{9,1},... | collective-permute-start | bytes 1105928 | tf_op jit(solution)/shard_map/ppermute | solution.py:99
  151.4 21.0 %collective-permute-start.51 = (bf16[96,3840]{1,0:T(8,128)(2,1)S(1)}, bf16[96,3840]{1,0:T(8,128)(2,1)S(1)}, u32[]{:S(2)}, u32[]{:S(2)}) collective-permute-start(bf16[96,3840]{1,0:T(8,128)(2,1)S(1)} %get-tuple-element.222), channel_id=1, source_target_pairs={{0,16},{1,17},{2,18},{3,19},{4,20},{5,21},{6,22},{7,23},{8,24},{9,... | collective-permute-start | bytes 2211848 | tf_op jit(solution)/shard_map/ppermute | solution.py:99
  152.5 19.9 %collective-permute-start.50 = (bf16[96,3840]{1,0:T(8,128)(2,1)S(1)}, bf16[96,3840]{1,0:T(8,128)(2,1)S(1)}, u32[]{:S(2)}, u32[]{:S(2)}) collective-permute-start(bf16[96,3840]{1,0:T(8,128)(2,1)S(1)} %get-tuple-element.206), channel_id=1, source_target_pairs={{0,8},{1,9},{2,10},{3,11},{4,12},{5,13},{6,14},{7,15},{8,0},{9,1},... | collective-permute-start | bytes 2211848 | tf_op jit(solution)/shard_map/ppermute | solution.py:99
  153.6 16.6 %collective-permute-start.49 = (bf16[192,768]{1,0:T(8,128)(2,1)S(1)}, bf16[192,768]{1,0:T(8,128)(2,1)S(1)}, u32[]{:S(2)}, u32[]{:S(2)}) collective-permute-start(bf16[192,768]{1,0:T(8,128)(2,1)S(1)} %get-tuple-element.219), channel_id=1, source_target_pairs={{0,2},{1,3},{2,0},{3,1},{4,6},{5,7},{6,4},{7,5},{8,10},{9,11},{10,... | collective-permute-start | bytes 884744 | tf_op jit(solution)/shard_map/ppermute | solution.py:99
  173.0 11.2 %collective-permute-start.52 = (bf16[48,3840]{1,0:T(8,128)(2,1)S(1)}, bf16[48,3840]{1,0:T(8,128)(2,1)S(1)}, u32[]{:S(2)}, u32[]{:S(2)}) collective-permute-start(bf16[48,3840]{1,0:T(8,128)(2,1)S(1)} %get-tuple-element.224), channel_id=1, source_target_pairs={{0,1},{1,0},{2,3},{3,2},{4,5},{5,4},{6,7},{7,6},{8,9},{9,8},{10,11... | collective-permute-start | bytes 1105928 | tf_op jit(solution)/shard_map/ppermute | solution.py:99
  178.3 15.4 %collective-permute-start.57 = (bf16[96,2432]{1,0:T(8,128)(2,1)S(1)}, bf16[96,2432]{1,0:T(8,128)(2,1)S(1)}, u32[]{:S(2)}, u32[]{:S(2)}) collective-permute-start(bf16[96,2432]{1,0:T(8,128)(2,1)S(1)} %get-tuple-element.238), channel_id=1, source_target_pairs={{0,8},{1,9},{2,10},{3,11},{4,12},{5,13},{6,14},{7,15},{8,0},{9,1},... | collective-permute-start | bytes 1400840 | tf_op jit(solution)/shard_map/ppermute | solution.py:99
  179.4 14.3 %collective-permute-start.58 = (bf16[96,2432]{1,0:T(8,128)(2,1)S(1)}, bf16[96,2432]{1,0:T(8,128)(2,1)S(1)}, u32[]{:S(2)}, u32[]{:S(2)}) collective-permute-start(bf16[96,2432]{1,0:T(8,128)(2,1)S(1)} %get-tuple-element.239), channel_id=1, source_target_pairs={{0,16},{1,17},{2,18},{3,19},{4,20},{5,21},{6,22},{7,23},{8,24},{9,... | collective-permute-start | bytes 1400840 | tf_op jit(solution)/shard_map/ppermute | solution.py:99
  (41 other events, 330.9 us)
